TPU v7x, 512 devices: a whole 4x8x8 slice. The times are simulated.
512 devices in a mesh: sx: 32 (over y_lo, z), sy: 16 (over y_hi, x, core).
Axes of the slice: x: 4, y: 8 (y_hi: 2, y_lo: 4; y = y_hi * 4 + y_lo), z: 8, core: 2. Of those that a mesh axis runs over, the one named last changes fastest.
Arguments:
- right_vectors: bfloat16 [32, 1024, 4096], P(None, 'sx', 'sy'), may hold values from -6 to 6
- left_vectors: bfloat16 [64, 1024, 4096], P(None, 'sx', 'sy'), may hold values from -6 to 6
- classes: int32 [1024, 4096], P('sx', 'sy'), may hold values from 0 to 3
- class_energy: float32 [4], replicated, may hold values from -1.5 to 1.5
- bond_mask_grid: int32 [2, 1024, 4096], P(None, 'sx', 'sy'), may hold values 0 or 1
- order: int32 [5], replicated, may hold values from 0 to 4, each once
Outputs:
- gamma: float32 [5, 64, 32], P(None, 'sy')
Inputs may be any that keep to these rules, and one draw needn't show every extreme that they name: Each order from 0 to 4 appears once.
All inputs are finite; a program needn't handle non-finite values. No bound on the sum of `bond_mask_grid` on one device may be relied on, other than what follows from the above.
Results may differ from a plain program's by a relative error of at most 0.0003.
Values sent between devices are 32-bit elements; how exact they have to be, the bound alone decides.
No kernel may reach another device: no remote copies, remote signals or barrier semaphores. Data moves between devices by JAX's collectives and lax.ppermute only.
A program may use at most 64 MiB of HBM per device.

v0:
```python
import jax
import jax.numpy as jnp
from jax import lax
from jax.sharding import PartitionSpec as P

MOMENTS = 5


half_root = 0.8660254037844386
spectral_scale = 4.6


def shifted(value, axis, by):
    length = lax.axis_size(axis)
    return lax.ppermute(value, axis, [(i, (i + by) % length) for i in range(length)])


def with_halo(value, sides, width):
    for axis, dim in sides:
        size, length = (lax.axis_size(axis), value.shape[dim])
        up = [(i, (i + 1) % size) for i in range(size)]
        down = [(j, i) for i, j in up]
        last = lax.slice_in_dim(value, length - width, length, axis=dim)
        initial = lax.slice_in_dim(value, 0, width, axis=dim)
        before = lax.ppermute(last, axis, up)
        after = lax.ppermute(initial, axis, down)
        value = jnp.concatenate([before, value, after], axis=dim)
    return value


def offsets(padded):
    return (padded[:, 2:, 1:-1], padded[:, :-2, 1:-1], padded[:, 1:-1, 2:], padded[:, 1:-1, :-2])


def shards(right_vectors, left_vectors, classes, class_energy, bond_mask_grid, order):
    rows_x, rows_y = classes.shape
    west_row = shifted(bond_mask_grid[0, -1:, :], "sx", 1)
    south_column = shifted(bond_mask_grid[1, :, -1:], "sy", 1)
    hmask = bond_mask_grid[0].astype(jnp.float32)
    vertical_mask = bond_mask_grid[1].astype(jnp.float32)
    west_mask = jnp.concatenate([west_row.astype(jnp.float32), hmask[:-1]], axis=0)
    south_mask = jnp.concatenate([south_column.astype(jnp.float32), vertical_mask[:, :-1]], axis=1)
    xpos = jnp.arange(rows_x, dtype=jnp.int32)[:, None]
    ypos = jnp.arange(rows_y, dtype=jnp.int32)[None, :]
    sublattice_first = ((xpos + ypos) % 2 == 0).astype(jnp.float32)
    sublattice_second = 1.0 - sublattice_first
    sign = sublattice_first - sublattice_second
    upper_neighbour = vertical_mask * sublattice_first
    lower_neighbour = south_mask * sublattice_second
    energy = jnp.zeros((rows_x, rows_y), jnp.float32)
    for level in range(class_energy.shape[0]):
        energy = energy + (classes == level).astype(jnp.float32) * class_energy[level]

    def beside_all(field):
        return offsets(with_halo(field, (("sx", 1), ("sy", 2)), 1))

    nleft = left_vectors.shape[0]
    nright = right_vectors.shape[0]
    cells = rows_x * rows_y
    left_field = left_vectors.astype(jnp.float32)
    left_flat = left_field.reshape(nleft, cells)
    count = MOMENTS
    moments = []
    u_prev = None
    pe, pw, pn, ps = beside_all(right_vectors.astype(jnp.float32))
    u_now = 0.5 * sign * (hmask * pe + west_mask * pw) - upper_neighbour * pn + lower_neighbour * ps
    for step in range(count):
        final = step == count - 1
        parts = None
        parts = beside_all(u_now)
        vel_pe, vel_pw, vel_pn, vel_ps = parts
        moved = (-half_root * (hmask * vel_pe - west_mask * vel_pw)).reshape(nright, cells)
        moments.append(
            jnp.dot(
                left_flat,
                moved.T,
                precision=lax.Precision.HIGHEST,
                preferred_element_type=jnp.float32,
            )
        )
        if not final:
            hamilton_pe, hamilton_pw, hamilton_pn, hamilton_ps = parts
            image = (
                energy * u_now
                - hmask * hamilton_pe
                - west_mask * hamilton_pw
                - upper_neighbour * hamilton_pn
                - lower_neighbour * hamilton_ps
            ) / spectral_scale
            if step == 0:
                u_next = image
            else:
                u_next = 2.0 * image - u_prev
            u_prev, u_now = (u_now, u_next)
    partial_tiles = jnp.stack(moments)
    owned = nleft // lax.axis_size("sy")
    total = lax.psum(partial_tiles, ("sx", "sy"))
    mine = lax.dynamic_slice_in_dim(total, lax.axis_index("sy") * owned, owned, 1)
    all_sites = cells * lax.axis_size("sx") * lax.axis_size("sy")
    mine = mine * (1.0 / jnp.sqrt(jnp.float32(all_sites)))
    select = (order[:, None] == jnp.arange(count, dtype=jnp.int32)[None, :]).astype(jnp.float32)
    return jnp.einsum("sm,mlr->slr", select, mine, precision=lax.Precision.HIGHEST)


def solution(mesh):
    in_specs = (
        P(None, "sx", "sy"),
        P(None, "sx", "sy"),
        P("sx", "sy"),
        P(),
        P(None, "sx", "sy"),
        P(),
    )
    out_specs = P(None, "sy", None)
    return jax.shard_map(shards, mesh=mesh, in_specs=in_specs, out_specs=out_specs, check_vma=False)
```

profile of v0, /device:TPU:1, one launch (start us, length us, event | category | flops | bytes accessed | tf_op | source)
XLA Modules:
  0.0 309.3 jit_solution(4009982580344775790)
XLA Ops:
  1.5 14.5 %collective-permute-start = (f32[32,1,256]{2,0,1:T(8,128)S(1)}, f32[32,1,256]{2,0,1:T(8,128)S(1)}, u32[]{:S(2)}, u32[]{:S(2)}) collective-permute-start(f32[32,1,256]{2,0,1:T(8,128)S(1)} %get-tuple-element.30), channel_id=1, source_target_pairs={{16,0},{32,16},{48,32},{64,48},{80,64},{96,80},{112,96},{128,112},... | collective-permute-start | bytes 98312 | tf_op jit(solution)/shard_map/ppermute | solution.py:26
  16.0 1.9 collective-permute-start.2
  18.1 4.0 %collective-permute-start.4 = (s32[32,1]{0,1:T(1,128)S(1)}, s32[32,1]{0,1:T(1,128)S(1)}, u32[]{:S(2)}, u32[]{:S(2)}) collective-permute-start(s32[32,1]{0,1:T(1,128)S(1)} %bitcast.60), channel_id=1, source_target_pairs={{0,1},{1,2},{2,3},{3,4},{4,5},{5,6},{6,7},{7,8},{8,9},{9,10},{10,1... | collective-permute-start | bytes 392 | tf_op jit(solution)/shard_map/ppermute | solution.py:15
  22.1 1.9 collective-permute-start.1
  24.3 6.3 %collective-permute-done.1 = s32[1,256]{1,0:T(1,128)S(1)} collective-permute-done((s32[1,256]{1,0:T(1,128)S(1)}, s32[1,256]{1,0:T(1,128)S(1)}, u32[]{:S(2)}, u32[]{:S(2)}) %collective-permute-start.1) | collective-permute-done | bytes 1056 | tf_op jit(solution)/shard_map/ppermute | solution.py:15
  31.4 2.8 collective-permute-start.5
  34.6 1.9 collective-permute-start.3
  37.9 2.0 collective-permute-done.3
  41.3 2.0 fusion.44
  43.3 4.2 %collective-permute-start.6 = (f32[32,1,256]{2,0,1:T(8,128)S(1)}, f32[32,1,256]{2,0,1:T(8,128)S(1)}, u32[]{:S(2)}, u32[]{:S(2)}) collective-permute-start(f32[32,1,256]{2,0,1:T(8,128)S(1)} %get-tuple-element.28), channel_id=1, source_target_pairs={{16,0},{32,16},{48,32},{64,48},{80,64},{96,80},{112,96},{128,112},... | collective-permute-start | bytes 98312 | tf_op jit(solution)/shard_map/ppermute | solution.py:26
  47.5 1.9 collective-permute-start.7
  50.1 6.0 %collective-permute-done.7 = f32[32,1,256]{2,0,1:T(8,128)S(1)} collective-permute-done((f32[32,1,256]{2,0,1:T(8,128)S(1)}, f32[32,1,256]{2,0,1:T(8,128)S(1)}, u32[]{:S(2)}, u32[]{:S(2)}) %collective-permute-start.7) | collective-permute-done | bytes 32800 | tf_op jit(solution)/shard_map/ppermute | solution.py:25
  58.8 2.5 collective-permute-start.9
  62.7 10.5 %collective-permute-start.8 = (f32[32,34,1]{1,0,2:T(8,128)S(1)}, f32[32,34,1]{1,0,2:T(8,128)}, u32[]{:S(2)}, u32[]{:S(2)}) collective-permute-start(f32[32,34,1]{1,0,2:T(8,128)S(1)} %copy.129), channel_id=1, source_target_pairs={{1,0},{2,1},{3,2},{4,3},{5,4},{6,5},{7,6},{8,7},{9,8},{10,9},{11,1... | collective-permute-start | bytes 13064 | tf_op jit(solution)/shard_map/ppermute | solution.py:26
  73.2 3.2 %broadcast_multiply_fusion.1 = (f32[32,256]{1,0:T(8,128)}, f32[32,256]{1,0:T(8,128)S(1)}) fusion(f32[]{:T(128)} %bitcast.12, s32[32,256]{1,0:T(8,128)S(1)} %copy-done.25, f32[]{:T(128)} %bitcast.11, f32[]{:T(128)} %bitcast.10, f32[]{:T(128)} %bitcast.9), kind=kLoop, calls=%fused_computation.158 | loop fusion | flops 98304 | bytes 98320 | tf_op jit(solution)/shard_map/mul | solution.py:84
  77.8 2.1 copy.92
  79.9 2.9 broadcast_multiply_fusion
  82.9 1.9 collective-permute-start.10
  84.8 3.4 %collective-permute-start.11 = (f32[32,1,256]{2,0,1:T(8,128)S(1)}, f32[32,1,256]{2,0,1:T(8,128)S(1)}, u32[]{:S(2)}, u32[]{:S(2)}) collective-permute-start(f32[32,1,256]{2,0,1:T(8,128)S(1)} %get-tuple-element.25), channel_id=1, source_target_pairs={{0,16},{16,32},{32,48},{48,64},{64,80},{80,96},{96,112},{112,128},... | collective-permute-start | bytes 98312 | tf_op jit(solution)/shard_map/ppermute | solution.py:25
  88.2 5.2 %collective-permute-done.11 = f32[32,1,256]{2,0,1:T(8,128)S(1)} collective-permute-done((f32[32,1,256]{2,0,1:T(8,128)S(1)}, f32[32,1,256]{2,0,1:T(8,128)S(1)}, u32[]{:S(2)}, u32[]{:S(2)}) %collective-permute-start.11) | collective-permute-done | bytes 32800 | tf_op jit(solution)/shard_map/ppermute | solution.py:25
  94.1 2.0 collective-permute-start.13
  96.6 10.8 %collective-permute-start.12 = (f32[32,34,1]{1,0,2:T(8,128)S(1)}, f32[32,34,1]{1,0,2:T(8,128)S(1)}, u32[]{:S(2)}, u32[]{:S(2)}) collective-permute-start(f32[32,34,1]{1,0,2:T(8,128)S(1)} %copy.131), channel_id=1, source_target_pairs={{1,0},{2,1},{3,2},{4,3},{5,4},{6,5},{7,6},{8,7},{9,8},{10,9},{11,1... | collective-permute-start | bytes 13064 | tf_op jit(solution)/shard_map/ppermute | solution.py:26
  110.1 5.8 %fusion.32 = f32[32,32,256]{2,0,1:T(8,128)S(1)} fusion(f32[32,34,1]{2,0,1:T(8,128)} %copy.100, f32[32,1,256]{2,0,1:T(8,128)S(1)} %collective-permute-done.10, f32[32,32,256]{2,0,1:T(8,128)} %copy-done.1, f32[32,1,256]{2,0,1:T(8,128)S(1)} %collective-permute-done.11, f32[32,34,1]{2,0,1:T(8,128)} %copy.98, f32[32,32,256]{2,0,1:T(8,128)} %get-tuple-element.8, ...), kind=kLoop, calls=%fused_computation.59 | loop fusion | flops 9175040 | bytes 4539392 | tf_op jit(solution)/shard_map/sub | solution.py:93
  115.9 1.9 collective-permute-start.14
  117.8 3.4 %collective-permute-start.15 = (f32[32,1,256]{2,0,1:T(8,128)S(1)}, f32[32,1,256]{2,0,1:T(8,128)S(1)}, u32[]{:S(2)}, u32[]{:S(2)}) collective-permute-start(f32[32,1,256]{2,0,1:T(8,128)S(1)} %get-tuple-element.23), channel_id=1, source_target_pairs={{0,16},{16,32},{32,48},{48,64},{64,80},{80,96},{96,112},{112,128},... | collective-permute-start | bytes 98312 | tf_op jit(solution)/shard_map/ppermute | solution.py:25
  121.2 5.2 %collective-permute-done.15 = f32[32,1,256]{2,0,1:T(8,128)S(1)} collective-permute-done((f32[32,1,256]{2,0,1:T(8,128)S(1)}, f32[32,1,256]{2,0,1:T(8,128)S(1)}, u32[]{:S(2)}, u32[]{:S(2)}) %collective-permute-start.15) | collective-permute-done | bytes 32800 | tf_op jit(solution)/shard_map/ppermute | solution.py:25
  129.7 1.9 collective-permute-start.17
  131.6 2.0 copy.133
  133.7 11.0 %collective-permute-start.16 = (f32[32,34,1]{1,0,2:T(8,128)}, f32[32,34,1]{1,0,2:T(8,128)}, u32[]{:S(2)}, u32[]{:S(2)}) collective-permute-start(f32[32,34,1]{1,0,2:T(8,128)} %copy.133), channel_id=1, source_target_pairs={{1,0},{2,1},{3,2},{4,3},{5,4},{6,5},{7,6},{8,7},{9,8},{10,9},{11,1... | collective-permute-start | bytes 13064 | tf_op jit(solution)/shard_map/ppermute | solution.py:26
  144.7 2.1 fusion.4
  146.8 2.1 copy.106
  148.9 2.1 copy.104
  151.0 2.4 fusion.24
  153.4 1.9 collective-permute-start.18
  155.4 3.4 %collective-permute-start.19 = (f32[32,1,256]{2,0,1:T(8,128)S(1)}, f32[32,1,256]{2,0,1:T(8,128)S(1)}, u32[]{:S(2)}, u32[]{:S(2)}) collective-permute-start(f32[32,1,256]{2,0,1:T(8,128)S(1)} %get-tuple-element.21), channel_id=1, source_target_pairs={{0,16},{16,32},{32,48},{48,64},{64,80},{80,96},{96,112},{112,128},... | collective-permute-start | bytes 98312 | tf_op jit(solution)/shard_map/ppermute | solution.py:25
  158.8 2.2 fusion.3
  161.0 3.0 collective-permute-done.19
  167.0 1.9 collective-permute-start.21
  170.0 10.8 %collective-permute-start.20 = (f32[32,34,1]{1,0,2:T(8,128)}, f32[32,34,1]{1,0,2:T(8,128)}, u32[]{:S(2)}, u32[]{:S(2)}) collective-permute-start(f32[32,34,1]{1,0,2:T(8,128)} %copy.135), channel_id=1, source_target_pairs={{1,0},{2,1},{3,2},{4,3},{5,4},{6,5},{7,6},{8,7},{9,8},{10,9},{11,1... | collective-permute-start | bytes 13064 | tf_op jit(solution)/shard_map/ppermute | solution.py:26
  180.8 2.1 fusion.2
  182.9 2.2 copy.112
  185.1 2.1 copy.110
  187.1 1.9 fusion.16
  189.1 1.9 collective-permute-start.23
  191.0 7.5 %collective-permute-start.22 = (f32[32,1,256]{2,0,1:T(8,128)S(1)}, f32[32,1,256]{2,0,1:T(8,128)S(1)}, u32[]{:S(2)}, u32[]{:S(2)}) collective-permute-start(f32[32,1,256]{2,0,1:T(8,128)S(1)} %get-tuple-element.19), channel_id=1, source_target_pairs={{16,0},{32,16},{48,32},{64,48},{80,64},{96,80},{112,96},{128,112},... | collective-permute-start | bytes 98312 | tf_op jit(solution)/shard_map/ppermute | solution.py:26
  198.5 2.1 fusion.1
  200.7 2.2 fusion
  202.8 105.7 %psum.7 = f32[5,64,32]{2,1,0:T(8,128)S(1)} all-reduce(f32[5,64,32]{2,1,0:T(8,128)S(1)} %fusion), channel_id=1, replica_groups=mesh['sx'=32,'sy'=16] {'sx','sy'}, use_global_device_ids=true, to_apply=%region_0.1 | all-reduce | flops 10240 | bytes 81920 | tf_op jit(solution)/shard_map/psum | solution.py:97
  (119 shorter events, 24.1 us)
Async XLA Ops:
  0.0 144.7 %copy-start = (bf16[64,32,256]{2,1,0:T(8,128)(2,1)S(1)}, bf16[64,32,256]{2,1,0:T(8,128)(2,1)}, u32[]{:S(2)}) copy-start(bf16[64,32,256]{2,1,0:T(8,128)(2,1)} %param.7) | copy-start | bytes 3145732
  0.0 17.9 %copy-start.7 = (s32[2,32,256]{2,1,0:T(8,128)S(1)}, s32[2,32,256]{2,1,0:T(8,128)}, u32[]{:S(2)}) copy-start(s32[2,32,256]{2,1,0:T(8,128)} %param.10) | copy-start | bytes 196612
  1.5 29.1 %collective-permute-start = (f32[32,1,256]{2,0,1:T(8,128)S(1)}, f32[32,1,256]{2,0,1:T(8,128)S(1)}, u32[]{:S(2)}, u32[]{:S(2)}) collective-permute-start(f32[32,1,256]{2,0,1:T(8,128)S(1)} %get-tuple-element.30), channel_id=1, source_target_pairs={{16,0},{32,16},{48,32},{64,48},{80,64},{96,80},{112,96},{128,112},... | collective-permute-start | bytes 98312 | tf_op jit(solution)/shard_map/ppermute | solution.py:26
  16.0 14.6 %collective-permute-start.2 = (f32[32,1,256]{2,0,1:T(8,128)S(1)}, f32[32,1,256]{2,0,1:T(8,128)S(1)}, u32[]{:S(2)}, u32[]{:S(2)}) collective-permute-start(f32[32,1,256]{2,0,1:T(8,128)S(1)} %get-tuple-element.29), channel_id=1, source_target_pairs={{0,16},{16,32},{32,48},{48,64},{64,80},{80,96},{96,112},{112,128},... | collective-permute-start | bytes 98312 | tf_op jit(solution)/shard_map/ppermute | solution.py:25
  18.1 6.0 %collective-permute-start.4 = (s32[32,1]{0,1:T(1,128)S(1)}, s32[32,1]{0,1:T(1,128)S(1)}, u32[]{:S(2)}, u32[]{:S(2)}) collective-permute-start(s32[32,1]{0,1:T(1,128)S(1)} %bitcast.60), channel_id=1, source_target_pairs={{0,1},{1,2},{2,3},{3,4},{4,5},{5,6},{6,7},{7,8},{8,9},{9,10},{10,1... | collective-permute-start | bytes 392 | tf_op jit(solution)/shard_map/ppermute | solution.py:15
  22.1 8.5 %collective-permute-start.1 = (s32[1,256]{1,0:T(1,128)S(1)}, s32[1,256]{1,0:T(1,128)S(1)}, u32[]{:S(2)}, u32[]{:S(2)}) collective-permute-start(s32[1,256]{1,0:T(1,128)S(1)} %slice_bitcast_fusion.1), channel_id=1, source_target_pairs={{0,16},{16,32},{32,48},{48,64},{64,80},{80,96},{96,112},{112,128},... | collective-permute-start | bytes 3080 | tf_op jit(solution)/shard_map/ppermute | solution.py:15
  31.4 5.1 %collective-permute-start.5 = (f32[32,34,1]{1,0,2:T(8,128)S(1)}, f32[32,34,1]{1,0,2:T(8,128)S(1)}, u32[]{:S(2)}, u32[]{:S(2)}) collective-permute-start(f32[32,34,1]{1,0,2:T(8,128)S(1)} %copy.128), channel_id=1, source_target_pairs={{0,1},{1,2},{2,3},{3,4},{4,5},{5,6},{6,7},{7,8},{8,9},{9,10},{10,1... | collective-permute-start | bytes 13064 | tf_op jit(solution)/shard_map/ppermute | solution.py:25
  34.6 5.3 %collective-permute-start.3 = (f32[32,34,1]{1,0,2:T(8,128)S(1)}, f32[32,34,1]{1,0,2:T(8,128)S(1)}, u32[]{:S(2)}, u32[]{:S(2)}) collective-permute-start(f32[32,34,1]{1,0,2:T(8,128)S(1)} %copy.127), channel_id=1, source_target_pairs={{1,0},{2,1},{3,2},{4,3},{5,4},{6,5},{7,6},{8,7},{9,8},{10,9},{11,1... | collective-permute-start | bytes 13064 | tf_op jit(solution)/shard_map/ppermute | solution.py:26
  41.3 8.1 %copy-start.26 = (f32[4]{0:T(128)S(1)}, f32[4]{0:T(128)}, u32[]{:S(2)}) copy-start(f32[4]{0:T(128)} %param.9) | copy-start | bytes 52
  43.3 36.6 %copy-start.5 = (f32[32,32,256]{2,0,1:T(8,128)}, f32[32,32,256]{2,0,1:T(8,128)S(1)}, u32[]{:S(2)}) copy-start(f32[32,32,256]{2,0,1:T(8,128)S(1)} %fusion.44) | copy-start | bytes 3145732
  43.3 6.8 %collective-permute-start.6 = (f32[32,1,256]{2,0,1:T(8,128)S(1)}, f32[32,1,256]{2,0,1:T(8,128)S(1)}, u32[]{:S(2)}, u32[]{:S(2)}) collective-permute-start(f32[32,1,256]{2,0,1:T(8,128)S(1)} %get-tuple-element.28), channel_id=1, source_target_pairs={{16,0},{32,16},{48,32},{64,48},{80,64},{96,80},{112,96},{128,112},... | collective-permute-start | bytes 98312 | tf_op jit(solution)/shard_map/ppermute | solution.py:26
  47.5 8.6 %collective-permute-start.7 = (f32[32,1,256]{2,0,1:T(8,128)S(1)}, f32[32,1,256]{2,0,1:T(8,128)S(1)}, u32[]{:S(2)}, u32[]{:S(2)}) collective-permute-start(f32[32,1,256]{2,0,1:T(8,128)S(1)} %get-tuple-element.27), channel_id=1, source_target_pairs={{0,16},{16,32},{32,48},{48,64},{64,80},{80,96},{96,112},{112,128},... | collective-permute-start | bytes 98312 | tf_op jit(solution)/shard_map/ppermute | solution.py:25
  50.1 29.8 %copy-start.8 = (f32[32,1,256]{2,0,1:T(8,128)}, f32[32,1,256]{2,0,1:T(8,128)S(1)}, u32[]{:S(2)}) copy-start(f32[32,1,256]{2,0,1:T(8,128)S(1)} %collective-permute-done.6) | copy-start | bytes 98308
  56.0 23.9 %copy-start.10 = (f32[32,1,256]{2,0,1:T(8,128)}, f32[32,1,256]{2,0,1:T(8,128)S(1)}, u32[]{:S(2)}) copy-start(f32[32,1,256]{2,0,1:T(8,128)S(1)} %collective-permute-done.7) | copy-start | bytes 98308
  57.3 15.9 %copy-start.25 = (s32[32,256]{1,0:T(8,128)S(1)}, s32[32,256]{1,0:T(8,128)}, u32[]{:S(2)}) copy-start(s32[32,256]{1,0:T(8,128)} %param.8) | copy-start | bytes 98308
  58.8 17.7 %collective-permute-start.9 = (f32[32,34,1]{1,0,2:T(8,128)S(1)}, f32[32,34,1]{1,0,2:T(8,128)S(1)}, u32[]{:S(2)}, u32[]{:S(2)}) collective-permute-start(f32[32,34,1]{1,0,2:T(8,128)S(1)} %copy.130), channel_id=1, source_target_pairs={{0,1},{1,2},{2,3},{3,4},{4,5},{5,6},{6,7},{7,8},{8,9},{9,10},{10,1... | collective-permute-start | bytes 13064 | tf_op jit(solution)/shard_map/ppermute | solution.py:25
  62.7 15.1 %collective-permute-start.8 = (f32[32,34,1]{1,0,2:T(8,128)S(1)}, f32[32,34,1]{1,0,2:T(8,128)}, u32[]{:S(2)}, u32[]{:S(2)}) collective-permute-start(f32[32,34,1]{1,0,2:T(8,128)S(1)} %copy.129), channel_id=1, source_target_pairs={{1,0},{2,1},{3,2},{4,3},{5,4},{6,5},{7,6},{8,7},{9,8},{10,9},{11,1... | collective-permute-start | bytes 13064 | tf_op jit(solution)/shard_map/ppermute | solution.py:26
  82.8 10.6 %copy-start.1 = (f32[32,32,256]{2,0,1:T(8,128)}, f32[32,32,256]{2,0,1:T(8,128)S(1)}, u32[]{:S(2)}) copy-start(f32[32,32,256]{2,0,1:T(8,128)S(1)} %get-tuple-element.7) | copy-start | bytes 3145732
  82.9 5.3 %collective-permute-start.10 = (f32[32,1,256]{2,0,1:T(8,128)S(1)}, f32[32,1,256]{2,0,1:T(8,128)S(1)}, u32[]{:S(2)}, u32[]{:S(2)}) collective-permute-start(f32[32,1,256]{2,0,1:T(8,128)S(1)} %get-tuple-element.26), channel_id=1, source_target_pairs={{16,0},{32,16},{48,32},{64,48},{80,64},{96,80},{112,96},{128,112},... | collective-permute-start | bytes 98312 | tf_op jit(solution)/shard_map/ppermute | solution.py:26
  84.8 8.6 %collective-permute-start.11 = (f32[32,1,256]{2,0,1:T(8,128)S(1)}, f32[32,1,256]{2,0,1:T(8,128)S(1)}, u32[]{:S(2)}, u32[]{:S(2)}) collective-permute-start(f32[32,1,256]{2,0,1:T(8,128)S(1)} %get-tuple-element.25), channel_id=1, source_target_pairs={{0,16},{16,32},{32,48},{48,64},{64,80},{80,96},{96,112},{112,128},... | collective-permute-start | bytes 98312 | tf_op jit(solution)/shard_map/ppermute | solution.py:25
  88.2 21.9 %copy-start.12 = (f32[32,1,256]{2,0,1:T(8,128)}, f32[32,1,256]{2,0,1:T(8,128)S(1)}, u32[]{:S(2)}) copy-start(f32[32,1,256]{2,0,1:T(8,128)S(1)} %collective-permute-done.10) | copy-start | bytes 98308
  93.4 16.7 %copy-start.14 = (f32[32,1,256]{2,0,1:T(8,128)}, f32[32,1,256]{2,0,1:T(8,128)S(1)}, u32[]{:S(2)}) copy-start(f32[32,1,256]{2,0,1:T(8,128)S(1)} %collective-permute-done.11) | copy-start | bytes 98308
  94.1 16.0 %copy-start.24 = (f32[32,256]{1,0:T(8,128)S(1)}, f32[32,256]{1,0:T(8,128)}, u32[]{:S(2)}) copy-start(f32[32,256]{1,0:T(8,128)} %get-tuple-element.5) | copy-start | bytes 98308
  94.1 13.3 %collective-permute-start.13 = (f32[32,34,1]{1,0,2:T(8,128)S(1)}, f32[32,34,1]{1,0,2:T(8,128)S(1)}, u32[]{:S(2)}, u32[]{:S(2)}) collective-permute-start(f32[32,34,1]{1,0,2:T(8,128)S(1)} %copy.132), channel_id=1, source_target_pairs={{0,1},{1,2},{2,3},{3,4},{4,5},{5,6},{6,7},{7,8},{8,9},{9,10},{10,1... | collective-permute-start | bytes 13064 | tf_op jit(solution)/shard_map/ppermute | solution.py:25
  96.6 12.2 %collective-permute-start.12 = (f32[32,34,1]{1,0,2:T(8,128)S(1)}, f32[32,34,1]{1,0,2:T(8,128)S(1)}, u32[]{:S(2)}, u32[]{:S(2)}) collective-permute-start(f32[32,34,1]{1,0,2:T(8,128)S(1)} %copy.131), channel_id=1, source_target_pairs={{1,0},{2,1},{3,2},{4,3},{5,4},{6,5},{7,6},{8,7},{9,8},{10,9},{11,1... | collective-permute-start | bytes 13064 | tf_op jit(solution)/shard_map/ppermute | solution.py:26
  115.9 5.3 %collective-permute-start.14 = (f32[32,1,256]{2,0,1:T(8,128)S(1)}, f32[32,1,256]{2,0,1:T(8,128)S(1)}, u32[]{:S(2)}, u32[]{:S(2)}) collective-permute-start(f32[32,1,256]{2,0,1:T(8,128)S(1)} %get-tuple-element.24), channel_id=1, source_target_pairs={{16,0},{32,16},{48,32},{64,48},{80,64},{96,80},{112,96},{128,112},... | collective-permute-start | bytes 98312 | tf_op jit(solution)/shard_map/ppermute | solution.py:26
  117.8 8.6 %collective-permute-start.15 = (f32[32,1,256]{2,0,1:T(8,128)S(1)}, f32[32,1,256]{2,0,1:T(8,128)S(1)}, u32[]{:S(2)}, u32[]{:S(2)}) collective-permute-start(f32[32,1,256]{2,0,1:T(8,128)S(1)} %get-tuple-element.23), channel_id=1, source_target_pairs={{0,16},{16,32},{32,48},{48,64},{64,80},{80,96},{96,112},{112,128},... | collective-permute-start | bytes 98312 | tf_op jit(solution)/shard_map/ppermute | solution.py:25
  121.2 5.3 %copy-start.16 = (f32[32,1,256]{2,0,1:T(8,128)}, f32[32,1,256]{2,0,1:T(8,128)S(1)}, u32[]{:S(2)}) copy-start(f32[32,1,256]{2,0,1:T(8,128)S(1)} %collective-permute-done.14) | copy-start | bytes 98308
  128.2 16.5 %copy-start.6 = (f32[32,32,256]{2,0,1:T(8,128)S(1)}, f32[32,32,256]{2,0,1:T(8,128)}, u32[]{:S(2)}) copy-start(f32[32,32,256]{2,0,1:T(8,128)} %copy-done.5) | copy-start | bytes 3145732
  128.2 16.5 %copy-start.9 = (f32[32,1,256]{2,0,1:T(8,128)S(1)}, f32[32,1,256]{2,0,1:T(8,128)}, u32[]{:S(2)}) copy-start(f32[32,1,256]{2,0,1:T(8,128)} %copy-done.8) | copy-start | bytes 98308
  128.2 16.5 %copy-start.11 = (f32[32,1,256]{2,0,1:T(8,128)S(1)}, f32[32,1,256]{2,0,1:T(8,128)}, u32[]{:S(2)}) copy-start(f32[32,1,256]{2,0,1:T(8,128)} %copy-done.10) | copy-start | bytes 98308
  129.7 17.1 %collective-permute-start.17 = (f32[32,34,1]{1,0,2:T(8,128)S(1)}, f32[32,34,1]{1,0,2:T(8,128)}, u32[]{:S(2)}, u32[]{:S(2)}) collective-permute-start(f32[32,34,1]{1,0,2:T(8,128)S(1)} %copy.134), channel_id=1, source_target_pairs={{0,1},{1,2},{2,3},{3,4},{4,5},{5,6},{6,7},{7,8},{8,9},{9,10},{10,1... | collective-permute-start | bytes 13064 | tf_op jit(solution)/shard_map/ppermute | solution.py:25
  133.7 15.3 %collective-permute-start.16 = (f32[32,34,1]{1,0,2:T(8,128)}, f32[32,34,1]{1,0,2:T(8,128)}, u32[]{:S(2)}, u32[]{:S(2)}) collective-permute-start(f32[32,34,1]{1,0,2:T(8,128)} %copy.133), channel_id=1, source_target_pairs={{1,0},{2,1},{3,2},{4,3},{5,4},{6,5},{7,6},{8,7},{9,8},{10,9},{11,1... | collective-permute-start | bytes 13064 | tf_op jit(solution)/shard_map/ppermute | solution.py:26
  151.0 7.8 %copy-start.2 = (f32[32,32,256]{2,0,1:T(8,128)S(1)}, f32[32,32,256]{2,0,1:T(8,128)}, u32[]{:S(2)}) copy-start(f32[32,32,256]{2,0,1:T(8,128)} %copy-done.1) | copy-start | bytes 3145732
  151.0 7.8 %copy-start.13 = (f32[32,1,256]{2,0,1:T(8,128)S(1)}, f32[32,1,256]{2,0,1:T(8,128)}, u32[]{:S(2)}) copy-start(f32[32,1,256]{2,0,1:T(8,128)} %copy-done.12) | copy-start | bytes 98308
  151.0 7.8 %copy-start.15 = (f32[32,1,256]{2,0,1:T(8,128)S(1)}, f32[32,1,256]{2,0,1:T(8,128)}, u32[]{:S(2)}) copy-start(f32[32,1,256]{2,0,1:T(8,128)} %copy-done.14) | copy-start | bytes 98308
  153.4 10.5 %copy-start.3 = (f32[32,32,256]{2,0,1:T(8,128)}, f32[32,32,256]{2,0,1:T(8,128)S(1)}, u32[]{:S(2)}) copy-start(f32[32,32,256]{2,0,1:T(8,128)S(1)} %fusion.24) | copy-start | bytes 3145732
  153.4 7.5 %collective-permute-start.18 = (f32[32,1,256]{2,0,1:T(8,128)S(1)}, f32[32,1,256]{2,0,1:T(8,128)S(1)}, u32[]{:S(2)}, u32[]{:S(2)}) collective-permute-start(f32[32,1,256]{2,0,1:T(8,128)S(1)} %get-tuple-element.22), channel_id=1, source_target_pairs={{16,0},{32,16},{48,32},{64,48},{80,64},{96,80},{112,96},{128,112},... | collective-permute-start | bytes 98312 | tf_op jit(solution)/shard_map/ppermute | solution.py:26
  155.4 8.6 %collective-permute-start.19 = (f32[32,1,256]{2,0,1:T(8,128)S(1)}, f32[32,1,256]{2,0,1:T(8,128)S(1)}, u32[]{:S(2)}, u32[]{:S(2)}) collective-permute-start(f32[32,1,256]{2,0,1:T(8,128)S(1)} %get-tuple-element.21), channel_id=1, source_target_pairs={{0,16},{16,32},{32,48},{48,64},{64,80},{80,96},{96,112},{112,128},... | collective-permute-start | bytes 98312 | tf_op jit(solution)/shard_map/ppermute | solution.py:25
  165.6 15.2 %copy-start.17 = (f32[32,1,256]{2,0,1:T(8,128)S(1)}, f32[32,1,256]{2,0,1:T(8,128)}, u32[]{:S(2)}) copy-start(f32[32,1,256]{2,0,1:T(8,128)} %copy-done.16) | copy-start | bytes 98308
  165.6 15.2 %copy-start.19 = (f32[32,1,256]{2,0,1:T(8,128)S(1)}, f32[32,1,256]{2,0,1:T(8,128)}, u32[]{:S(2)}) copy-start(f32[32,1,256]{2,0,1:T(8,128)} %copy-done.18) | copy-start | bytes 98308
  167.0 15.9 %collective-permute-start.21 = (f32[32,34,1]{1,0,2:T(8,128)S(1)}, f32[32,34,1]{1,0,2:T(8,128)}, u32[]{:S(2)}, u32[]{:S(2)}) collective-permute-start(f32[32,34,1]{1,0,2:T(8,128)S(1)} %copy.136), channel_id=1, source_target_pairs={{0,1},{1,2},{2,3},{3,4},{4,5},{5,6},{6,7},{7,8},{8,9},{9,10},{10,1... | collective-permute-start | bytes 13064 | tf_op jit(solution)/shard_map/ppermute | solution.py:25
  170.0 15.1 %collective-permute-start.20 = (f32[32,34,1]{1,0,2:T(8,128)}, f32[32,34,1]{1,0,2:T(8,128)}, u32[]{:S(2)}, u32[]{:S(2)}) collective-permute-start(f32[32,34,1]{1,0,2:T(8,128)} %copy.135), channel_id=1, source_target_pairs={{1,0},{2,1},{3,2},{4,3},{5,4},{6,5},{7,6},{8,7},{9,8},{10,9},{11,1... | collective-permute-start | bytes 13064 | tf_op jit(solution)/shard_map/ppermute | solution.py:26
  182.9 4.3 %copy-start.4 = (f32[32,32,256]{2,0,1:T(8,128)S(1)}, f32[32,32,256]{2,0,1:T(8,128)}, u32[]{:S(2)}) copy-start(f32[32,32,256]{2,0,1:T(8,128)} %copy-done.3) | copy-start | bytes 3145732
  182.9 4.3 %copy-start.21 = (f32[32,1,256]{2,0,1:T(8,128)S(1)}, f32[32,1,256]{2,0,1:T(8,128)}, u32[]{:S(2)}) copy-start(f32[32,1,256]{2,0,1:T(8,128)} %copy-done.20) | copy-start | bytes 98308
  189.1 11.5 %collective-permute-start.23 = (f32[32,1,256]{2,0,1:T(8,128)S(1)}, f32[32,1,256]{2,0,1:T(8,128)S(1)}, u32[]{:S(2)}, u32[]{:S(2)}) collective-permute-start(f32[32,1,256]{2,0,1:T(8,128)S(1)} %get-tuple-element.20), channel_id=1, source_target_pairs={{0,16},{16,32},{32,48},{48,64},{64,80},{80,96},{96,112},{112,128},... | collective-permute-start | bytes 98312 | tf_op jit(solution)/shard_map/ppermute | solution.py:25
  191.0 9.6 %collective-permute-start.22 = (f32[32,1,256]{2,0,1:T(8,128)S(1)}, f32[32,1,256]{2,0,1:T(8,128)S(1)}, u32[]{:S(2)}, u32[]{:S(2)}) collective-permute-start(f32[32,1,256]{2,0,1:T(8,128)S(1)} %get-tuple-element.19), channel_id=1, source_target_pairs={{16,0},{32,16},{48,32},{64,48},{80,64},{96,80},{112,96},{128,112},... | collective-permute-start | bytes 98312 | tf_op jit(solution)/shard_map/ppermute | solution.py:26
  200.6 107.9 %copy-start.27 = (s32[5]{0:T(128)S(1)}, s32[5]{0:T(128)}, u32[]{:S(2)}) copy-start(s32[5]{0:T(128)} %param.11) | copy-start | bytes 64
  (4 other events, 8.6 us)
where the time goes:
time: 311 us; the launch traced here: 309 us
  starting transfers between devices  110 us (35%)
  blocking collectives  106 us (34%)
  local copies, waits for them, and re-layouts  34.3 us (11%)
  waiting for transfers between devices  27.7 us (9%)
  other arithmetic  20.3 us (7%)
  matrix products  10.8 us (3%)
    psum x1, blocking collectives, shards(): total = lax.psum(partial_tiles, ('sx', 'sy'))  106 us
    ppermute x11, starting transfers between devices, with_halo(): after = lax.ppermute(initial, axis, down)  76.9 us
    ppermute x11, starting transfers between devices, with_halo(): before = lax.ppermute(last, axis, up)  27 us
    ppermute x11, waiting for transfers between devices, with_halo(): before = lax.ppermute(last, axis, up)  19.3 us
    unnamed x66, local copies, waits for them, and re-layouts  11.6 us
    dot_general x5, matrix products, shards(): jnp.dot(left_flat, moved.T, precision=lax.Precision.HIGHEST, preferred_el...  10.6 us
    sub x3, other arithmetic, shards(): u_next = 2.0 * image - u_prev  10.2 us
    ppermute x5, local copies, waits for them, and re-layouts, with_halo(): after = lax.ppermute(initial, axis, down)  8.93 us
  transfers between devices with their start and end apart: 24, of which 6 were waited for; matrix products, arithmetic and copies ran while one was open for 9% of the time, Pallas kernels for 0%

commit v1 on v0

v1 whole, which is shorter than its diff:
```python
import functools

import jax
import jax.numpy as jnp
from jax import lax
from jax.experimental import pallas as pl
from jax.experimental.pallas import tpu as pltpu
from jax.sharding import PartitionSpec as P

MOMENTS = 5
HALF_ROOT = 0.8660254037844386
SPECTRAL = 4.6
TWICE = 2.0 / SPECTRAL
DEPTH_X = MOMENTS + 1
SLOT = 4
REACH_Y = 3
LANES = 128
SUB = 8
PAD = 5


def slot_of(row, tile, tiles):
    at = row * tiles + tile
    per = LANES // SLOT
    return at // per, (at % per) * SLOT


def lane_iota():
    return lax.broadcasted_iota(jnp.int32, (SUB, LANES), 1)


def ext_block(own_ref, lo_ref, hi_ref, row, tile, lanes):
    depth, rows = lo_ref.shape[0], own_ref.shape[0]
    sub = pl.ds(tile * SUB, SUB)
    if row < depth:
        return lo_ref[row, sub, lanes]
    if row < depth + rows:
        return own_ref[row - depth, sub, lanes]
    return hi_ref[row - depth - rows, sub, lanes]


def pack_kernel(own_ref, lo_ref, hi_ref, first_ref, last_ref):
    rows = own_ref.shape[0] + 2 * lo_ref.shape[0]
    tiles = own_ref.shape[1] // SUB
    width = own_ref.shape[2]
    lane = lane_iota()
    first = [jnp.zeros((SUB, LANES), jnp.float32) for _ in range(first_ref.shape[0])]
    last = list(first)
    for row in range(rows):
        for tile in range(tiles):
            v, at = slot_of(row, tile, tiles)
            here = (lane >= at) & (lane < at + REACH_Y)
            a = ext_block(own_ref, lo_ref, hi_ref, row, tile, pl.ds(0, LANES))
            b = ext_block(own_ref, lo_ref, hi_ref, row, tile, pl.ds(width - LANES, LANES))
            first[v] = jnp.where(here, pltpu.roll(a, at, 1) if at else a, first[v])
            turn = (at + REACH_Y) % LANES
            last[v] = jnp.where(here, pltpu.roll(b, turn, 1) if turn else b, last[v])
    for v in range(first_ref.shape[0]):
        first_ref[v] = first[v]
        last_ref[v] = last[v]


def pack(own, lo, hi):
    rows = own.shape[0] + 2 * lo.shape[0]
    tiles = own.shape[1] // SUB
    count = -(-rows * tiles * SLOT // LANES)
    strip = jax.ShapeDtypeStruct((count, SUB, LANES), jnp.float32)
    return pl.pallas_call(
        pack_kernel,
        out_shape=(strip, strip),
        in_specs=[pl.BlockSpec(memory_space=pltpu.VMEM)] * 3,
        out_specs=(pl.BlockSpec(memory_space=pltpu.VMEM),) * 2,
        compiler_params=pltpu.CompilerParams(vmem_limit_bytes=12 << 20),
        name="pack_strips",
    )(own, lo, hi)


def partner(blocks, lane, odd):
    low = (lane & 1) == (1 if odd else 0)
    swapped = [
        jnp.where(low, pltpu.roll(b, LANES - 1, 1), pltpu.roll(b, 1, 1)) for b in blocks
    ]
    if not odd:
        return swapped
    n = len(blocks)
    return [
        jnp.where(
            lane == 0,
            swapped[(i - 1) % n],
            jnp.where(lane == LANES - 1, swapped[(i + 1) % n], swapped[i]),
        )
        for i in range(n)
    ]


def main_kernel(nright, own_ref, lo_ref, hi_ref, before_ref, after_ref, left_ref, out_ref, field, coup, acc, spaced):
    depth, rows_x, width = lo_ref.shape[0], own_ref.shape[0], own_ref.shape[2]
    rows = rows_x + 2 * depth
    tiles = own_ref.shape[1] // SUB
    rtiles = nright // SUB
    inner = width // LANES
    ntile = inner + 1
    lane = lane_iota()
    zero = jnp.zeros((SUB, LANES), jnp.float32)

    for row in range(rows):
        for tile in range(tiles):
            v, at = slot_of(row, tile, tiles)
            right_part = pltpu.roll(after_ref[v], (LANES - at) % LANES, 1) if at else after_ref[v]
            turn = (LANES - REACH_Y - at) % LANES
            left_part = pltpu.roll(before_ref[v], turn, 1) if turn else before_ref[v]
            rim = jnp.where(lane < REACH_Y, right_part, jnp.where(lane >= LANES - REACH_Y, left_part, zero))
            blocks = [
                ext_block(own_ref, lo_ref, hi_ref, row, tile, pl.ds(i * LANES, LANES)) for i in range(inner)
            ] + [rim]
            if tile < rtiles:
                for i in range(ntile):
                    field[0, row + PAD, tile * SUB : (tile + 1) * SUB, i * LANES : (i + 1) * LANES] = blocks[i]
            else:
                odd = (row - depth) % 2 == 1
                turned = partner(blocks, lane, odd)
                first_kind = ((lane + row - depth) & 1) == 0
                for i in range(ntile):
                    both = jnp.where(first_kind, blocks[i], turned[i])
                    for c, source in enumerate((blocks[i][0:1], both[1:2], blocks[i][2:3])):
                        coup[row + PAD, c, :, i * LANES : (i + 1) * LANES] = jnp.broadcast_to(source, (SUB, LANES))

    acc[...] = jnp.zeros_like(acc)

    def load(k, row, t, i):
        return field[k, row, t * SUB : (t + 1) * SUB, i * LANES : (i + 1) * LANES]

    def coupling(c, row, i):
        return coup[row, c, :, i * LANES : (i + 1) * LANES]

    def advance(k, row, odd):
        east = [coupling(0, row, i) for i in range(ntile)]
        west = [coupling(0, row - 1, i) for i in range(ntile)]
        vertical = [coupling(1, row, i) for i in range(ntile)]
        site = [coupling(2, row, i) for i in range(ntile)] if k else None
        sign = jnp.where((lane & 1) == (1 if odd else 0), 1.0 / TWICE, -1.0 / TWICE)
        for t in range(rtiles):
            here = [load(k, row, t, i) for i in range(ntile)]
            turned = partner(here, lane, odd)
            for i in range(ntile):
                a = east[i] * load(k, row + 1, t, i)
                b = west[i] * load(k, row - 1, t, i)
                if k == 0:
                    new = sign * (0.5 * (a + b) - vertical[i] * turned[i])
                else:
                    new = site[i] * here[i] - (a + b) - vertical[i] * turned[i]
                    new = 0.5 * new if k == 1 else new - load(k - 1, row, t, i)
                field[k + 1, row, t * SUB : (t + 1) * SUB, i * LANES : (i + 1) * LANES] = new

    def contract(row):
        east = [coupling(0, row, i) for i in range(inner)]
        west = [coupling(0, row - 1, i) for i in range(inner)]
        high, low = [], []
        for k in range(MOMENTS):
            parts = []
            for t in range(rtiles):
                parts.append(
                    jnp.concatenate(
                        [
                            east[i] * load(k + 1, row + 1, t, i) - west[i] * load(k + 1, row - 1, t, i)
                            for i in range(inner)
                        ],
                        axis=1,
                    )
                )
            value = jnp.concatenate(parts, axis=0)
            top = value.astype(jnp.bfloat16)
            high.append(top)
            low.append((value - top.astype(jnp.float32)).astype(jnp.bfloat16))
        block = left_ref[row - PAD - depth]
        dims = (((1,), (1,)), ((), ()))
        acc[...] += lax.dot_general(
            block, jnp.concatenate(high, axis=0), dims, preferred_element_type=jnp.float32
        ) + lax.dot_general(block, jnp.concatenate(low, axis=0), dims, preferred_element_type=jnp.float32)

    def step(front, odd, moments):
        for k in range(MOMENTS):
            advance(k, front - k, (odd + k) % 2 == 1)
        if moments:
            contract(front - MOMENTS)

    begin = 1 + PAD
    lead = 2 * MOMENTS

    def warm(n, _):
        front = begin + 2 * n
        step(front, (1 - depth) % 2, False)
        step(front + 1, (2 - depth) % 2, False)
        return 0

    lax.fori_loop(0, lead // 2, warm, 0)

    def full(n, _):
        front = begin + lead + 2 * n
        step(front, (1 + lead - depth) % 2, True)
        step(front + 1, (2 + lead - depth) % 2, True)
        return 0

    lax.fori_loop(0, rows_x // 2, full, 0)
    groups, _, flat = out_ref.shape
    owned = flat // nright
    for k in range(MOMENTS):
        spaced[:, 0:nright] = acc[:, k * nright : (k + 1) * nright]
        rows_of = [spaced[pl.ds(q, groups, stride=owned), :] for q in range(owned)]
        out_ref[:, k, :] = jnp.concatenate([r[:, 0:nright] for r in rows_of], axis=1)


def finish_kernel(scale, order_ref, blocks_ref, out_ref, total):
    total[...] = jnp.sum(blocks_ref[...], axis=0) * scale
    _, owned, nright = out_ref.shape
    for j in range(MOMENTS):
        row = total[pl.ds(order_ref[j], 1), :]
        for q in range(owned):
            out_ref[j, q : q + 1, :] = row[:, q * nright : (q + 1) * nright]


def moments_of_tile(own, lo, hi, before, after, left, nright, groups):
    rows = own.shape[0] + 2 * lo.shape[0]
    width = own.shape[2]
    nleft = left.shape[1]
    return pl.pallas_call(
        functools.partial(main_kernel, nright),
        out_shape=jax.ShapeDtypeStruct((groups, MOMENTS, nleft // groups * nright), jnp.float32),
        in_specs=[pl.BlockSpec(memory_space=pltpu.VMEM)] * 6,
        out_specs=pl.BlockSpec(memory_space=pltpu.VMEM),
        scratch_shapes=[
            pltpu.VMEM((MOMENTS + 1, rows + PAD, nright, width + LANES), jnp.float32),
            pltpu.VMEM((rows + PAD, 3, SUB, width + LANES), jnp.float32),
            pltpu.VMEM((nleft, MOMENTS * nright), jnp.float32),
            pltpu.VMEM((nleft, LANES), jnp.float32),
        ],
        compiler_params=pltpu.CompilerParams(vmem_limit_bytes=36 << 20),
        name="chebyshev_moments",
    )(own, lo, hi, before, after, left)


def ring(axis, by):
    size = lax.axis_size(axis)
    return [(i, (i + by) % size) for i in range(size)]


def shards(right_vectors, left_vectors, classes, class_energy, bond_mask_grid, order):
    rows_x, rows_y = classes.shape
    nright, nleft = right_vectors.shape[0], left_vectors.shape[0]

    def channels(start, size):
        right = lax.slice_in_dim(right_vectors, start, start + size, axis=1).astype(jnp.float32)
        masks = lax.slice_in_dim(bond_mask_grid, start, start + size, axis=1).astype(jnp.float32) * TWICE
        kinds = lax.slice_in_dim(classes, start, start + size, axis=0)
        energy = jnp.zeros((size, rows_y), jnp.float32)
        for level in range(class_energy.shape[0]):
            energy = jnp.where(kinds == level, class_energy[level] * TWICE, energy)
        rest = jnp.zeros((size, SUB - 3, rows_y), jnp.float32)
        return jnp.concatenate(
            [right.transpose(1, 0, 2), masks.transpose(1, 0, 2), energy[:, None], rest], axis=1
        )

    with jax.named_scope("halo_x"):
        lo = lax.ppermute(channels(rows_x - DEPTH_X, DEPTH_X), "sx", ring("sx", 1))
        hi = lax.ppermute(channels(0, DEPTH_X), "sx", ring("sx", -1))
    own = channels(0, rows_x)
    left = left_vectors.transpose(1, 0, 2)
    first, last = pack(own, lo, hi)
    with jax.named_scope("halo_y"):
        before = lax.ppermute(last, "sy", ring("sy", 1))
        after = lax.ppermute(first, "sy", ring("sy", -1))
    nsx, nsy = lax.axis_size("sx"), lax.axis_size("sy")
    owned = nleft // nsy
    tile = moments_of_tile(own, lo, hi, before, after, left, nright, nsy)
    with jax.named_scope("reduce_sy"):
        mine = jnp.sum(lax.all_to_all(tile, "sy", 0, 0), axis=0)
    with jax.named_scope("reduce_sx"):
        shares = lax.all_to_all(jnp.broadcast_to(mine[None], (nsx,) + mine.shape), "sx", 0, 0)
    sites = rows_x * rows_y * nsx * nsy
    return pl.pallas_call(
        functools.partial(finish_kernel, -HALF_ROOT / TWICE / sites**0.5),
        out_shape=jax.ShapeDtypeStruct((MOMENTS, owned, nright), jnp.float32),
        in_specs=[pl.BlockSpec(memory_space=pltpu.SMEM), pl.BlockSpec(memory_space=pltpu.VMEM)],
        out_specs=pl.BlockSpec(memory_space=pltpu.VMEM),
        scratch_shapes=[pltpu.VMEM(mine.shape, jnp.float32)],
        compiler_params=pltpu.CompilerParams(vmem_limit_bytes=4 << 20),
        name="finish",
    )(order, shares)


def solution(mesh):
    in_specs = (
        P(None, "sx", "sy"),
        P(None, "sx", "sy"),
        P("sx", "sy"),
        P(),
        P(None, "sx", "sy"),
        P(),
    )
    out_specs = P(None, "sy", None)
    return jax.shard_map(shards, mesh=mesh, in_specs=in_specs, out_specs=out_specs, check_vma=False)
```

time: 311 us -> 93.4 us (0.30)
  starting transfers between devices: 110 us -> 22.9 us
  blocking collectives: 106 us -> 40.2 us
  local copies, waits for them, and re-layouts: 34.3 us -> 2.23 us
  waiting for transfers between devices: 27.7 us -> 7.19 us
  other arithmetic: 20.3 us -> 3.21 us
  Pallas kernels: 0 us -> 14.6 us
  matrix products: 10.8 us -> 0 us
    psum x1 -> x0, blocking collectives: 106 us -> none  [shards(): total = lax.psum(partial_tiles, ('sx', 'sy'))]
    ppermute x24 -> x4, starting transfers between devices: 110 us -> 22.9 us  [the longest x1 11.6 us: shards(): hi = lax.ppermute(channels(0, DEPTH_X), 'sx', ring('sx', -1))]
    all_to_all x0 -> x2, blocking collectives: none -> 40.2 us  [the longest x1 23.2 us: shards(): mine = jnp.sum(lax.all_to_all(tile, 'sy', 0, 0), axis=0)]
    ppermute x24 -> x4, waiting for transfers between devices: 27.7 us -> 7.19 us  [the longest x1 3.38 us: shards(): lo = lax.ppermute(channels(rows_x - DEPTH_X, DEPTH_X), 'sx', ring('sx', 1))]
    ppermute x10 -> x0, local copies, waits for them, and re-layouts: 17.2 us -> none  [the longest x5 8.93 us: with_halo(): after = lax.ppermute(initial, axis, down)]
    pallas_call x0 -> x3, Pallas kernels: none -> 14.6 us  [the longest x1 12.8 us: moments_of_tile(): pl.pallas_call(functools.partial(main_kernel, nright), out_shape=jax.Shap...]
    unnamed x66 -> x10, local copies, waits for them, and re-layouts: 11.6 us -> 0.66 us
    dot_general x6 -> x0, matrix products: 10.8 us -> none  [the longest x5 10.6 us: shards(): jnp.dot(left_flat, moved.T, precision=lax.Precision.HIGHEST, preferred_el...]
  transfers between devices with their start and end apart: 24 -> 4, of which waited for: 6 -> 3; matrix products, arithmetic and copies ran while one was open for 9% -> 1% of each run, Pallas kernels for 0% -> 0%
where the time goes in v1:
time: 93.4 us; the launch traced here: 92.9 us
  blocking collectives  40.2 us (43%)
  starting transfers between devices  22.9 us (25%)
  Pallas kernels  14.6 us (16%)
  waiting for transfers between devices  7.19 us (8%)
  other arithmetic  3.21 us (3%)
  between operations  2.57 us (3%)
  local copies, waits for them, and re-layouts  2.23 us (2%)
    all_to_all x1, blocking collectives, shards(): mine = jnp.sum(lax.all_to_all(tile, 'sy', 0, 0), axis=0)  23.2 us
    all_to_all x1, blocking collectives, shards(): lax.all_to_all(jnp.broadcast_to(mine[None], (nsx,) + mine.shape), 'sx', 0...  17 us
    pallas_call x1, Pallas kernels, moments_of_tile(): pl.pallas_call(functools.partial(main_kernel, nright), out_shape=jax.Shap...  12.8 us
    ppermute x1, starting transfers between devices, shards(): hi = lax.ppermute(channels(0, DEPTH_X), 'sx', ring('sx', -1))  11.6 us
    ppermute x1, starting transfers between devices, shards(): lo = lax.ppermute(channels(rows_x - DEPTH_X, DEPTH_X), 'sx', ring('sx', 1))  4.83 us
    ppermute x1, starting transfers between devices, shards(): before = lax.ppermute(last, 'sy', ring('sy', 1))  4.55 us
    ppermute x1, waiting for transfers between devices, shards(): lo = lax.ppermute(channels(rows_x - DEPTH_X, DEPTH_X), 'sx', ring('sx', 1))  3.38 us
    ppermute x1, waiting for transfers between devices, shards(): after = lax.ppermute(first, 'sy', ring('sy', -1))  2.94 us
  transfers between devices with their start and end apart: 4, of which 3 were waited for; matrix products, arithmetic and copies ran while one was open for 1% of the time, Pallas kernels for 0%

profile of v1, /device:TPU:1, one launch (start us, length us, event | category | flops | bytes accessed | tf_op | source)
XLA Modules:
  0.0 92.9 jit_solution(10444813350234923001)
XLA Ops:
  0.0 1.4 %fusion.1 = (f32[1]{0:T(128)}, f32[1]{0:T(128)}, f32[1]{0:T(128)}, f32[1]{0:T(128)}) fusion(f32[4]{0:T(128)} %param.9), kind=kLoop, calls=%fused_computation.17 | loop fusion | bytes 32 | tf_op jit(solution)/shard_map/slice | solution.py:257
  3.8 0.7 select_select_fusion.1
  4.6 0.7 convert_multiply_fusion.1
  5.3 1.4 %fusion = (bf16[32,32,256]{2,0,1:T(8,128)(2,1)S(1)}, f32[32,32,256]{2,1,0:T(8,128)S(1)}) fusion(bf16[32,32,256]{2,1,0:T(8,128)(2,1)} %param.6), kind=kLoop, calls=%fused_computation.16 | loop fusion | flops 262144 | bytes 2097152 | tf_op args[0]
  6.7 0.0 copy-start.3
  6.7 0.0 copy-start.2
  6.8 0.1 pad.11.clone
  6.9 0.1 maximum_maximum_fusion.2
  7.0 4.8 %collective-permute-start = (f32[6,40,256]{2,1,0:T(8,128)S(1)}, f32[6,40,256]{2,1,0:T(8,128)S(1)}, u32[]{:S(2)}, u32[]{:S(2)}) collective-permute-start(f32[6,40,256]{2,1,0:T(8,128)S(1)} %get-tuple-element.18), channel_id=1, source_target_pairs={{0,16},{16,32},{32,48},{48,64},{64,80},{80,96},{96,112},{112,128},... | collective-permute-start | bytes 737288 | tf_op jit(solution)/shard_map/halo_x/ppermute | solution.py:264
  11.8 11.6 %collective-permute-start.1 = (f32[6,40,256]{2,1,0:T(8,128)S(1)}, f32[6,40,256]{2,1,0:T(8,128)S(1)}, u32[]{:S(2)}, u32[]{:S(2)}) collective-permute-start(f32[6,40,256]{2,1,0:T(8,128)S(1)} %get-tuple-element.17), channel_id=1, source_target_pairs={{0,496},{16,0},{32,16},{48,32},{64,48},{80,64},{96,80},{112,96},{1... | collective-permute-start | bytes 737288 | tf_op jit(solution)/shard_map/halo_x/ppermute | solution.py:265
  23.4 0.0 copy-done.3
  23.5 0.0 copy-done.2
  23.5 0.1 copy.35
  23.6 0.2 maximum_maximum_fusion.own_ref
  23.8 0.0 copy-start.1
  23.8 3.4 %collective-permute-done.lo_ref = f32[6,40,256]{2,1,0:T(8,128)S(1)} collective-permute-done((f32[6,40,256]{2,1,0:T(8,128)S(1)}, f32[6,40,256]{2,1,0:T(8,128)S(1)}, u32[]{:S(2)}, u32[]{:S(2)}) %collective-permute-start) | collective-permute-done | bytes 245792 | tf_op jit(solution)/shard_map/halo_x/ppermute | solution.py:264
  27.2 0.9 collective-permute-done.1.hi_ref
  28.0 0.5 pack_strips.1
  28.6 4.5 %collective-permute-start.2 = (f32[7,8,128]{2,1,0:T(8,128)S(1)}, f32[7,8,128]{2,1,0:T(8,128)S(1)}, u32[]{:S(2)}, u32[]{:S(2)}) collective-permute-start(f32[7,8,128]{2,1,0:T(8,128)S(1)} %get-tuple-element.7), channel_id=1, source_target_pairs={{0,1},{1,2},{2,3},{3,4},{4,5},{5,6},{6,7},{7,8},{8,9},{9,10},{10,1... | collective-permute-start | bytes 86024 | tf_op jit(solution)/shard_map/halo_y/ppermute | solution.py:270
  33.1 1.9 %collective-permute-start.3 = (f32[7,8,128]{2,1,0:T(8,128)S(1)}, f32[7,8,128]{2,1,0:T(8,128)S(1)}, u32[]{:S(2)}, u32[]{:S(2)}) collective-permute-start(f32[7,8,128]{2,1,0:T(8,128)S(1)} %get-tuple-element.8), channel_id=1, source_target_pairs={{0,15},{1,0},{2,1},{3,2},{4,3},{5,4},{6,5},{7,6},{8,7},{9,8},{10,9... | collective-permute-start | bytes 86024 | tf_op jit(solution)/shard_map/halo_y/ppermute | solution.py:271
  35.1 0.0 copy-done.1
  35.1 0.6 copy.34
  35.7 0.0 collective-permute-done.2.before_ref
  35.7 2.9 %collective-permute-done.3.after_ref = f32[7,8,128]{2,1,0:T(8,128)S(1)} collective-permute-done((f32[7,8,128]{2,1,0:T(8,128)S(1)}, f32[7,8,128]{2,1,0:T(8,128)S(1)}, u32[]{:S(2)}, u32[]{:S(2)}) %collective-permute-start.3) | collective-permute-done | bytes 28704 | tf_op jit(solution)/shard_map/halo_y/ppermute | solution.py:271
  38.6 0.0 copy-start
  38.6 12.8 %chebyshev_moments.1 = f32[16,5,128]{2,1,0:T(8,128)S(1)} custom-call(f32[32,40,256]{2,1,0:T(8,128)S(1)} %maximum_maximum_fusion.own_ref, f32[6,40,256]{2,1,0:T(8,128)S(1)} %collective-permute-done.lo_ref, f32[6,40,256]{2,1,0:T(8,128)S(1)} %collective-permute-done.1.hi_ref, f32[7,8,128]{2,1,0:T(8,128)S(1)} %collective-permute-done.2.before_ref, ...), custom_call_target="tpu_custom_call" | custom-call | tf_op jit(solution)/shard_map/chebyshev_moments/pallas_call | solution.py:226
  51.4 23.2 %all_to_all.10 = f32[16,5,128]{2,1,0:T(8,128)S(1)} all-to-all(f32[16,5,128]{2,1,0:T(8,128)S(1)} %chebyshev_moments.1), channel_id=1, replica_groups=mesh['sx'=32,'sy'=16] {'sy'}, dimensions={0} | all-to-all | bytes 81920 | tf_op jit(solution)/shard_map/reduce_sy/all_to_all | solution.py:276
  74.7 17.0 %all_to_all.11.blocks_ref = f32[32,5,128]{2,1,0:T(8,128)S(1)} all-to-all(f32[32,5,128]{2,1,0:T(8,128)S(1)} %broadcast_in_dim.64), channel_id=1, replica_groups=mesh['sx'=32,'sy'=16] {'sx'}, dimensions={0} | all-to-all | bytes 163840 | tf_op jit(solution)/shard_map/reduce_sx/all_to_all | solution.py:278
  91.6 0.0 copy-done
  91.7 1.3 %finish.1 = f32[5,4,32]{2,1,0:T(4,128)} custom-call(s32[5]{0:T(128)S(1)} %copy-done, f32[32,5,128]{2,1,0:T(8,128)S(1)} %all_to_all.11.blocks_ref), custom_call_target="tpu_custom_call" | custom-call | tf_op jit(solution)/shard_map/finish/pallas_call | solution.py:280
  (10 shorter events, 0.1 us)
Async XLA Ops:
  6.7 16.8 %copy-start.3 = (s32[32,256]{1,0:T(8,128)S(1)}, s32[32,256]{1,0:T(8,128)}, u32[]{:S(2)}) copy-start(s32[32,256]{1,0:T(8,128)} %param.8) | copy-start | bytes 98308
  6.7 16.8 %copy-start.2 = (s32[2,32,256]{2,1,0:T(8,128)S(1)}, s32[2,32,256]{2,1,0:T(8,128)}, u32[]{:S(2)}) copy-start(s32[2,32,256]{2,1,0:T(8,128)} %param.10) | copy-start | bytes 196612
  7.0 20.2 %collective-permute-start = (f32[6,40,256]{2,1,0:T(8,128)S(1)}, f32[6,40,256]{2,1,0:T(8,128)S(1)}, u32[]{:S(2)}, u32[]{:S(2)}) collective-permute-start(f32[6,40,256]{2,1,0:T(8,128)S(1)} %get-tuple-element.18), channel_id=1, source_target_pairs={{0,16},{16,32},{32,48},{48,64},{64,80},{80,96},{96,112},{112,128},... | collective-permute-start | bytes 737288 | tf_op jit(solution)/shard_map/halo_x/ppermute | solution.py:264
  11.8 16.2 %collective-permute-start.1 = (f32[6,40,256]{2,1,0:T(8,128)S(1)}, f32[6,40,256]{2,1,0:T(8,128)S(1)}, u32[]{:S(2)}, u32[]{:S(2)}) collective-permute-start(f32[6,40,256]{2,1,0:T(8,128)S(1)} %get-tuple-element.17), channel_id=1, source_target_pairs={{0,496},{16,0},{32,16},{48,32},{64,48},{80,64},{96,80},{112,96},{1... | collective-permute-start | bytes 737288 | tf_op jit(solution)/shard_map/halo_x/ppermute | solution.py:265
  23.8 11.3 %copy-start.1 = (bf16[64,32,256]{2,1,0:T(8,128)(2,1)S(1)}, bf16[64,32,256]{2,1,0:T(8,128)(2,1)}, u32[]{:S(2)}) copy-start(bf16[64,32,256]{2,1,0:T(8,128)(2,1)} %param.7) | copy-start | bytes 3145732
  28.6 7.1 %collective-permute-start.2 = (f32[7,8,128]{2,1,0:T(8,128)S(1)}, f32[7,8,128]{2,1,0:T(8,128)S(1)}, u32[]{:S(2)}, u32[]{:S(2)}) collective-permute-start(f32[7,8,128]{2,1,0:T(8,128)S(1)} %get-tuple-element.7), channel_id=1, source_target_pairs={{0,1},{1,2},{2,3},{3,4},{4,5},{5,6},{6,7},{7,8},{8,9},{9,10},{10,1... | collective-permute-start | bytes 86024 | tf_op jit(solution)/shard_map/halo_y/ppermute | solution.py:270
  33.1 5.5 %collective-permute-start.3 = (f32[7,8,128]{2,1,0:T(8,128)S(1)}, f32[7,8,128]{2,1,0:T(8,128)S(1)}, u32[]{:S(2)}, u32[]{:S(2)}) collective-permute-start(f32[7,8,128]{2,1,0:T(8,128)S(1)} %get-tuple-element.8), channel_id=1, source_target_pairs={{0,15},{1,0},{2,1},{3,2},{4,3},{5,4},{6,5},{7,6},{8,7},{9,8},{10,9... | collective-permute-start | bytes 86024 | tf_op jit(solution)/shard_map/halo_y/ppermute | solution.py:271
  38.6 53.0 %copy-start = (s32[5]{0:T(128)S(1)}, s32[5]{0:T(128)}, u32[]{:S(2)}) copy-start(s32[5]{0:T(128)} %order_ref.1) | copy-start | bytes 64

commit v2 on v1

v2 whole, which is shorter than its diff:
```python
import functools

import jax
import jax.numpy as jnp
from jax import lax
from jax.experimental import pallas as pl
from jax.experimental.pallas import tpu as pltpu
from jax.sharding import PartitionSpec as P

MOMENTS = 5
HALF_ROOT = 0.8660254037844386
SPECTRAL = 4.6
TWICE = 2.0 / SPECTRAL
DEPTH = MOMENTS + 1
REACH = 3
SLOT = 4
COUPLINGS = 3
LANES = 128
SUB = 8
SPAN = 32


def lane_iota():
    return lax.broadcasted_iota(jnp.int32, (SUB, LANES), 1)


def turn(value, by):
    by %= LANES
    return pltpu.roll(value, by, 1) if by else value


def swap_major(blocks, sub):
    for s in (4, 2, 1):
        keep = (sub & s) == 0
        for i in range(SUB):
            if i & s == 0:
                a, b = blocks[i], blocks[i + s]
                blocks[i] = jnp.where(keep, a, pltpu.roll(b, s, 0))
                blocks[i + s] = jnp.where(keep, pltpu.roll(a, SUB - s, 0), b)
    return blocks


def prepare_kernel(energy_ref, right_ref, class_ref, bond_ref, own_ref, coup_ref, top_ref, bottom_ref, first_ref, last_ref):
    nright, rows, width = right_ref.shape
    lane = lane_iota()
    sub = lax.broadcasted_iota(jnp.int32, (SUB, LANES), 0)
    xtiles, rtiles, inner = rows // SUB, nright // SUB, width // LANES
    zero = jnp.zeros((SUB, LANES), jnp.float32)
    first, last = [zero] * (xtiles + 1), [zero] * (xtiles + 1)

    def strip(v, at, i, block):
        here = (lane >= at) & (lane < at + REACH)
        if i == 0:
            first[v] = jnp.where(here, turn(block, at), first[v])
        if i == inner - 1:
            last[v] = jnp.where(here, turn(block, at + REACH), last[v])

    for half in range(xtiles // 2):
        for i in range(inner):
            lanes = slice(i * LANES, (i + 1) * LANES)
            for t in range(rtiles):
                wide = [
                    right_ref[t * SUB + q, half * 2 * SUB : (half + 1) * 2 * SUB, lanes].astype(jnp.float32)
                    for q in range(SUB)
                ]
                for part in range(2):
                    xt = half * 2 + part
                    turned = swap_major([w[part * SUB : (part + 1) * SUB] for w in wide], sub)
                    for j in range(SUB):
                        x = xt * SUB + j
                        own_ref[x, t * SUB : (t + 1) * SUB, lanes] = turned[j]
                        if x < DEPTH:
                            top_ref[x * nright + t * SUB : x * nright + (t + 1) * SUB, lanes] = turned[j]
                        if x >= rows - DEPTH:
                            at = (x - rows + DEPTH) * nright + t * SUB
                            bottom_ref[at : at + SUB, lanes] = turned[j]
                        strip(xt, t * SPAN + j * SLOT, i, turned[j])
    for xt in range(xtiles):
        here = slice(xt * SUB, (xt + 1) * SUB)
        for i in range(inner):
            lanes = slice(i * LANES, (i + 1) * LANES)
            kinds = class_ref[here, lanes]
            energy = zero
            for level in range(energy_ref.shape[0]):
                energy = jnp.where(kinds == level, energy_ref[level] * TWICE, energy)
            fields = [bond_ref[c, here, lanes].astype(jnp.float32) * TWICE for c in range(2)] + [energy]
            for c in range(COUPLINGS):
                coup_ref[c, here, lanes] = fields[c]
                strip(xtiles, (c * xtiles + xt) * SLOT, i, fields[c])
                at = DEPTH * nright + c * SUB
                if xt == 0:
                    top_ref[at : at + SUB, lanes] = fields[c]
                if xt == xtiles - 1:
                    bottom_ref[at : at + SUB, lanes] = fields[c]
    for v in range(xtiles + 1):
        first_ref[v] = first[v]
        last_ref[v] = last[v]


def prepare(right, classes, energy, bonds):
    nright, rows, width = right.shape
    rim = jax.ShapeDtypeStruct((DEPTH * nright + COUPLINGS * SUB, width), jnp.float32)
    strip = jax.ShapeDtypeStruct((rows // SUB + 1, SUB, LANES), jnp.float32)
    return pl.pallas_call(
        prepare_kernel,
        out_shape=(
            jax.ShapeDtypeStruct((rows, nright, width), jnp.float32),
            jax.ShapeDtypeStruct((COUPLINGS, rows, width), jnp.float32),
            rim,
            rim,
            strip,
            strip,
        ),
        in_specs=[pl.BlockSpec(memory_space=pltpu.SMEM)] + [pl.BlockSpec(memory_space=pltpu.VMEM)] * 3,
        out_specs=(pl.BlockSpec(memory_space=pltpu.VMEM),) * 6,
        compiler_params=pltpu.CompilerParams(vmem_limit_bytes=8 << 20),
        name="prepare",
    )(energy, right, classes, bonds)


def swapped(block, lane, odd):
    low = (lane & 1) == (1 if odd else 0)
    target = jnp.where(low, lane + 1, lane + LANES - 1) & (LANES - 1)
    return jnp.take_along_axis(block, target, axis=1)


def main_kernel(own_ref, coup_ref, lo_ref, hi_ref, before_ref, after_ref, clo_ref, chi_ref, left_ref, out_ref, field, rim, coup, acc, spaced):
    rows_x, nright, width = own_ref.shape
    rows = rows_x + 2 * DEPTH
    rtiles, inner, xtiles = nright // SUB, width // LANES, rows_x // SUB
    lane = lane_iota()
    sub = lax.broadcasted_iota(jnp.int32, (SUB, LANES), 0)
    zero = jnp.zeros((SUB, LANES), jnp.float32)

    def lanes_of(i):
        return slice(i * LANES, (i + 1) * LANES)

    for e in range(rows):
        x = (e - DEPTH) % rows_x
        if e < DEPTH:
            before, after = clo_ref[0], clo_ref[2]
        elif e >= DEPTH + rows_x:
            before, after = chi_ref[0], chi_ref[2]
        else:
            before, after = before_ref[x // SUB], after_ref[x // SUB]
        shift = (x % SUB) * SLOT
        rim[0, e] = jnp.where(
            lane % SPAN < REACH,
            turn(after, -shift),
            jnp.where(lane % SPAN >= SPAN - REACH, turn(before, -shift - REACH), zero),
        )
        if e < DEPTH:
            field[0, e] = lo_ref[e * nright : (e + 1) * nright, :]
        elif e >= DEPTH + rows_x:
            at = (e - DEPTH - rows_x) * nright
            field[0, e] = hi_ref[at : at + nright, :]
        else:
            field[0, e] = own_ref[x]

    for g in range(xtiles + 2):
        xt = (g - 1) % xtiles
        if g == 0:
            before, after = clo_ref[1], clo_ref[3]
        elif g == xtiles + 1:
            before, after = chi_ref[1], chi_ref[3]
        else:
            before, after = before_ref[xtiles], after_ref[xtiles]
        whole = []
        for c in range(COUPLINGS):
            at = DEPTH * nright + c * SUB
            if g == 0:
                blocks = [lo_ref[at : at + SUB, lanes_of(i)] for i in range(inner)]
            elif g == xtiles + 1:
                blocks = [hi_ref[at : at + SUB, lanes_of(i)] for i in range(inner)]
            else:
                blocks = [coup_ref[c, xt * SUB : (xt + 1) * SUB, lanes_of(i)] for i in range(inner)]
            shift = (c * xtiles + xt) * SLOT
            blocks.append(
                jnp.where(
                    lane < REACH,
                    turn(after, -shift),
                    jnp.where(lane >= LANES - REACH, turn(before, -shift - REACH), zero),
                )
            )
            if c == 1:
                even = [swapped(b, lane, False) for b in blocks]
                odd = [swapped(b, lane, True) for b in blocks]
                n = len(blocks)
                odd = [
                    jnp.where(lane == 0, odd[(i - 1) % n], jnp.where(lane == LANES - 1, odd[(i + 1) % n], odd[i]))
                    for i in range(n)
                ]
                blocks = [
                    jnp.where(((lane + sub) & 1) == 0, b, jnp.where((sub & 1) == 1, o, v))
                    for b, o, v in zip(blocks, odd, even)
                ]
            edge = blocks[inner]
            edge = edge + turn(edge, LANES // 2)
            blocks[inner] = edge + turn(edge, LANES // 4)
            whole.append(blocks)
        for s in range(SUB):
            e = (g - 1) * SUB + s + DEPTH
            if 0 <= e < rows:
                for c in range(COUPLINGS):
                    for i in range(inner + 1):
                        coup[e, c, :, lanes_of(i)] = jnp.broadcast_to(whole[c][i][s : s + 1], (SUB, LANES))

    acc[...] = jnp.zeros_like(acc)

    def load(k, row, t, i):
        if i == inner:
            return rim[k, row]
        return field[k, row, t * SUB : (t + 1) * SUB, lanes_of(i)]

    def coupling(c, row, i):
        return coup[row, c, :, lanes_of(i)]

    where = [(t, i) for t in range(rtiles) for i in range(inner)] + [(0, inner)]

    def partners(here, odd):
        moved = {at: swapped(value, lane, odd) for at, value in here.items()}
        if not odd:
            return moved
        edge = moved[0, inner]
        start, end = lane == 0, lane == LANES - 1
        result, fill = {}, edge
        for t in range(rtiles):
            outer = turn(edge, -t * SPAN)
            for i in range(inner):
                left = moved[t, i - 1] if i else outer
                right = moved[t, i + 1] if i < inner - 1 else outer
                result[t, i] = jnp.where(start, left, jnp.where(end, right, moved[t, i]))
            facing = turn(jnp.where(lane < LANES // 2, moved[t, inner - 1], moved[t, 0]), t * SPAN)
            fill = jnp.where((lane == t * SPAN) | (lane == (t * SPAN - 1) % LANES), facing, fill)
        result[0, inner] = fill
        return result

    def advance(k, row, odd):
        here = {at: load(k, row, *at) for at in where}
        turned = partners(here, odd)
        east = [coupling(0, row, i) for i in range(inner + 1)]
        west = [coupling(0, row - 1, i) for i in range(inner + 1)]
        vertical = [coupling(1, row, i) for i in range(inner + 1)]
        site = [coupling(2, row, i) for i in range(inner + 1)] if k else None
        sign = jnp.where((lane & 1) == (1 if odd else 0), 1.0 / TWICE, -1.0 / TWICE)
        new = {}
        for t, i in where:
            beside = east[i] * load(k, row + 1, t, i) + west[i] * load(k, row - 1, t, i)
            across = vertical[i] * turned[t, i]
            if k == 0:
                new[t, i] = sign * (0.5 * beside - across)
            else:
                image = site[i] * here[t, i] - beside - across
                new[t, i] = 0.5 * image if k == 1 else image - load(k - 1, row, t, i)
        for t, i in where:
            if i == inner:
                rim[k + 1, row] = new[t, i]
            else:
                field[k + 1, row, t * SUB : (t + 1) * SUB, lanes_of(i)] = new[t, i]

    def contract(row):
        east = [coupling(0, row, i) for i in range(inner)]
        west = [coupling(0, row - 1, i) for i in range(inner)]
        high, low = [], []
        for k in range(MOMENTS):
            parts = []
            for t in range(rtiles):
                parts.append(
                    jnp.concatenate(
                        [
                            east[i] * load(k + 1, row + 1, t, i) - west[i] * load(k + 1, row - 1, t, i)
                            for i in range(inner)
                        ],
                        axis=1,
                    )
                )
            value = jnp.concatenate(parts, axis=0)
            top = value.astype(jnp.bfloat16)
            high.append(top)
            low.append((value - top.astype(jnp.float32)).astype(jnp.bfloat16))
        block = left_ref[row - DEPTH]
        dims = (((1,), (1,)), ((), ()))
        acc[...] += lax.dot_general(
            block, jnp.concatenate(high, axis=0), dims, preferred_element_type=jnp.float32
        ) + lax.dot_general(block, jnp.concatenate(low, axis=0), dims, preferred_element_type=jnp.float32)

    lead = DEPTH + 2 * MOMENTS
    for front in range(1, lead):
        for k in reversed(range(MOMENTS)):
            if front >= 3 * k + 1:
                advance(k, front - 2 * k, front % 2 == 1)

    def both(n, _):
        for part in range(2):
            front = lead + 2 * n + part
            contract(front - 2 * MOMENTS)
            for k in reversed(range(MOMENTS)):
                advance(k, front - 2 * k, (lead + part) % 2 == 1)
        return 0

    lax.fori_loop(0, rows_x // 2, both, 0)
    groups, _, flat = out_ref.shape
    owned = flat // nright
    for k in range(MOMENTS):
        spaced[:, 0:nright] = acc[:, k * nright : (k + 1) * nright]
        rows_of = [spaced[pl.ds(q, groups, stride=owned), :] for q in range(owned)]
        out_ref[:, k, :] = jnp.concatenate([r[:, 0:nright] for r in rows_of], axis=1)


def finish_kernel(scale, order_ref, blocks_ref, out_ref, total):
    total[...] = jnp.sum(blocks_ref[...], axis=0) * scale
    _, owned, nright = out_ref.shape
    for j in range(MOMENTS):
        row = total[pl.ds(order_ref[j], 1), :]
        for q in range(owned):
            out_ref[j, q : q + 1, :] = row[:, q * nright : (q + 1) * nright]


def moments_of_tile(own, coup, lo, hi, before, after, clo, chi, left, groups):
    rows_x, nright, width = own.shape
    rows = rows_x + 2 * DEPTH + MOMENTS
    nleft = left.shape[1]
    return pl.pallas_call(
        main_kernel,
        out_shape=jax.ShapeDtypeStruct((groups, MOMENTS, nleft // groups * nright), jnp.float32),
        in_specs=[pl.BlockSpec(memory_space=pltpu.VMEM)] * 9,
        out_specs=pl.BlockSpec(memory_space=pltpu.VMEM),
        scratch_shapes=[
            pltpu.VMEM((MOMENTS + 1, rows, nright, width), jnp.float32),
            pltpu.VMEM((MOMENTS + 1, rows, SUB, LANES), jnp.float32),
            pltpu.VMEM((rows, COUPLINGS, SUB, width + LANES), jnp.float32),
            pltpu.VMEM((nleft, MOMENTS * nright), jnp.float32),
            pltpu.VMEM((nleft, LANES), jnp.float32),
        ],
        compiler_params=pltpu.CompilerParams(vmem_limit_bytes=28 << 20),
        name="chebyshev_moments",
    )(own, coup, lo, hi, before, after, clo, chi, left)


def ring(axis, by):
    size = lax.axis_size(axis)
    return [(i, (i + by) % size) for i in range(size)]


def shards(right_vectors, left_vectors, classes, class_energy, bond_mask_grid, order):
    rows_x, rows_y = classes.shape
    nright, nleft = right_vectors.shape[0], left_vectors.shape[0]
    nsx, nsy = lax.axis_size("sx"), lax.axis_size("sy")
    owned = nleft // nsy

    own, coup, top, bottom, first, last = prepare(right_vectors, classes, class_energy, bond_mask_grid)
    with jax.named_scope("halo_y"):
        before = lax.ppermute(last, "sy", ring("sy", 1))
        after = lax.ppermute(first, "sy", ring("sy", -1))
    with jax.named_scope("halo_x"):
        lo = lax.ppermute(bottom, "sx", ring("sx", 1))
        hi = lax.ppermute(top, "sx", ring("sx", -1))
    with jax.named_scope("halo_corner"):
        up = jnp.concatenate([before[-2:], after[-2:]], axis=0)
        down = jnp.concatenate([before[:1], before[-1:], after[:1], after[-1:]], axis=0)
        clo = lax.ppermute(up, "sx", ring("sx", 1))
        chi = lax.ppermute(down, "sx", ring("sx", -1))
    left = left_vectors.transpose(1, 0, 2)
    tile = moments_of_tile(own, coup, lo, hi, before, after, clo, chi, left, nsy)
    with jax.named_scope("reduce_sy"):
        mine = jnp.sum(lax.all_to_all(tile, "sy", 0, 0), axis=0)
    with jax.named_scope("reduce_sx"):
        shares = lax.all_to_all(jnp.broadcast_to(mine[None], (nsx,) + mine.shape), "sx", 0, 0)
    sites = rows_x * rows_y * nsx * nsy
    return pl.pallas_call(
        functools.partial(finish_kernel, -HALF_ROOT / TWICE / sites**0.5),
        out_shape=jax.ShapeDtypeStruct((MOMENTS, owned, nright), jnp.float32),
        in_specs=[pl.BlockSpec(memory_space=pltpu.SMEM), pl.BlockSpec(memory_space=pltpu.VMEM)],
        out_specs=pl.BlockSpec(memory_space=pltpu.VMEM),
        scratch_shapes=[pltpu.VMEM(mine.shape, jnp.float32)],
        compiler_params=pltpu.CompilerParams(vmem_limit_bytes=4 << 20),
        name="finish",
    )(order, shares)


def solution(mesh):
    in_specs = (
        P(None, "sx", "sy"),
        P(None, "sx", "sy"),
        P("sx", "sy"),
        P(),
        P(None, "sx", "sy"),
        P(),
    )
    out_specs = P(None, "sy", None)
    return jax.shard_map(shards, mesh=mesh, in_specs=in_specs, out_specs=out_specs, check_vma=False)
```

time: 93.4 us -> 86.6 us (0.927)
  blocking collectives: 40.2 us -> 34.9 us
  starting transfers between devices: 22.9 us -> 27.5 us
  local copies, waits for them, and re-layouts: 2.23 us -> 5.82 us
  other arithmetic: 3.21 us -> 0.03 us
  waiting for transfers between devices: 7.19 us -> 4.65 us
  between operations: 2.57 us -> 0.17 us
  Pallas kernels: 14.6 us -> 12.9 us
    all_to_all x1, blocking collectives: 17 us -> 12.3 us  [shards(): lax.all_to_all(jnp.broadcast_to(mine[None], (nsx,) + mine.shape), 'sx', 0...]
    unnamed x10 -> x15, local copies, waits for them, and re-layouts: 0.66 us -> 5.12 us
    ppermute x1, starting transfers between devices: 1.92 us -> 6.2 us  [shards(): after = lax.ppermute(first, 'sy', ring('sy', -1))]
    ppermute x1, waiting for transfers between devices: 2.94 us -> 0.01 us  [shards(): after = lax.ppermute(first, 'sy', ring('sy', -1))]
    pallas_call x2, Pallas kernels: 13.3 us -> 11.6 us  [the longest x1 10.7 us: moments_of_tile(): pl.pallas_call(main_kernel, out_shape=jax.ShapeDtypeStruct((groups, MOMEN...]
    unnamed x1 -> x0, other arithmetic: 1.37 us -> none
    ppermute x2 -> x4, waiting for transfers between devices: 4.24 us -> 4.65 us  [the longest x1 4.64 us: shards(): clo = lax.ppermute(up, 'sx', ring('sx', 1))]
    ppermute x2 -> x4, starting transfers between devices: 16.5 us -> 16.8 us  [the longest x1 9.43 us: shards(): hi = lax.ppermute(top, 'sx', ring('sx', -1))]
  transfers between devices with their start and end apart: 4 -> 6, of which waited for: 3 -> 1; matrix products, arithmetic and copies ran while one was open for 1% -> 2% of each run, Pallas kernels for 0% -> 0%
where the time goes in v2:
time: 86.6 us; the launch traced here: 86 us
  blocking collectives  34.9 us (40%)
  starting transfers between devices  27.5 us (32%)
  Pallas kernels  12.9 us (15%)
  local copies, waits for them, and re-layouts  5.82 us (7%)
  waiting for transfers between devices  4.65 us (5%)
    all_to_all x1, blocking collectives, shards(): mine = jnp.sum(lax.all_to_all(tile, 'sy', 0, 0), axis=0)  22.6 us
    all_to_all x1, blocking collectives, shards(): lax.all_to_all(jnp.broadcast_to(mine[None], (nsx,) + mine.shape), 'sx', 0...  12.3 us
    pallas_call x1, Pallas kernels, moments_of_tile(): pl.pallas_call(main_kernel, out_shape=jax.ShapeDtypeStruct((groups, MOMEN...  10.7 us
    ppermute x1, starting transfers between devices, shards(): hi = lax.ppermute(top, 'sx', ring('sx', -1))  9.43 us
    ppermute x1, starting transfers between devices, shards(): after = lax.ppermute(first, 'sy', ring('sy', -1))  6.2 us
    unnamed x15, local copies, waits for them, and re-layouts  5.12 us
    ppermute x1, waiting for transfers between devices, shards(): clo = lax.ppermute(up, 'sx', ring('sx', 1))  4.64 us
    ppermute x1, starting transfers between devices, shards(): before = lax.ppermute(last, 'sy', ring('sy', 1))  4.51 us
  transfers between devices with their start and end apart: 6, of which 1 were waited for; matrix products, arithmetic and copies ran while one was open for 2% of the time, Pallas kernels for 0%

profile of v2, /device:TPU:1, one launch (start us, length us, event | category | flops | bytes accessed | tf_op | source)
XLA Modules:
  0.0 86.0 jit_solution(6098526953328222858)
XLA Ops:
  0.0 0.0 copy-start
  0.0 1.0 %copy-done = bf16[32,32,256]{2,1,0:T(8,128)(2,1)S(1)} copy-done((bf16[32,32,256]{2,1,0:T(8,128)(2,1)S(1)}, bf16[32,32,256]{2,1,0:T(8,128)(2,1)}, u32[]{:S(2)}) %copy-start) | copy-done | bytes 524312
  1.0 0.0 copy-start.3
  1.0 0.8 copy-done.3
  1.9 0.0 copy-start.4
  1.9 0.8 copy-done.4
  2.6 0.0 copy-start.6
  2.6 0.7 copy-done.6
  3.3 1.0 %prepare.1 = (f32[32,32,256]{2,1,0:T(8,128)S(1)}, f32[3,32,256]{2,1,0:T(8,128)S(1)}, f32[216,256]{1,0:T(8,128)S(1)}, f32[216,256]{1,0:T(8,128)S(1)}, f32[5,8,128]{2,1,0:T(8,128)S(1)}, /*index=5*/f32[5,8,128]{2,1,0:T(8,128)S(1)}) custom-call(f32[4]{0:T(128)S(1)} %copy-done.6, bf16[32,32,256]{2,1,0:T(8,128)(2,1)S(1)} %copy-done, s32[32,256]{1,0:T(8,128)S(1)} %copy-done.4, ...), custom_call_target="tpu_custom_call" | custom-call | tf_op jit(solution)/shard_map/prepare/pallas_call | solution.py:104
  4.3 4.5 %collective-permute-start.2 = (f32[5,8,128]{2,1,0:T(8,128)S(1)}, f32[5,8,128]{2,1,0:T(8,128)S(1)}, u32[]{:S(2)}, u32[]{:S(2)}) collective-permute-start(f32[5,8,128]{2,1,0:T(8,128)S(1)} %get-tuple-element.15), channel_id=1, source_target_pairs={{0,1},{1,2},{2,3},{3,4},{4,5},{5,6},{6,7},{7,8},{8,9},{9,10},{10,1... | collective-permute-start | bytes 61448 | tf_op jit(solution)/shard_map/halo_y/ppermute | solution.py:353
  8.8 6.2 %collective-permute-start.3 = (f32[5,8,128]{2,1,0:T(8,128)S(1)}, f32[5,8,128]{2,1,0:T(8,128)S(1)}, u32[]{:S(2)}, u32[]{:S(2)}) collective-permute-start(f32[5,8,128]{2,1,0:T(8,128)S(1)} %get-tuple-element.16), channel_id=1, source_target_pairs={{0,15},{1,0},{2,1},{3,2},{4,3},{5,4},{6,5},{7,6},{8,7},{9,8},{10,9... | collective-permute-start | bytes 61448 | tf_op jit(solution)/shard_map/halo_y/ppermute | solution.py:354
  15.0 1.9 %collective-permute-start = (f32[216,256]{1,0:T(8,128)S(1)}, f32[216,256]{1,0:T(8,128)S(1)}, u32[]{:S(2)}, u32[]{:S(2)}) collective-permute-start(f32[216,256]{1,0:T(8,128)S(1)} %get-tuple-element.13), channel_id=1, source_target_pairs={{0,16},{16,32},{32,48},{48,64},{64,80},{80,96},{96,112},{112,128},... | collective-permute-start | bytes 663560 | tf_op jit(solution)/shard_map/halo_x/ppermute | solution.py:356
  16.9 9.4 %collective-permute-start.1 = (f32[216,256]{1,0:T(8,128)S(1)}, f32[216,256]{1,0:T(8,128)S(1)}, u32[]{:S(2)}, u32[]{:S(2)}) collective-permute-start(f32[216,256]{1,0:T(8,128)S(1)} %get-tuple-element.14), channel_id=1, source_target_pairs={{0,496},{16,0},{32,16},{48,32},{64,48},{80,64},{96,80},{112,96},{1... | collective-permute-start | bytes 663560 | tf_op jit(solution)/shard_map/halo_x/ppermute | solution.py:357
  26.4 0.0 collective-permute-done.2.before_ref
  26.4 0.0 copy-start.1
  26.4 0.0 collective-permute-done.3.after_ref
  26.4 3.4 %collective-permute-start.5 = (f32[4,8,128]{2,1,0:T(8,128)S(1)}, f32[4,8,128]{2,1,0:T(8,128)S(1)}, u32[]{:S(2)}, u32[]{:S(2)}) collective-permute-start(f32[4,8,128]{2,1,0:T(8,128)S(1)} %pad_maximum_fusion.1), channel_id=1, source_target_pairs={{0,496},{16,0},{32,16},{48,32},{64,48},{80,64},{96,80},{112,96},{1... | collective-permute-start | bytes 49160 | tf_op jit(solution)/shard_map/halo_corner/ppermute | solution.py:362
  29.8 0.0 copy-done.1
  29.8 0.0 slice-start
  29.8 0.7 slice-done
  30.5 0.0 copy-start.2
  30.5 2.0 %collective-permute-start.4 = (f32[4,8,128]{2,1,0:T(8,128)S(1)}, f32[4,8,128]{2,1,0:T(8,128)S(1)}, u32[]{:S(2)}, u32[]{:S(2)}) collective-permute-start(f32[4,8,128]{2,1,0:T(8,128)S(1)} %pad_maximum_fusion), channel_id=1, source_target_pairs={{0,16},{16,32},{32,48},{48,64},{64,80},{80,96},{96,112},{112,128},... | collective-permute-start | bytes 49160 | tf_op jit(solution)/shard_map/halo_corner/ppermute | solution.py:361
  32.6 1.8 %copy.9 = bf16[64,32,256]{2,0,1:T(8,128)(2,1)S(1)} copy(bf16[64,32,256]{2,1,0:T(8,128)(2,1)} %param.7) | data formatting | bytes 2097152 | tf_op args[1]
  34.4 0.0 collective-permute-done.5.chi_ref
  34.4 4.6 %collective-permute-done.4.clo_ref = f32[4,8,128]{2,1,0:T(8,128)S(1)} collective-permute-done((f32[4,8,128]{2,1,0:T(8,128)S(1)}, f32[4,8,128]{2,1,0:T(8,128)S(1)}, u32[]{:S(2)}, u32[]{:S(2)}) %collective-permute-start.4) | collective-permute-done | bytes 16416 | tf_op jit(solution)/shard_map/halo_corner/ppermute | solution.py:361
  39.0 0.0 collective-permute-done.lo_ref
  39.0 0.0 collective-permute-done.1.hi_ref
  39.0 0.0 copy-done.2
  39.0 10.7 %chebyshev_moments.1 = f32[16,5,128]{2,1,0:T(8,128)S(1)} custom-call(f32[32,32,256]{2,1,0:T(8,128)S(1)} %get-tuple-element.11.own_ref, f32[3,32,256]{2,1,0:T(8,128)S(1)} %get-tuple-element.12.coup_ref, f32[216,256]{1,0:T(8,128)S(1)} %collective-permute-done.lo_ref, f32[216,256]{1,0:T(8,128)S(1)} %collective-permute-done.1.hi_ref, ...), custom_call_target="tpu_custom_call" | custom-call | tf_op jit(solution)/shard_map/chebyshev_moments/pallas_call | solution.py:323
  49.7 22.6 %all_to_all.10 = f32[16,5,128]{2,1,0:T(8,128)S(1)} all-to-all(f32[16,5,128]{2,1,0:T(8,128)S(1)} %chebyshev_moments.1), channel_id=1, replica_groups=mesh['sx'=32,'sy'=16] {'sy'}, dimensions={0} | all-to-all | bytes 81920 | tf_op jit(solution)/shard_map/reduce_sy/all_to_all | solution.py:366
  72.3 0.0 copy-start.5
  72.4 12.3 %all_to_all.11.blocks_ref = f32[32,5,128]{2,1,0:T(8,128)S(1)} all-to-all(f32[32,5,128]{2,1,0:T(8,128)S(1)} %broadcast_in_dim.2), channel_id=1, replica_groups=mesh['sx'=32,'sy'=16] {'sx'}, dimensions={0} | all-to-all | bytes 163840 | tf_op jit(solution)/shard_map/reduce_sx/all_to_all | solution.py:368
  84.7 0.0 copy-done.5
  84.7 1.3 %finish.1 = f32[5,4,32]{2,1,0:T(4,128)} custom-call(s32[5]{0:T(128)S(1)} %copy-done.5, f32[32,5,128]{2,1,0:T(8,128)S(1)} %all_to_all.11.blocks_ref), custom_call_target="tpu_custom_call" | custom-call | tf_op jit(solution)/shard_map/finish/pallas_call | solution.py:370
  (7 shorter events, 0.1 us)
Async XLA Ops:
  0.0 1.0 %copy-start = (bf16[32,32,256]{2,1,0:T(8,128)(2,1)S(1)}, bf16[32,32,256]{2,1,0:T(8,128)(2,1)}, u32[]{:S(2)}) copy-start(bf16[32,32,256]{2,1,0:T(8,128)(2,1)} %right_ref.1) | copy-start | bytes 1572868
  1.0 0.8 copy-start.3
  1.9 0.8 copy-start.4
  2.6 0.7 copy-start.6
  4.3 22.1 %collective-permute-start.2 = (f32[5,8,128]{2,1,0:T(8,128)S(1)}, f32[5,8,128]{2,1,0:T(8,128)S(1)}, u32[]{:S(2)}, u32[]{:S(2)}) collective-permute-start(f32[5,8,128]{2,1,0:T(8,128)S(1)} %get-tuple-element.15), channel_id=1, source_target_pairs={{0,1},{1,2},{2,3},{3,4},{4,5},{5,6},{6,7},{7,8},{8,9},{9,10},{10,1... | collective-permute-start | bytes 61448 | tf_op jit(solution)/shard_map/halo_y/ppermute | solution.py:353
  8.8 17.6 %collective-permute-start.3 = (f32[5,8,128]{2,1,0:T(8,128)S(1)}, f32[5,8,128]{2,1,0:T(8,128)S(1)}, u32[]{:S(2)}, u32[]{:S(2)}) collective-permute-start(f32[5,8,128]{2,1,0:T(8,128)S(1)} %get-tuple-element.16), channel_id=1, source_target_pairs={{0,15},{1,0},{2,1},{3,2},{4,3},{5,4},{6,5},{7,6},{8,7},{9,8},{10,9... | collective-permute-start | bytes 61448 | tf_op jit(solution)/shard_map/halo_y/ppermute | solution.py:354
  15.0 24.0 %collective-permute-start = (f32[216,256]{1,0:T(8,128)S(1)}, f32[216,256]{1,0:T(8,128)S(1)}, u32[]{:S(2)}, u32[]{:S(2)}) collective-permute-start(f32[216,256]{1,0:T(8,128)S(1)} %get-tuple-element.13), channel_id=1, source_target_pairs={{0,16},{16,32},{32,48},{48,64},{64,80},{80,96},{96,112},{112,128},... | collective-permute-start | bytes 663560 | tf_op jit(solution)/shard_map/halo_x/ppermute | solution.py:356
  16.9 22.1 %collective-permute-start.1 = (f32[216,256]{1,0:T(8,128)S(1)}, f32[216,256]{1,0:T(8,128)S(1)}, u32[]{:S(2)}, u32[]{:S(2)}) collective-permute-start(f32[216,256]{1,0:T(8,128)S(1)} %get-tuple-element.14), channel_id=1, source_target_pairs={{0,496},{16,0},{32,16},{48,32},{64,48},{80,64},{96,80},{112,96},{1... | collective-permute-start | bytes 663560 | tf_op jit(solution)/shard_map/halo_x/ppermute | solution.py:357
  26.4 3.4 %copy-start.1 = (f32[5,8,128]{2,1,0:T(8,128)}, f32[5,8,128]{2,1,0:T(8,128)S(1)}, u32[]{:S(2)}) copy-start(f32[5,8,128]{2,1,0:T(8,128)S(1)} %collective-permute-done.2.before_ref) | copy-start | bytes 61444
  26.4 7.9 %collective-permute-start.5 = (f32[4,8,128]{2,1,0:T(8,128)S(1)}, f32[4,8,128]{2,1,0:T(8,128)S(1)}, u32[]{:S(2)}, u32[]{:S(2)}) collective-permute-start(f32[4,8,128]{2,1,0:T(8,128)S(1)} %pad_maximum_fusion.1), channel_id=1, source_target_pairs={{0,496},{16,0},{32,16},{48,32},{64,48},{80,64},{96,80},{112,96},{1... | collective-permute-start | bytes 49160 | tf_op jit(solution)/shard_map/halo_corner/ppermute | solution.py:362
  29.8 0.7 slice-start
  30.5 8.5 %copy-start.2 = (f32[5,8,128]{2,1,0:T(8,128)S(1)}, f32[5,8,128]{2,1,0:T(8,128)}, u32[]{:S(2)}) copy-start(f32[5,8,128]{2,1,0:T(8,128)} %copy-done.1) | copy-start | bytes 61444
  30.5 8.5 %collective-permute-start.4 = (f32[4,8,128]{2,1,0:T(8,128)S(1)}, f32[4,8,128]{2,1,0:T(8,128)S(1)}, u32[]{:S(2)}, u32[]{:S(2)}) collective-permute-start(f32[4,8,128]{2,1,0:T(8,128)S(1)} %pad_maximum_fusion), channel_id=1, source_target_pairs={{0,16},{16,32},{32,48},{48,64},{64,80},{80,96},{96,112},{112,128},... | collective-permute-start | bytes 49160 | tf_op jit(solution)/shard_map/halo_corner/ppermute | solution.py:361
  72.3 12.3 %copy-start.5 = (s32[5]{0:T(128)S(1)}, s32[5]{0:T(128)}, u32[]{:S(2)}) copy-start(s32[5]{0:T(128)} %order_ref.1) | copy-start | bytes 64

commit v3 on v2

--- a/solution.py
+++ b/solution.py
@@ -40,7 +40,15 @@
     return blocks
 
 
-def prepare_kernel(energy_ref, right_ref, class_ref, bond_ref, own_ref, coup_ref, top_ref, bottom_ref, first_ref, last_ref):
+def prepare_kernel(*refs):
+    sources, outputs, held, sems = refs[:4], refs[4:10], refs[10:14], refs[14]
+    copies = [pltpu.make_async_copy(a, b, sems.at[n]) for n, (a, b) in enumerate(zip(sources, held))]
+    for copy in copies:
+        copy.start()
+    for copy in copies:
+        copy.wait()
+    energy_ref, right_ref, class_ref, bond_ref = held
+    own_ref, coup_ref, top_ref, bottom_ref, first_ref, last_ref = outputs
     nright, rows, width = right_ref.shape
     lane = lane_iota()
     sub = lax.broadcasted_iota(jnp.int32, (SUB, LANES), 0)
@@ -111,9 +119,15 @@
             strip,
             strip,
         ),
-        in_specs=[pl.BlockSpec(memory_space=pltpu.SMEM)] + [pl.BlockSpec(memory_space=pltpu.VMEM)] * 3,
+        in_specs=[pl.BlockSpec(memory_space=pltpu.HBM)] * 4,
         out_specs=(pl.BlockSpec(memory_space=pltpu.VMEM),) * 6,
-        compiler_params=pltpu.CompilerParams(vmem_limit_bytes=8 << 20),
+        scratch_shapes=[
+            pltpu.SMEM(energy.shape, energy.dtype),
+            pltpu.VMEM(right.shape, right.dtype),
+            pltpu.VMEM(classes.shape, classes.dtype),
+            pltpu.VMEM(bonds.shape, bonds.dtype),
+            pltpu.SemaphoreType.DMA((4,)),
+        ],
         name="prepare",
     )(energy, right, classes, bonds)
 
@@ -124,7 +138,7 @@
     return jnp.take_along_axis(block, target, axis=1)
 
 
-def main_kernel(own_ref, coup_ref, lo_ref, hi_ref, before_ref, after_ref, clo_ref, chi_ref, left_ref, out_ref, field, rim, coup, acc, spaced):
+def main_kernel(own_ref, coup_ref, lo_ref, hi_ref, before_ref, after_ref, clo_ref, chi_ref, left_ref, out_ref, field, rim, coup, open_bond, acc, spaced):
     rows_x, nright, width = own_ref.shape
     rows = rows_x + 2 * DEPTH
     rtiles, inner, xtiles = nright // SUB, width // LANES, rows_x // SUB
@@ -203,7 +217,11 @@
             if 0 <= e < rows:
                 for c in range(COUPLINGS):
                     for i in range(inner + 1):
-                        coup[e, c, :, lanes_of(i)] = jnp.broadcast_to(whole[c][i][s : s + 1], (SUB, LANES))
+                        wide = jnp.broadcast_to(whole[c][i][s : s + 1], (SUB, LANES))
+                        coup[e, c, :, lanes_of(i)] = wide
+                        if c == 0 and i < inner:
+                            shown = (wide > 0.0).astype(jnp.float32)
+                            open_bond[e, :, lanes_of(i)] = jnp.concatenate([shown, shown], axis=0).astype(jnp.bfloat16)
 
     acc[...] = jnp.zeros_like(acc)
 
@@ -258,34 +276,34 @@
             else:
                 field[k + 1, row, t * SUB : (t + 1) * SUB, lanes_of(i)] = new[t, i]
 
-    def contract(row):
-        east = [coupling(0, row, i) for i in range(inner)]
-        west = [coupling(0, row - 1, i) for i in range(inner)]
-        high, low = [], []
-        for k in range(MOMENTS):
-            parts = []
-            for t in range(rtiles):
-                parts.append(
-                    jnp.concatenate(
-                        [
-                            east[i] * load(k + 1, row + 1, t, i) - west[i] * load(k + 1, row - 1, t, i)
-                            for i in range(inner)
-                        ],
-                        axis=1,
-                    )
-                )
-            value = jnp.concatenate(parts, axis=0)
-            top = value.astype(jnp.bfloat16)
-            high.append(top)
-            low.append((value - top.astype(jnp.float32)).astype(jnp.bfloat16))
-        block = left_ref[row - DEPTH]
-        dims = (((1,), (1,)), ((), ()))
+    def contract(row, below=True, above=True):
+        parts = []
+        for t in range(rtiles * MOMENTS):
+            k, q = divmod(t, rtiles)
+            parts.append(field[k + 1, row, q * SUB : (q + 1) * SUB, :])
+        value = jnp.concatenate(parts, axis=0)
+        high = value.astype(jnp.bfloat16)
+        low = (value - high.astype(jnp.float32)).astype(jnp.bfloat16)
+        sides = []
+        for there, bond, wanted in ((row - 1, row - 1, below), (row + 1, row, above)):
+            for q in range(left_ref.shape[1] // (2 * SUB)):
+                if wanted:
+                    sides.append(left_ref[there - DEPTH, q * 2 * SUB : (q + 1) * 2 * SUB, :] * open_bond[bond])
+                else:
+                    sides.append(jnp.zeros((2 * SUB, width), jnp.bfloat16))
+        block = jnp.concatenate(sides, axis=0)
         acc[...] += lax.dot_general(
-            block, jnp.concatenate(high, axis=0), dims, preferred_element_type=jnp.float32
-        ) + lax.dot_general(block, jnp.concatenate(low, axis=0), dims, preferred_element_type=jnp.float32)
-
-    lead = DEPTH + 2 * MOMENTS
+            jnp.concatenate([high, low], axis=1),
+            jnp.concatenate([block, block], axis=1),
+            (((1,), (1,)), ((), ())),
+            preferred_element_type=jnp.float32,
+        )
+
+    lag = 2 * MOMENTS - 1
+    lead = DEPTH + 1 + lag
     for front in range(1, lead):
+        if front >= lead - 2:
+            contract(front - lag, below=False)
         for k in reversed(range(MOMENTS)):
             if front >= 3 * k + 1:
                 advance(k, front - 2 * k, front % 2 == 1)
@@ -293,16 +311,23 @@
     def both(n, _):
         for part in range(2):
             front = lead + 2 * n + part
-            contract(front - 2 * MOMENTS)
+            contract(front - lag)
             for k in reversed(range(MOMENTS)):
                 advance(k, front - 2 * k, (lead + part) % 2 == 1)
         return 0
 
-    lax.fori_loop(0, rows_x // 2, both, 0)
+    lax.fori_loop(0, rows_x // 2 - 1, both, 0)
+    end = rows_x + DEPTH
+    advance(MOMENTS - 1, end, end % 2 == 1)
+    contract(end - 1, above=False)
+    contract(end, above=False)
     groups, _, flat = out_ref.shape
     owned = flat // nright
+    both_sides = acc[...].T
+    half = both_sides.shape[0] // 2
+    total = both_sides[:half] - both_sides[half:]
     for k in range(MOMENTS):
-        spaced[:, 0:nright] = acc[:, k * nright : (k + 1) * nright]
+        spaced[:, 0:nright] = total[:, k * nright : (k + 1) * nright]
         rows_of = [spaced[pl.ds(q, groups, stride=owned), :] for q in range(owned)]
         out_ref[:, k, :] = jnp.concatenate([r[:, 0:nright] for r in rows_of], axis=1)
 
@@ -329,7 +354,8 @@
             pltpu.VMEM((MOMENTS + 1, rows, nright, width), jnp.float32),
             pltpu.VMEM((MOMENTS + 1, rows, SUB, LANES), jnp.float32),
             pltpu.VMEM((rows, COUPLINGS, SUB, width + LANES), jnp.float32),
-            pltpu.VMEM((nleft, MOMENTS * nright), jnp.float32),
+            pltpu.VMEM((rows, 2 * SUB, width), jnp.bfloat16),
+            pltpu.VMEM((MOMENTS * nright, 2 * nleft), jnp.float32),
             pltpu.VMEM((nleft, LANES), jnp.float32),
         ],
         compiler_params=pltpu.CompilerParams(vmem_limit_bytes=28 << 20),
@@ -368,7 +394,7 @@
         shares = lax.all_to_all(jnp.broadcast_to(mine[None], (nsx,) + mine.shape), "sx", 0, 0)
     sites = rows_x * rows_y * nsx * nsy
     return pl.pallas_call(
-        functools.partial(finish_kernel, -HALF_ROOT / TWICE / sites**0.5),
+        functools.partial(finish_kernel, -HALF_ROOT / sites**0.5),
         out_shape=jax.ShapeDtypeStruct((MOMENTS, owned, nright), jnp.float32),
         in_specs=[pl.BlockSpec(memory_space=pltpu.SMEM), pl.BlockSpec(memory_space=pltpu.VMEM)],
         out_specs=pl.BlockSpec(memory_space=pltpu.VMEM),

time: 86.6 us -> 85.3 us (0.985)
  local copies, waits for them, and re-layouts: 5.82 us -> 2.54 us
  Pallas kernels: 12.9 us -> 15.1 us
    unnamed x15 -> x11, local copies, waits for them, and re-layouts: 5.12 us -> 1.83 us
    pallas_call x1, Pallas kernels: 0.98 us -> 2.67 us  [prepare(): pl.pallas_call(prepare_kernel, out_shape=(jax.ShapeDtypeStruct((rows, nri...]
where the time goes in v3:
time: 85.3 us; the launch traced here: 84.9 us
  blocking collectives  34.9 us (41%)
  starting transfers between devices  27.5 us (32%)
  Pallas kernels  15.1 us (18%)
  waiting for transfers between devices  4.65 us (5%)
  local copies, waits for them, and re-layouts  2.54 us (3%)
    all_to_all x1, blocking collectives, shards(): mine = jnp.sum(lax.all_to_all(tile, 'sy', 0, 0), axis=0)  22.6 us
    all_to_all x1, blocking collectives, shards(): lax.all_to_all(jnp.broadcast_to(mine[None], (nsx,) + mine.shape), 'sx', 0...  12.3 us
    pallas_call x1, Pallas kernels, moments_of_tile(): pl.pallas_call(main_kernel, out_shape=jax.ShapeDtypeStruct((groups, MOMEN...  11.1 us
    ppermute x1, starting transfers between devices, shards(): hi = lax.ppermute(top, 'sx', ring('sx', -1))  9.43 us
    ppermute x1, starting transfers between devices, shards(): after = lax.ppermute(first, 'sy', ring('sy', -1))  6.2 us
    ppermute x1, waiting for transfers between devices, shards(): clo = lax.ppermute(up, 'sx', ring('sx', 1))  4.64 us
    ppermute x1, starting transfers between devices, shards(): before = lax.ppermute(last, 'sy', ring('sy', 1))  4.51 us
    ppermute x1, starting transfers between devices, shards(): chi = lax.ppermute(down, 'sx', ring('sx', -1))  3.36 us
  transfers between devices with their start and end apart: 6, of which 1 were waited for; matrix products, arithmetic and copies ran while one was open for 2% of the time, Pallas kernels for 0%

profile of v3, /device:TPU:1, one launch (start us, length us, event | category | flops | bytes accessed | tf_op | source)
XLA Modules:
  0.0 84.9 jit_solution(15494929261621180496)
XLA Ops:
  0.0 2.7 %prepare.1 = (f32[32,32,256]{2,1,0:T(8,128)}, f32[3,32,256]{2,1,0:T(8,128)}, f32[216,256]{1,0:T(8,128)}, f32[216,256]{1,0:T(8,128)}, f32[5,8,128]{2,1,0:T(8,128)}, /*index=5*/f32[5,8,128]{2,1,0:T(8,128)}) custom-call(f32[4]{0:T(128)} %refs_0_.1, bf16[32,32,256]{2,1,0:T(8,128)(2,1)} %refs_1_.1, s32[32,256]{1,0:T(8,128)} %refs_2_.1, s32[2,32,256]{2,1,0:T(8,128)} %refs_3_.1), custom_call_target="tpu_custom_call" | custom-call | tf_op jit(solution)/shard_map/prepare/pallas_call | solution.py:112
  2.7 4.5 %collective-permute-start.2 = (f32[5,8,128]{2,1,0:T(8,128)}, f32[5,8,128]{2,1,0:T(8,128)S(1)}, u32[]{:S(2)}, u32[]{:S(2)}) collective-permute-start(f32[5,8,128]{2,1,0:T(8,128)} %get-tuple-element.15), channel_id=1, source_target_pairs={{0,1},{1,2},{2,3},{3,4},{4,5},{5,6},{6,7},{7,8},{8,9},{9,10},{10,1... | collective-permute-start | bytes 61448 | tf_op jit(solution)/shard_map/halo_y/ppermute | solution.py:379
  7.2 6.2 %collective-permute-start.3 = (f32[5,8,128]{2,1,0:T(8,128)}, f32[5,8,128]{2,1,0:T(8,128)S(1)}, u32[]{:S(2)}, u32[]{:S(2)}) collective-permute-start(f32[5,8,128]{2,1,0:T(8,128)} %get-tuple-element.16), channel_id=1, source_target_pairs={{0,15},{1,0},{2,1},{3,2},{4,3},{5,4},{6,5},{7,6},{8,7},{9,8},{10,9... | collective-permute-start | bytes 61448 | tf_op jit(solution)/shard_map/halo_y/ppermute | solution.py:380
  13.4 1.9 %collective-permute-start = (f32[216,256]{1,0:T(8,128)}, f32[216,256]{1,0:T(8,128)S(1)}, u32[]{:S(2)}, u32[]{:S(2)}) collective-permute-start(f32[216,256]{1,0:T(8,128)} %get-tuple-element.13), channel_id=1, source_target_pairs={{0,16},{16,32},{32,48},{48,64},{64,80},{80,96},{96,112},{112,128},... | collective-permute-start | bytes 663560 | tf_op jit(solution)/shard_map/halo_x/ppermute | solution.py:382
  15.3 9.4 %collective-permute-start.1 = (f32[216,256]{1,0:T(8,128)}, f32[216,256]{1,0:T(8,128)S(1)}, u32[]{:S(2)}, u32[]{:S(2)}) collective-permute-start(f32[216,256]{1,0:T(8,128)} %get-tuple-element.14), channel_id=1, source_target_pairs={{0,496},{16,0},{32,16},{48,32},{64,48},{80,64},{96,80},{112,96},{1... | collective-permute-start | bytes 663560 | tf_op jit(solution)/shard_map/halo_x/ppermute | solution.py:383
  24.8 0.0 collective-permute-done.2.before_ref
  24.8 0.0 copy-start.2
  24.8 0.0 collective-permute-done.3.after_ref
  24.8 3.4 %collective-permute-start.5 = (f32[4,8,128]{2,1,0:T(8,128)S(1)}, f32[4,8,128]{2,1,0:T(8,128)S(1)}, u32[]{:S(2)}, u32[]{:S(2)}) collective-permute-start(f32[4,8,128]{2,1,0:T(8,128)S(1)} %pad_maximum_fusion.1), channel_id=1, source_target_pairs={{0,496},{16,0},{32,16},{48,32},{64,48},{80,64},{96,80},{112,96},{1... | collective-permute-start | bytes 49160 | tf_op jit(solution)/shard_map/halo_corner/ppermute | solution.py:388
  28.2 0.0 copy-done.2
  28.2 0.0 slice-start
  28.2 0.7 slice-done
  28.9 0.0 copy-start
  28.9 0.0 copy-start.1
  28.9 0.0 copy-start.3
  28.9 2.1 %collective-permute-start.4 = (f32[4,8,128]{2,1,0:T(8,128)S(1)}, f32[4,8,128]{2,1,0:T(8,128)S(1)}, u32[]{:S(2)}, u32[]{:S(2)}) collective-permute-start(f32[4,8,128]{2,1,0:T(8,128)S(1)} %pad_maximum_fusion), channel_id=1, source_target_pairs={{0,16},{16,32},{32,48},{48,64},{64,80},{80,96},{96,112},{112,128},... | collective-permute-start | bytes 49160 | tf_op jit(solution)/shard_map/halo_corner/ppermute | solution.py:387
  31.0 1.8 %copy.9 = bf16[64,32,256]{2,0,1:T(8,128)(2,1)S(1)} copy(bf16[64,32,256]{2,1,0:T(8,128)(2,1)} %param.7) | data formatting | bytes 2097152 | tf_op args[1]
  32.8 0.0 collective-permute-done.5.chi_ref
  32.8 4.6 %collective-permute-done.4.clo_ref = f32[4,8,128]{2,1,0:T(8,128)S(1)} collective-permute-done((f32[4,8,128]{2,1,0:T(8,128)S(1)}, f32[4,8,128]{2,1,0:T(8,128)S(1)}, u32[]{:S(2)}, u32[]{:S(2)}) %collective-permute-start.4) | collective-permute-done | bytes 16416 | tf_op jit(solution)/shard_map/halo_corner/ppermute | solution.py:387
  37.4 0.0 collective-permute-done.lo_ref
  37.4 0.0 collective-permute-done.1.hi_ref
  37.5 0.0 copy-done
  37.5 0.0 copy-done.1
  37.5 0.0 copy-done.3
  37.5 11.1 %chebyshev_moments.1 = f32[16,5,128]{2,1,0:T(8,128)S(1)} custom-call(f32[32,32,256]{2,1,0:T(8,128)S(1)} %copy-done, f32[3,32,256]{2,1,0:T(8,128)S(1)} %copy-done.1, f32[216,256]{1,0:T(8,128)S(1)} %collective-permute-done.lo_ref, f32[216,256]{1,0:T(8,128)S(1)} %collective-permute-done.1.hi_ref, f32[5,8,128]{2,1,0:T(8,128)S(1)} %copy-done.3, ...), custom_call_target="tpu_custom_call" | custom-call | tf_op jit(solution)/shard_map/chebyshev_moments/pallas_call | solution.py:348
  48.6 22.6 %all_to_all.10 = f32[16,5,128]{2,1,0:T(8,128)S(1)} all-to-all(f32[16,5,128]{2,1,0:T(8,128)S(1)} %chebyshev_moments.1), channel_id=1, replica_groups=mesh['sx'=32,'sy'=16] {'sy'}, dimensions={0} | all-to-all | bytes 81920 | tf_op jit(solution)/shard_map/reduce_sy/all_to_all | solution.py:392
  71.2 0.0 copy-start.4
  71.3 12.3 %all_to_all.11.blocks_ref = f32[32,5,128]{2,1,0:T(8,128)S(1)} all-to-all(f32[32,5,128]{2,1,0:T(8,128)S(1)} %broadcast_in_dim.2), channel_id=1, replica_groups=mesh['sx'=32,'sy'=16] {'sx'}, dimensions={0} | all-to-all | bytes 163840 | tf_op jit(solution)/shard_map/reduce_sx/all_to_all | solution.py:394
  83.6 0.0 copy-done.4
  83.6 1.3 %finish.1 = f32[5,4,32]{2,1,0:T(4,128)} custom-call(s32[5]{0:T(128)S(1)} %copy-done.4, f32[32,5,128]{2,1,0:T(8,128)S(1)} %all_to_all.11.blocks_ref), custom_call_target="tpu_custom_call" | custom-call | tf_op jit(solution)/shard_map/finish/pallas_call | solution.py:396
  (7 shorter events, 0.1 us)
Async XLA Ops:
  2.7 22.1 %collective-permute-start.2 = (f32[5,8,128]{2,1,0:T(8,128)}, f32[5,8,128]{2,1,0:T(8,128)S(1)}, u32[]{:S(2)}, u32[]{:S(2)}) collective-permute-start(f32[5,8,128]{2,1,0:T(8,128)} %get-tuple-element.15), channel_id=1, source_target_pairs={{0,1},{1,2},{2,3},{3,4},{4,5},{5,6},{6,7},{7,8},{8,9},{9,10},{10,1... | collective-permute-start | bytes 61448 | tf_op jit(solution)/shard_map/halo_y/ppermute | solution.py:379
  7.2 17.6 %collective-permute-start.3 = (f32[5,8,128]{2,1,0:T(8,128)}, f32[5,8,128]{2,1,0:T(8,128)S(1)}, u32[]{:S(2)}, u32[]{:S(2)}) collective-permute-start(f32[5,8,128]{2,1,0:T(8,128)} %get-tuple-element.16), channel_id=1, source_target_pairs={{0,15},{1,0},{2,1},{3,2},{4,3},{5,4},{6,5},{7,6},{8,7},{9,8},{10,9... | collective-permute-start | bytes 61448 | tf_op jit(solution)/shard_map/halo_y/ppermute | solution.py:380
  13.4 24.0 %collective-permute-start = (f32[216,256]{1,0:T(8,128)}, f32[216,256]{1,0:T(8,128)S(1)}, u32[]{:S(2)}, u32[]{:S(2)}) collective-permute-start(f32[216,256]{1,0:T(8,128)} %get-tuple-element.13), channel_id=1, source_target_pairs={{0,16},{16,32},{32,48},{48,64},{64,80},{80,96},{96,112},{112,128},... | collective-permute-start | bytes 663560 | tf_op jit(solution)/shard_map/halo_x/ppermute | solution.py:382
  15.3 22.1 %collective-permute-start.1 = (f32[216,256]{1,0:T(8,128)}, f32[216,256]{1,0:T(8,128)S(1)}, u32[]{:S(2)}, u32[]{:S(2)}) collective-permute-start(f32[216,256]{1,0:T(8,128)} %get-tuple-element.14), channel_id=1, source_target_pairs={{0,496},{16,0},{32,16},{48,32},{64,48},{80,64},{96,80},{112,96},{1... | collective-permute-start | bytes 663560 | tf_op jit(solution)/shard_map/halo_x/ppermute | solution.py:383
  24.8 3.4 %copy-start.2 = (f32[5,8,128]{2,1,0:T(8,128)}, f32[5,8,128]{2,1,0:T(8,128)S(1)}, u32[]{:S(2)}) copy-start(f32[5,8,128]{2,1,0:T(8,128)S(1)} %collective-permute-done.2.before_ref) | copy-start | bytes 61444
  24.8 8.0 %collective-permute-start.5 = (f32[4,8,128]{2,1,0:T(8,128)S(1)}, f32[4,8,128]{2,1,0:T(8,128)S(1)}, u32[]{:S(2)}, u32[]{:S(2)}) collective-permute-start(f32[4,8,128]{2,1,0:T(8,128)S(1)} %pad_maximum_fusion.1), channel_id=1, source_target_pairs={{0,496},{16,0},{32,16},{48,32},{64,48},{80,64},{96,80},{112,96},{1... | collective-permute-start | bytes 49160 | tf_op jit(solution)/shard_map/halo_corner/ppermute | solution.py:388
  28.2 0.7 slice-start
  28.9 8.5 %copy-start = (f32[32,32,256]{2,1,0:T(8,128)S(1)}, f32[32,32,256]{2,1,0:T(8,128)}, u32[]{:S(2)}) copy-start(f32[32,32,256]{2,1,0:T(8,128)} %get-tuple-element.11.own_ref) | copy-start | bytes 3145732
  28.9 8.5 %copy-start.1 = (f32[3,32,256]{2,1,0:T(8,128)S(1)}, f32[3,32,256]{2,1,0:T(8,128)}, u32[]{:S(2)}) copy-start(f32[3,32,256]{2,1,0:T(8,128)} %get-tuple-element.12.coup_ref) | copy-start | bytes 294916
  28.9 8.6 %copy-start.3 = (f32[5,8,128]{2,1,0:T(8,128)S(1)}, f32[5,8,128]{2,1,0:T(8,128)}, u32[]{:S(2)}) copy-start(f32[5,8,128]{2,1,0:T(8,128)} %copy-done.2) | copy-start | bytes 61444
  28.9 8.5 %collective-permute-start.4 = (f32[4,8,128]{2,1,0:T(8,128)S(1)}, f32[4,8,128]{2,1,0:T(8,128)S(1)}, u32[]{:S(2)}, u32[]{:S(2)}) collective-permute-start(f32[4,8,128]{2,1,0:T(8,128)S(1)} %pad_maximum_fusion), channel_id=1, source_target_pairs={{0,16},{16,32},{32,48},{48,64},{64,80},{80,96},{96,112},{112,128},... | collective-permute-start | bytes 49160 | tf_op jit(solution)/shard_map/halo_corner/ppermute | solution.py:387
  71.2 12.3 %copy-start.4 = (s32[5]{0:T(128)S(1)}, s32[5]{0:T(128)}, u32[]{:S(2)}) copy-start(s32[5]{0:T(128)} %order_ref.1) | copy-start | bytes 64

commit v4 on v3

--- a/solution.py
+++ b/solution.py
@@ -138,56 +138,16 @@
     return jnp.take_along_axis(block, target, axis=1)
 
 
-def main_kernel(own_ref, coup_ref, lo_ref, hi_ref, before_ref, after_ref, clo_ref, chi_ref, left_ref, out_ref, field, rim, coup, open_bond, acc, spaced):
-    rows_x, nright, width = own_ref.shape
-    rows = rows_x + 2 * DEPTH
-    rtiles, inner, xtiles = nright // SUB, width // LANES, rows_x // SUB
+def coupling_rows(blocks_of, strips_of, groups, xtiles, inner, coup, open_bond, rows):
     lane = lane_iota()
     sub = lax.broadcasted_iota(jnp.int32, (SUB, LANES), 0)
     zero = jnp.zeros((SUB, LANES), jnp.float32)
-
-    def lanes_of(i):
-        return slice(i * LANES, (i + 1) * LANES)
-
-    for e in range(rows):
-        x = (e - DEPTH) % rows_x
-        if e < DEPTH:
-            before, after = clo_ref[0], clo_ref[2]
-        elif e >= DEPTH + rows_x:
-            before, after = chi_ref[0], chi_ref[2]
-        else:
-            before, after = before_ref[x // SUB], after_ref[x // SUB]
-        shift = (x % SUB) * SLOT
-        rim[0, e] = jnp.where(
-            lane % SPAN < REACH,
-            turn(after, -shift),
-            jnp.where(lane % SPAN >= SPAN - REACH, turn(before, -shift - REACH), zero),
-        )
-        if e < DEPTH:
-            field[0, e] = lo_ref[e * nright : (e + 1) * nright, :]
-        elif e >= DEPTH + rows_x:
-            at = (e - DEPTH - rows_x) * nright
-            field[0, e] = hi_ref[at : at + nright, :]
-        else:
-            field[0, e] = own_ref[x]
-
-    for g in range(xtiles + 2):
+    for g in groups:
         xt = (g - 1) % xtiles
-        if g == 0:
-            before, after = clo_ref[1], clo_ref[3]
-        elif g == xtiles + 1:
-            before, after = chi_ref[1], chi_ref[3]
-        else:
-            before, after = before_ref[xtiles], after_ref[xtiles]
+        before, after = strips_of(g)
         whole = []
         for c in range(COUPLINGS):
-            at = DEPTH * nright + c * SUB
-            if g == 0:
-                blocks = [lo_ref[at : at + SUB, lanes_of(i)] for i in range(inner)]
-            elif g == xtiles + 1:
-                blocks = [hi_ref[at : at + SUB, lanes_of(i)] for i in range(inner)]
-            else:
-                blocks = [coup_ref[c, xt * SUB : (xt + 1) * SUB, lanes_of(i)] for i in range(inner)]
+            blocks = blocks_of(g, c, xt)
             shift = (c * xtiles + xt) * SLOT
             blocks.append(
                 jnp.where(
@@ -218,12 +178,32 @@
                 for c in range(COUPLINGS):
                     for i in range(inner + 1):
                         wide = jnp.broadcast_to(whole[c][i][s : s + 1], (SUB, LANES))
-                        coup[e, c, :, lanes_of(i)] = wide
+                        coup[e, c, :, i * LANES : (i + 1) * LANES] = wide
                         if c == 0 and i < inner:
                             shown = (wide > 0.0).astype(jnp.float32)
-                            open_bond[e, :, lanes_of(i)] = jnp.concatenate([shown, shown], axis=0).astype(jnp.bfloat16)
-
-    acc[...] = jnp.zeros_like(acc)
+                            open_bond[e, :, i * LANES : (i + 1) * LANES] = jnp.concatenate(
+                                [shown, shown], axis=0
+                            ).astype(jnp.bfloat16)
+
+
+def rim_row(before, after, x):
+    lane = lane_iota()
+    shift = (x % SUB) * SLOT
+    return jnp.where(
+        lane % SPAN < REACH,
+        turn(after, -shift),
+        jnp.where(lane % SPAN >= SPAN - REACH, turn(before, -shift - REACH), jnp.zeros((SUB, LANES), jnp.float32)),
+    )
+
+
+def stepper(field, rim, coup, open_bond, acc, left_ref):
+    nright, width = field.shape[2:]
+    rtiles, inner = nright // SUB, width // LANES
+    rows_x = left_ref.shape[0]
+    lane = lane_iota()
+
+    def lanes_of(i):
+        return slice(i * LANES, (i + 1) * LANES)
 
     def load(k, row, t, i):
         if i == inner:
@@ -299,14 +279,41 @@
             preferred_element_type=jnp.float32,
         )
 
+    return advance, contract
+
+
+def interior_kernel(own_ref, coup_ref, before_ref, after_ref, left_ref, acc, edge_field, edge_rim, field, rim, coup, open_bond):
+    rows_x, nright, width = own_ref.shape
+    rows = rows_x + 2 * DEPTH
+    inner, xtiles = width // LANES, rows_x // SUB
+    for x in range(rows_x):
+        rim[0, x + DEPTH] = rim_row(before_ref[x // SUB], after_ref[x // SUB], x)
+        field[0, x + DEPTH] = own_ref[x]
+
+    def blocks_of(g, c, xt):
+        return [coup_ref[c, xt * SUB : (xt + 1) * SUB, i * LANES : (i + 1) * LANES] for i in range(inner)]
+
+    def strips_of(g):
+        return before_ref[xtiles], after_ref[xtiles]
+
+    coupling_rows(blocks_of, strips_of, range(1, xtiles + 1), xtiles, inner, coup, open_bond, rows)
+    acc[...] = jnp.zeros_like(acc)
+    advance, contract = stepper(field, rim, coup, open_bond, acc, left_ref)
+
+    first, last = DEPTH + 1, DEPTH + rows_x - 2
     lag = 2 * MOMENTS - 1
-    lead = DEPTH + 1 + lag
-    for front in range(1, lead):
-        if front >= lead - 2:
-            contract(front - lag, below=False)
+
+    def front_step(front):
+        if first + MOMENTS - 1 <= front - lag <= last - MOMENTS + 1:
+            contract(front - lag)
         for k in reversed(range(MOMENTS)):
-            if front >= 3 * k + 1:
+            if first + 3 * k <= front <= last + k:
                 advance(k, front - 2 * k, front % 2 == 1)
+
+    lead = first + MOMENTS - 1 + lag
+    pairs = (last - lead + 1) // 2
+    for front in range(first, lead):
+        front_step(front)
 
     def both(n, _):
         for part in range(2):
@@ -316,11 +323,69 @@
                 advance(k, front - 2 * k, (lead + part) % 2 == 1)
         return 0
 
-    lax.fori_loop(0, rows_x // 2 - 1, both, 0)
-    end = rows_x + DEPTH
-    advance(MOMENTS - 1, end, end % 2 == 1)
-    contract(end - 1, above=False)
-    contract(end, above=False)
+    lax.fori_loop(0, pairs, both, 0)
+    for front in range(lead + 2 * pairs, last - MOMENTS + 1 + lag + 1):
+        front_step(front)
+    for k in range(MOMENTS - 1):
+        for side, at in enumerate((first, last - MOMENTS + 1)):
+            edge_field[side, k] = field[k + 1, at : at + MOMENTS]
+            edge_rim[side, k] = rim[k + 1, at : at + MOMENTS]
+
+
+def border_kernel(ends_ref, coup_ref, lo_ref, hi_ref, before_ref, after_ref, left_ref, part_ref, edge_field, edge_rim, out_ref, field, rim, coup, open_bond, acc, spaced):
+    nright, width = ends_ref.shape[1:]
+    rows_x = left_ref.shape[0]
+    rows = rows_x + 2 * DEPTH
+    inner, xtiles = width // LANES, rows_x // SUB
+    base = DEPTH * nright + COUPLINGS * SUB
+
+    def corner(ref, which, v):
+        return ref[base + which * SUB : base + (which + 1) * SUB, v * LANES : (v + 1) * LANES]
+
+    for e in range(DEPTH):
+        rim[0, e] = rim_row(corner(lo_ref, 0, 0), corner(lo_ref, 1, 0), e - DEPTH)
+        field[0, e] = lo_ref[e * nright : (e + 1) * nright, :]
+        rim[0, e + DEPTH + rows_x] = rim_row(corner(hi_ref, 0, 0), corner(hi_ref, 1, 0), e)
+        field[0, e + DEPTH + rows_x] = hi_ref[e * nright : (e + 1) * nright, :]
+    for n, x in enumerate((0, 1, rows_x - 2, rows_x - 1)):
+        rim[0, x + DEPTH] = rim_row(before_ref[x // SUB], after_ref[x // SUB], x)
+        field[0, x + DEPTH] = ends_ref[n]
+
+    def blocks_of(g, c, xt):
+        at = DEPTH * nright + c * SUB
+        lanes = [slice(i * LANES, (i + 1) * LANES) for i in range(inner)]
+        if g == 0:
+            return [lo_ref[at : at + SUB, i] for i in lanes]
+        if g == xtiles + 1:
+            return [hi_ref[at : at + SUB, i] for i in lanes]
+        return [coup_ref[c, xt * SUB : (xt + 1) * SUB, i] for i in lanes]
+
+    def strips_of(g):
+        if g == 0:
+            return corner(lo_ref, 0, 1), corner(lo_ref, 1, 1)
+        if g == xtiles + 1:
+            return corner(hi_ref, 0, 1), corner(hi_ref, 1, 1)
+        return before_ref[xtiles], after_ref[xtiles]
+
+    coupling_rows(blocks_of, strips_of, (0, 1, xtiles, xtiles + 1), xtiles, inner, coup, open_bond, rows)
+    first, last = DEPTH + 1, DEPTH + rows_x - 2
+    for k in range(MOMENTS - 1):
+        for side, at in enumerate((first, last - MOMENTS + 1)):
+            field[k + 1, at : at + MOMENTS] = edge_field[side, k]
+            rim[k + 1, at : at + MOMENTS] = edge_rim[side, k]
+    acc[...] = part_ref[...]
+    advance, contract = stepper(field, rim, coup, open_bond, acc, left_ref)
+
+    for front in range(1, DEPTH + 3 * (MOMENTS - 1) + 1):
+        for k in reversed(range(MOMENTS)):
+            if 3 * k + 1 <= front <= 3 * k + DEPTH:
+                row = front - 2 * k
+                advance(k, row, row % 2 == 1)
+                advance(k, rows - 1 - row, (rows - 1 - row) % 2 == 1)
+    for n in range(DEPTH):
+        for row in (DEPTH - 1 + n, rows - DEPTH - n):
+            contract(row, 0 <= row - 1 - DEPTH < rows_x, 0 <= row + 1 - DEPTH < rows_x)
+
     groups, _, flat = out_ref.shape
     owned = flat // nright
     both_sides = acc[...].T
@@ -341,26 +406,29 @@
             out_ref[j, q : q + 1, :] = row[:, q * nright : (q + 1) * nright]
 
 
-def moments_of_tile(own, coup, lo, hi, before, after, clo, chi, left, groups):
-    rows_x, nright, width = own.shape
-    rows = rows_x + 2 * DEPTH + MOMENTS
-    nleft = left.shape[1]
+def vmem_call(kernel, name, out_shape, scratch, flops, *args):
+    several = isinstance(out_shape, tuple)
+    spec = pl.BlockSpec(memory_space=pltpu.VMEM)
     return pl.pallas_call(
-        main_kernel,
-        out_shape=jax.ShapeDtypeStruct((groups, MOMENTS, nleft // groups * nright), jnp.float32),
-        in_specs=[pl.BlockSpec(memory_space=pltpu.VMEM)] * 9,
-        out_specs=pl.BlockSpec(memory_space=pltpu.VMEM),
-        scratch_shapes=[
-            pltpu.VMEM((MOMENTS + 1, rows, nright, width), jnp.float32),
-            pltpu.VMEM((MOMENTS + 1, rows, SUB, LANES), jnp.float32),
-            pltpu.VMEM((rows, COUPLINGS, SUB, width + LANES), jnp.float32),
-            pltpu.VMEM((rows, 2 * SUB, width), jnp.bfloat16),
-            pltpu.VMEM((MOMENTS * nright, 2 * nleft), jnp.float32),
-            pltpu.VMEM((nleft, LANES), jnp.float32),
-        ],
+        kernel,
+        out_shape=out_shape,
+        in_specs=[spec] * len(args),
+        out_specs=(spec,) * len(out_shape) if several else spec,
+        scratch_shapes=scratch,
         compiler_params=pltpu.CompilerParams(vmem_limit_bytes=28 << 20),
-        name="chebyshev_moments",
-    )(own, coup, lo, hi, before, after, clo, chi, left)
+        cost_estimate=pl.CostEstimate(flops=flops, bytes_accessed=1 << 22, transcendentals=0),
+        name=name,
+    )(*args)
+
+
+def scratch_of(rows_x, nright, width):
+    rows = rows_x + 2 * DEPTH
+    return [
+        pltpu.VMEM((MOMENTS + 1, rows, nright, width), jnp.float32),
+        pltpu.VMEM((MOMENTS + 1, rows, SUB, LANES), jnp.float32),
+        pltpu.VMEM((rows, COUPLINGS, SUB, width + LANES), jnp.float32),
+        pltpu.VMEM((rows, 2 * SUB, width), jnp.bfloat16),
+    ]
 
 
 def ring(axis, by):
@@ -379,15 +447,36 @@
         before = lax.ppermute(last, "sy", ring("sy", 1))
         after = lax.ppermute(first, "sy", ring("sy", -1))
     with jax.named_scope("halo_x"):
-        lo = lax.ppermute(bottom, "sx", ring("sx", 1))
-        hi = lax.ppermute(top, "sx", ring("sx", -1))
-    with jax.named_scope("halo_corner"):
-        up = jnp.concatenate([before[-2:], after[-2:]], axis=0)
-        down = jnp.concatenate([before[:1], before[-1:], after[:1], after[-1:]], axis=0)
-        clo = lax.ppermute(up, "sx", ring("sx", 1))
-        chi = lax.ppermute(down, "sx", ring("sx", -1))
+        def with_corners(rows, v):
+            corners = [jnp.concatenate([part[v], part[-1]], axis=1) for part in (before, after)]
+            return jnp.concatenate([rows] + corners, axis=0)
+
+        lo = lax.ppermute(with_corners(bottom, -2), "sx", ring("sx", 1))
+        hi = lax.ppermute(with_corners(top, 0), "sx", ring("sx", -1))
     left = left_vectors.transpose(1, 0, 2)
-    tile = moments_of_tile(own, coup, lo, hi, before, after, clo, chi, left, nsy)
+    f32 = jnp.float32
+    part, edge_field, edge_rim = vmem_call(
+        interior_kernel,
+        "interior",
+        (
+            jax.ShapeDtypeStruct((MOMENTS * nright, 2 * nleft), f32),
+            jax.ShapeDtypeStruct((2, MOMENTS - 1, MOMENTS, nright, rows_y), f32),
+            jax.ShapeDtypeStruct((2, MOMENTS - 1, MOMENTS, SUB, LANES), f32),
+        ),
+        scratch_of(rows_x, nright, rows_y),
+        1 << 33,
+        own, coup, before, after, left,
+    )
+    ends = jnp.concatenate([own[:2], own[-2:]], axis=0)
+    tile = vmem_call(
+        border_kernel,
+        "border",
+        jax.ShapeDtypeStruct((nsy, MOMENTS, owned * nright), f32),
+        scratch_of(rows_x, nright, rows_y)
+        + [pltpu.VMEM((MOMENTS * nright, 2 * nleft), f32), pltpu.VMEM((nleft, LANES), f32)],
+        1 << 32,
+        ends, coup, lo, hi, before, after, left, part, edge_field, edge_rim,
+    )
     with jax.named_scope("reduce_sy"):
         mine = jnp.sum(lax.all_to_all(tile, "sy", 0, 0), axis=0)
     with jax.named_scope("reduce_sx"):

time: 85.3 us -> 79.6 us (0.933)
  starting transfers between devices: 27.5 us -> 24.1 us
  waiting for transfers between devices: 4.65 us -> 2.17 us
  blocking collectives: 34.9 us -> 37.3 us
  Pallas kernels: 15.1 us -> 13.9 us
  local copies, waits for them, and re-layouts: 2.54 us -> 1.56 us
    ppermute x4 -> x2, starting transfers between devices: 16.8 us -> 13.4 us  [the longest x1 11.5 us: shards(): hi = lax.ppermute(with_corners(top, 0), 'sx', ring('sx', -1))]
    ppermute x4 -> x2, waiting for transfers between devices: 4.65 us -> 2.16 us  [the longest x1 2.16 us: shards(): lo = lax.ppermute(with_corners(bottom, -2), 'sx', ring('sx', 1))]
    all_to_all x1, blocking collectives: 12.3 us -> 14.1 us  [shards(): lax.all_to_all(jnp.broadcast_to(mine[None], (nsx,) + mine.shape), 'sx', 0...]
    pallas_call x1 -> x2, Pallas kernels: 11.1 us -> 9.87 us  [vmem_call(): pl.pallas_call(kernel, out_shape=out_shape, in_specs=[spec] * len(args),...]
    unnamed x11 -> x13, local copies, waits for them, and re-layouts: 1.83 us -> 0.61 us
  transfers between devices with their start and end apart: 6 -> 4, of which waited for: 1 -> 1; matrix products, arithmetic and copies ran while one was open for 2% -> 2% of each run, Pallas kernels for 0% -> 8%
where the time goes in v4:
time: 79.6 us; the launch traced here: 79.3 us
  blocking collectives  37.3 us (47%)
  starting transfers between devices  24.1 us (30%)
  Pallas kernels  13.9 us (17%)
  waiting for transfers between devices  2.17 us (3%)
  local copies, waits for them, and re-layouts  1.56 us (2%)
    all_to_all x1, blocking collectives, shards(): mine = jnp.sum(lax.all_to_all(tile, 'sy', 0, 0), axis=0)  23.2 us
    all_to_all x1, blocking collectives, shards(): lax.all_to_all(jnp.broadcast_to(mine[None], (nsx,) + mine.shape), 'sx', 0...  14.1 us
    ppermute x1, starting transfers between devices, shards(): hi = lax.ppermute(with_corners(top, 0), 'sx', ring('sx', -1))  11.5 us
    pallas_call x2, Pallas kernels, vmem_call(): pl.pallas_call(kernel, out_shape=out_shape, in_specs=[spec] * len(args),...  9.87 us
    ppermute x1, starting transfers between devices, shards(): after = lax.ppermute(first, 'sy', ring('sy', -1))  6.2 us
    ppermute x1, starting transfers between devices, shards(): before = lax.ppermute(last, 'sy', ring('sy', 1))  4.51 us
    pallas_call x1, Pallas kernels, prepare(): pl.pallas_call(prepare_kernel, out_shape=(jax.ShapeDtypeStruct((rows, nri...  2.76 us
    ppermute x1, waiting for transfers between devices, shards(): lo = lax.ppermute(with_corners(bottom, -2), 'sx', ring('sx', 1))  2.16 us
  transfers between devices with their start and end apart: 4, of which 1 were waited for; matrix products, arithmetic and copies ran while one was open for 2% of the time, Pallas kernels for 8%

profile of v4, /device:TPU:1, one launch (start us, length us, event | category | flops | bytes accessed | tf_op | source)
XLA Modules:
  0.0 79.3 jit_solution(693849280968969213)
XLA Ops:
  0.0 0.0 copy-start.3
  0.0 2.8 %prepare.1 = (f32[32,32,256]{2,1,0:T(8,128)}, f32[3,32,256]{2,1,0:T(8,128)}, f32[216,256]{1,0:T(8,128)}, f32[216,256]{1,0:T(8,128)}, f32[5,8,128]{2,1,0:T(8,128)}, /*index=5*/f32[5,8,128]{2,1,0:T(8,128)}) custom-call(f32[4]{0:T(128)} %refs_0_.1, bf16[32,32,256]{2,1,0:T(8,128)(2,1)} %refs_1_.1, s32[32,256]{1,0:T(8,128)} %refs_2_.1, s32[2,32,256]{2,1,0:T(8,128)} %refs_3_.1), custom_call_target="tpu_custom_call" | custom-call | tf_op jit(solution)/shard_map/prepare/pallas_call | solution.py:112
  2.8 4.5 %collective-permute-start = (f32[5,8,128]{2,1,0:T(8,128)}, f32[5,8,128]{2,1,0:T(8,128)S(1)}, u32[]{:S(2)}, u32[]{:S(2)}) collective-permute-start(f32[5,8,128]{2,1,0:T(8,128)} %get-tuple-element.17), channel_id=1, source_target_pairs={{0,1},{1,2},{2,3},{3,4},{4,5},{5,6},{6,7},{7,8},{8,9},{9,10},{10,1... | collective-permute-start | bytes 61448 | tf_op jit(solution)/shard_map/halo_y/ppermute | solution.py:447
  7.3 6.2 %collective-permute-start.1 = (f32[5,8,128]{2,1,0:T(8,128)}, f32[5,8,128]{2,1,0:T(8,128)S(1)}, u32[]{:S(2)}, u32[]{:S(2)}) collective-permute-start(f32[5,8,128]{2,1,0:T(8,128)} %get-tuple-element.18), channel_id=1, source_target_pairs={{0,15},{1,0},{2,1},{3,2},{4,3},{5,4},{6,5},{7,6},{8,7},{9,8},{10,9... | collective-permute-start | bytes 61448 | tf_op jit(solution)/shard_map/halo_y/ppermute | solution.py:448
  13.5 0.0 copy-start.4
  13.5 0.0 copy-start.5
  13.5 0.9 %fusion.4 = (f32[2,32,256]{2,1,0:T(8,128)S(1)}, f32[2,32,256]{2,1,0:T(8,128)S(1)}) fusion(f32[32,32,256]{2,1,0:T(8,128)} %get-tuple-element.14.own_ref), kind=kLoop, calls=%fused_computation.16 | loop fusion | bytes 262144 | tf_op jit(solution)/shard_map/slice | solution.py:470
  14.5 0.0 copy-done.3
  14.5 0.0 copy-start
  14.5 0.0 copy-start.2
  14.5 0.6 copy.9
  15.1 0.0 collective-permute-done.before_ref
  15.1 0.0 collective-permute-done.1.after_ref
  15.1 0.0 copy-done.4
  15.1 0.0 copy-done.5
  15.2 11.5 %collective-permute-start.3 = (f32[232,256]{1,0:T(8,128)S(1)}, f32[232,256]{1,0:T(8,128)S(1)}, u32[]{:S(2)}, u32[]{:S(2)}) collective-permute-start(f32[232,256]{1,0:T(8,128)S(1)} %get-tuple-element.31), channel_id=1, source_target_pairs={{0,496},{16,0},{32,16},{48,32},{64,48},{80,64},{96,80},{112,96},{1... | collective-permute-start | bytes 712712 | tf_op jit(solution)/shard_map/halo_x/ppermute | solution.py:455
  26.7 1.9 %collective-permute-start.2 = (f32[232,256]{1,0:T(8,128)S(1)}, f32[232,256]{1,0:T(8,128)S(1)}, u32[]{:S(2)}, u32[]{:S(2)}) collective-permute-start(f32[232,256]{1,0:T(8,128)S(1)} %get-tuple-element.32), channel_id=1, source_target_pairs={{0,16},{16,32},{32,48},{48,64},{64,80},{80,96},{96,112},{112,128},... | collective-permute-start | bytes 712712 | tf_op jit(solution)/shard_map/halo_x/ppermute | solution.py:454
  28.6 0.0 copy-done
  28.6 0.0 copy-done.2
  28.6 6.6 %interior.1 = (f32[160,128]{1,0:T(8,128)S(1)}, f32[2,4,5,32,256]{4,3,2,1,0:T(8,128)S(1)}, f32[2,4,5,8,128]{4,3,2,1,0:T(8,128)S(1)}) custom-call(f32[32,32,256]{2,1,0:T(8,128)S(1)} %copy-done, f32[3,32,256]{2,1,0:T(8,128)S(1)} %copy-done.2, f32[5,8,128]{2,1,0:T(8,128)S(1)} %collective-permute-done.before_ref, ...), custom_call_target="tpu_custom_call" | custom-call | flops 8589934592 | bytes 4194304 | tf_op jit(solution)/shard_map/interior/pallas_call | solution.py:412
  35.3 0.0 collective-permute-done.3.hi_ref
  35.3 2.2 %collective-permute-done.2.lo_ref = f32[232,256]{1,0:T(8,128)S(1)} collective-permute-done((f32[232,256]{1,0:T(8,128)S(1)}, f32[232,256]{1,0:T(8,128)S(1)}, u32[]{:S(2)}, u32[]{:S(2)}) %collective-permute-start.2) | collective-permute-done | bytes 237600 | tf_op jit(solution)/shard_map/halo_x/ppermute | solution.py:454
  37.4 0.0 copy-start.1
  37.4 3.2 %border.1 = f32[16,5,128]{2,1,0:T(8,128)S(1)} custom-call(f32[4,32,256]{2,1,0:T(8,128)S(1)} %pad_maximum_fusion.4.ends_ref, f32[3,32,256]{2,1,0:T(8,128)S(1)} %copy-done.2, f32[232,256]{1,0:T(8,128)S(1)} %collective-permute-done.2.lo_ref, f32[232,256]{1,0:T(8,128)S(1)} %collective-permute-done.3.hi_ref, f32[5,8,128]{2,1,0:T(8,128)S(1)} %collective-permute-done.before_ref, ...), custom_call_target="tpu_custom_call" | custom-call | flops 4294967296 | bytes 4194304 | tf_op jit(solution)/shard_map/border/pallas_call | solution.py:412
  40.7 23.2 %all_to_all.10 = f32[16,5,128]{2,1,0:T(8,128)S(1)} all-to-all(f32[16,5,128]{2,1,0:T(8,128)S(1)} %border.1), channel_id=1, replica_groups=mesh['sx'=32,'sy'=16] {'sy'}, dimensions={0} | all-to-all | bytes 81920 | tf_op jit(solution)/shard_map/reduce_sy/all_to_all | solution.py:481
  63.9 14.1 %all_to_all.11.blocks_ref = f32[32,5,128]{2,1,0:T(8,128)S(1)} all-to-all(f32[32,5,128]{2,1,0:T(8,128)S(1)} %broadcast_in_dim.2), channel_id=1, replica_groups=mesh['sx'=32,'sy'=16] {'sx'}, dimensions={0} | all-to-all | bytes 163840 | tf_op jit(solution)/shard_map/reduce_sx/all_to_all | solution.py:483
  78.0 0.0 copy-done.1
  78.0 1.3 %finish.1 = f32[5,4,32]{2,1,0:T(4,128)} custom-call(s32[5]{0:T(128)S(1)} %copy-done.1, f32[32,5,128]{2,1,0:T(8,128)S(1)} %all_to_all.11.blocks_ref), custom_call_target="tpu_custom_call" | custom-call | tf_op jit(solution)/shard_map/finish/pallas_call | solution.py:485
  (6 shorter events, 0.1 us)
Async XLA Ops:
  0.0 14.5 %copy-start.3 = (bf16[64,32,256]{2,1,0:T(8,128)(2,1)S(1)}, bf16[64,32,256]{2,1,0:T(8,128)(2,1)}, u32[]{:S(2)}) copy-start(bf16[64,32,256]{2,1,0:T(8,128)(2,1)} %param.7) | copy-start | bytes 3145732
  2.8 12.3 %collective-permute-start = (f32[5,8,128]{2,1,0:T(8,128)}, f32[5,8,128]{2,1,0:T(8,128)S(1)}, u32[]{:S(2)}, u32[]{:S(2)}) collective-permute-start(f32[5,8,128]{2,1,0:T(8,128)} %get-tuple-element.17), channel_id=1, source_target_pairs={{0,1},{1,2},{2,3},{3,4},{4,5},{5,6},{6,7},{7,8},{8,9},{9,10},{10,1... | collective-permute-start | bytes 61448 | tf_op jit(solution)/shard_map/halo_y/ppermute | solution.py:447
  7.3 7.8 %collective-permute-start.1 = (f32[5,8,128]{2,1,0:T(8,128)}, f32[5,8,128]{2,1,0:T(8,128)S(1)}, u32[]{:S(2)}, u32[]{:S(2)}) collective-permute-start(f32[5,8,128]{2,1,0:T(8,128)} %get-tuple-element.18), channel_id=1, source_target_pairs={{0,15},{1,0},{2,1},{3,2},{4,3},{5,4},{6,5},{7,6},{8,7},{9,8},{10,9... | collective-permute-start | bytes 61448 | tf_op jit(solution)/shard_map/halo_y/ppermute | solution.py:448
  13.5 1.6 %copy-start.4 = (f32[216,256]{1,0:T(8,128)S(1)}, f32[216,256]{1,0:T(8,128)}, u32[]{:S(2)}) copy-start(f32[216,256]{1,0:T(8,128)} %get-tuple-element.19) | copy-start | bytes 663556
  13.5 1.6 %copy-start.5 = (f32[216,256]{1,0:T(8,128)S(1)}, f32[216,256]{1,0:T(8,128)}, u32[]{:S(2)}) copy-start(f32[216,256]{1,0:T(8,128)} %get-tuple-element.16) | copy-start | bytes 663556
  14.5 14.1 %copy-start = (f32[32,32,256]{2,1,0:T(8,128)S(1)}, f32[32,32,256]{2,1,0:T(8,128)}, u32[]{:S(2)}) copy-start(f32[32,32,256]{2,1,0:T(8,128)} %get-tuple-element.14.own_ref) | copy-start | bytes 3145732
  14.5 14.1 %copy-start.2 = (f32[3,32,256]{2,1,0:T(8,128)S(1)}, f32[3,32,256]{2,1,0:T(8,128)}, u32[]{:S(2)}) copy-start(f32[3,32,256]{2,1,0:T(8,128)} %get-tuple-element.15.coup_ref) | copy-start | bytes 294916
  15.2 20.1 %collective-permute-start.3 = (f32[232,256]{1,0:T(8,128)S(1)}, f32[232,256]{1,0:T(8,128)S(1)}, u32[]{:S(2)}, u32[]{:S(2)}) collective-permute-start(f32[232,256]{1,0:T(8,128)S(1)} %get-tuple-element.31), channel_id=1, source_target_pairs={{0,496},{16,0},{32,16},{48,32},{64,48},{80,64},{96,80},{112,96},{1... | collective-permute-start | bytes 712712 | tf_op jit(solution)/shard_map/halo_x/ppermute | solution.py:455
  26.7 10.8 %collective-permute-start.2 = (f32[232,256]{1,0:T(8,128)S(1)}, f32[232,256]{1,0:T(8,128)S(1)}, u32[]{:S(2)}, u32[]{:S(2)}) collective-permute-start(f32[232,256]{1,0:T(8,128)S(1)} %get-tuple-element.32), channel_id=1, source_target_pairs={{0,16},{16,32},{32,48},{48,64},{64,80},{80,96},{96,112},{112,128},... | collective-permute-start | bytes 712712 | tf_op jit(solution)/shard_map/halo_x/ppermute | solution.py:454
  37.4 40.6 %copy-start.1 = (s32[5]{0:T(128)S(1)}, s32[5]{0:T(128)}, u32[]{:S(2)}) copy-start(s32[5]{0:T(128)} %order_ref.1) | copy-start | bytes 64

commit v5 on v4

--- a/solution.py
+++ b/solution.py
@@ -41,14 +41,15 @@
 
 
 def prepare_kernel(*refs):
-    sources, outputs, held, sems = refs[:4], refs[4:10], refs[10:14], refs[14]
+    sources, outputs, held, sems = refs[:4], refs[4:8], refs[8:12], refs[12]
     copies = [pltpu.make_async_copy(a, b, sems.at[n]) for n, (a, b) in enumerate(zip(sources, held))]
     for copy in copies:
         copy.start()
     for copy in copies:
         copy.wait()
     energy_ref, right_ref, class_ref, bond_ref = held
-    own_ref, coup_ref, top_ref, bottom_ref, first_ref, last_ref = outputs
+    own_ref, coup_ref, rows_ref, strips_ref = outputs
+    top_at, first_at = lax.axis_index("sx") % 2, lax.axis_index("sy") % 2
     nright, rows, width = right_ref.shape
     lane = lane_iota()
     sub = lax.broadcasted_iota(jnp.int32, (SUB, LANES), 0)
@@ -78,10 +79,10 @@
                         x = xt * SUB + j
                         own_ref[x, t * SUB : (t + 1) * SUB, lanes] = turned[j]
                         if x < DEPTH:
-                            top_ref[x * nright + t * SUB : x * nright + (t + 1) * SUB, lanes] = turned[j]
+                            rows_ref[top_at, x * nright + t * SUB : x * nright + (t + 1) * SUB, lanes] = turned[j]
                         if x >= rows - DEPTH:
                             at = (x - rows + DEPTH) * nright + t * SUB
-                            bottom_ref[at : at + SUB, lanes] = turned[j]
+                            rows_ref[1 - top_at, at : at + SUB, lanes] = turned[j]
                         strip(xt, t * SPAN + j * SLOT, i, turned[j])
     for xt in range(xtiles):
         here = slice(xt * SUB, (xt + 1) * SUB)
@@ -97,30 +98,28 @@
                 strip(xtiles, (c * xtiles + xt) * SLOT, i, fields[c])
                 at = DEPTH * nright + c * SUB
                 if xt == 0:
-                    top_ref[at : at + SUB, lanes] = fields[c]
+                    rows_ref[top_at, at : at + SUB, lanes] = fields[c]
                 if xt == xtiles - 1:
-                    bottom_ref[at : at + SUB, lanes] = fields[c]
+                    rows_ref[1 - top_at, at : at + SUB, lanes] = fields[c]
     for v in range(xtiles + 1):
-        first_ref[v] = first[v]
-        last_ref[v] = last[v]
+        strips_ref[first_at, v] = first[v]
+        strips_ref[1 - first_at, v] = last[v]
 
 
 def prepare(right, classes, energy, bonds):
     nright, rows, width = right.shape
-    rim = jax.ShapeDtypeStruct((DEPTH * nright + COUPLINGS * SUB, width), jnp.float32)
-    strip = jax.ShapeDtypeStruct((rows // SUB + 1, SUB, LANES), jnp.float32)
+    rim = jax.ShapeDtypeStruct((2, DEPTH * nright + COUPLINGS * SUB, width), jnp.float32)
+    strip = jax.ShapeDtypeStruct((2, rows // SUB + 1, SUB, LANES), jnp.float32)
     return pl.pallas_call(
         prepare_kernel,
         out_shape=(
             jax.ShapeDtypeStruct((rows, nright, width), jnp.float32),
             jax.ShapeDtypeStruct((COUPLINGS, rows, width), jnp.float32),
             rim,
-            rim,
-            strip,
             strip,
         ),
         in_specs=[pl.BlockSpec(memory_space=pltpu.HBM)] * 4,
-        out_specs=(pl.BlockSpec(memory_space=pltpu.VMEM),) * 6,
+        out_specs=(pl.BlockSpec(memory_space=pltpu.VMEM),) * 4,
         scratch_shapes=[
             pltpu.SMEM(energy.shape, energy.dtype),
             pltpu.VMEM(right.shape, right.dtype),
@@ -282,7 +281,7 @@
     return advance, contract
 
 
-def interior_kernel(own_ref, coup_ref, before_ref, after_ref, left_ref, acc, edge_field, edge_rim, field, rim, coup, open_bond):
+def interior_kernel(own_ref, coup_ref, before_ref, after_ref, left_ref, acc, edge_field, edge_rim, ends_ref, field, rim, coup, open_bond):
     rows_x, nright, width = own_ref.shape
     rows = rows_x + 2 * DEPTH
     inner, xtiles = width // LANES, rows_x // SUB
@@ -330,14 +329,26 @@
         for side, at in enumerate((first, last - MOMENTS + 1)):
             edge_field[side, k] = field[k + 1, at : at + MOMENTS]
             edge_rim[side, k] = rim[k + 1, at : at + MOMENTS]
-
-
-def border_kernel(ends_ref, coup_ref, lo_ref, hi_ref, before_ref, after_ref, left_ref, part_ref, edge_field, edge_rim, out_ref, field, rim, coup, open_bond, acc, spaced):
+    for n, x in enumerate((0, 1, rows_x - 2, rows_x - 1)):
+        ends_ref[n] = own_ref[x]
+
+
+class Either:
+    def __init__(self, flag, one, other):
+        self.flag, self.one, self.other = flag, one, other
+
+    def __getitem__(self, at):
+        return jnp.where(self.flag, self.one[at], self.other[at])
+
+
+def border_kernel(scale, order_ref, ends_ref, coup_ref, near_ref, next_ref, before_ref, after_ref, left_ref, part_ref, edge_field, edge_rim, out_ref, field, rim, coup, open_bond, acc, spaced, ranked):
     nright, width = ends_ref.shape[1:]
     rows_x = left_ref.shape[0]
     rows = rows_x + 2 * DEPTH
     inner, xtiles = width // LANES, rows_x // SUB
     base = DEPTH * nright + COUPLINGS * SUB
+    even = lax.axis_index("sx") % 2 == 0
+    lo_ref, hi_ref = Either(even, near_ref, next_ref), Either(even, next_ref, near_ref)
 
     def corner(ref, which, v):
         return ref[base + which * SUB : base + (which + 1) * SUB, v * LANES : (v + 1) * LANES]
@@ -390,35 +401,28 @@
     owned = flat // nright
     both_sides = acc[...].T
     half = both_sides.shape[0] // 2
-    total = both_sides[:half] - both_sides[half:]
+    total = (both_sides[:half] - both_sides[half:]) * scale
     for k in range(MOMENTS):
         spaced[:, 0:nright] = total[:, k * nright : (k + 1) * nright]
         rows_of = [spaced[pl.ds(q, groups, stride=owned), :] for q in range(owned)]
-        out_ref[:, k, :] = jnp.concatenate([r[:, 0:nright] for r in rows_of], axis=1)
-
-
-def finish_kernel(scale, order_ref, blocks_ref, out_ref, total):
-    total[...] = jnp.sum(blocks_ref[...], axis=0) * scale
-    _, owned, nright = out_ref.shape
+        ranked[k] = jnp.concatenate([r[:, 0:nright] for r in rows_of], axis=1)
     for j in range(MOMENTS):
-        row = total[pl.ds(order_ref[j], 1), :]
-        for q in range(owned):
-            out_ref[j, q : q + 1, :] = row[:, q * nright : (q + 1) * nright]
-
-
-def vmem_call(kernel, name, out_shape, scratch, flops, *args):
+        out_ref[:, j, :] = ranked[order_ref[j]]
+
+
+def vmem_call(kernel, name, out_shape, scratch, flops, *args, scalars=()):
     several = isinstance(out_shape, tuple)
     spec = pl.BlockSpec(memory_space=pltpu.VMEM)
     return pl.pallas_call(
         kernel,
         out_shape=out_shape,
-        in_specs=[spec] * len(args),
+        in_specs=[pl.BlockSpec(memory_space=pltpu.SMEM)] * len(scalars) + [spec] * len(args),
         out_specs=(spec,) * len(out_shape) if several else spec,
         scratch_shapes=scratch,
         compiler_params=pltpu.CompilerParams(vmem_limit_bytes=28 << 20),
         cost_estimate=pl.CostEstimate(flops=flops, bytes_accessed=1 << 22, transcendentals=0),
         name=name,
-    )(*args)
+    )(*scalars, *args)
 
 
 def scratch_of(rows_x, nright, width):
@@ -431,9 +435,10 @@
     ]
 
 
-def ring(axis, by):
+def pairs(axis, start):
     size = lax.axis_size(axis)
-    return [(i, (i + by) % size) for i in range(size)]
+    swaps = [(i % size, (i + 1) % size) for i in range(start, size + start, 2)]
+    return swaps + [(b, a) for a, b in swaps]
 
 
 def shards(right_vectors, left_vectors, classes, class_energy, bond_mask_grid, order):
@@ -441,56 +446,58 @@
     nright, nleft = right_vectors.shape[0], left_vectors.shape[0]
     nsx, nsy = lax.axis_size("sx"), lax.axis_size("sy")
     owned = nleft // nsy
-
-    own, coup, top, bottom, first, last = prepare(right_vectors, classes, class_energy, bond_mask_grid)
+    even_x, even_y = lax.axis_index("sx") % 2 == 0, lax.axis_index("sy") % 2 == 0
+
+    own, coup, rows, strips = prepare(right_vectors, classes, class_energy, bond_mask_grid)
     with jax.named_scope("halo_y"):
-        before = lax.ppermute(last, "sy", ring("sy", 1))
-        after = lax.ppermute(first, "sy", ring("sy", -1))
+        near = lax.ppermute(strips[0], "sy", pairs("sy", -1))
+        across = lax.ppermute(strips[1], "sy", pairs("sy", 0))
+    before, after = jnp.where(even_y, near, across), jnp.where(even_y, across, near)
     with jax.named_scope("halo_x"):
-        def with_corners(rows, v):
-            corners = [jnp.concatenate([part[v], part[-1]], axis=1) for part in (before, after)]
-            return jnp.concatenate([rows] + corners, axis=0)
-
-        lo = lax.ppermute(with_corners(bottom, -2), "sx", ring("sx", 1))
-        hi = lax.ppermute(with_corners(top, 0), "sx", ring("sx", -1))
+        def with_corners(slot):
+            upper = even_x == (slot == 0)
+            corners = [
+                jnp.concatenate([jnp.where(upper, part[0], part[-2]), part[-1]], axis=1) for part in (before, after)
+            ]
+            return jnp.concatenate([rows[slot]] + corners, axis=0)
+
+        near_rows = lax.ppermute(with_corners(0), "sx", pairs("sx", -1))
+        next_rows = lax.ppermute(with_corners(1), "sx", pairs("sx", 0))
     left = left_vectors.transpose(1, 0, 2)
     f32 = jnp.float32
-    part, edge_field, edge_rim = vmem_call(
+    part, edge_field, edge_rim, ends = vmem_call(
         interior_kernel,
         "interior",
         (
             jax.ShapeDtypeStruct((MOMENTS * nright, 2 * nleft), f32),
             jax.ShapeDtypeStruct((2, MOMENTS - 1, MOMENTS, nright, rows_y), f32),
             jax.ShapeDtypeStruct((2, MOMENTS - 1, MOMENTS, SUB, LANES), f32),
+            jax.ShapeDtypeStruct((4, nright, rows_y), f32),
         ),
         scratch_of(rows_x, nright, rows_y),
         1 << 33,
         own, coup, before, after, left,
     )
-    ends = jnp.concatenate([own[:2], own[-2:]], axis=0)
+    sites = rows_x * rows_y * nsx * nsy
     tile = vmem_call(
-        border_kernel,
+        functools.partial(border_kernel, -HALF_ROOT / sites**0.5),
         "border",
         jax.ShapeDtypeStruct((nsy, MOMENTS, owned * nright), f32),
         scratch_of(rows_x, nright, rows_y)
-        + [pltpu.VMEM((MOMENTS * nright, 2 * nleft), f32), pltpu.VMEM((nleft, LANES), f32)],
+        + [
+            pltpu.VMEM((MOMENTS * nright, 2 * nleft), f32),
+            pltpu.VMEM((nleft, LANES), f32),
+            pltpu.VMEM((MOMENTS, nsy, owned * nright), f32),
+        ],
         1 << 32,
-        ends, coup, lo, hi, before, after, left, part, edge_field, edge_rim,
+        ends, coup, near_rows, next_rows, before, after, left, part, edge_field, edge_rim,
+        scalars=(order,),
     )
     with jax.named_scope("reduce_sy"):
         mine = jnp.sum(lax.all_to_all(tile, "sy", 0, 0), axis=0)
     with jax.named_scope("reduce_sx"):
         shares = lax.all_to_all(jnp.broadcast_to(mine[None], (nsx,) + mine.shape), "sx", 0, 0)
-    sites = rows_x * rows_y * nsx * nsy
-    return pl.pallas_call(
-        functools.partial(finish_kernel, -HALF_ROOT / sites**0.5),
-        out_shape=jax.ShapeDtypeStruct((MOMENTS, owned, nright), jnp.float32),
-        in_specs=[pl.BlockSpec(memory_space=pltpu.SMEM), pl.BlockSpec(memory_space=pltpu.VMEM)],
-        out_specs=pl.BlockSpec(memory_space=pltpu.VMEM),
-        scratch_shapes=[pltpu.VMEM(mine.shape, jnp.float32)],
-        compiler_params=pltpu.CompilerParams(vmem_limit_bytes=4 << 20),
-        name="finish",
-    )(order, shares)
+    return jnp.sum(shares, axis=0).reshape(MOMENTS, owned, nright)
 
 
 def solution(mesh):

time: 79.6 us -> 76.1 us (0.956)
  starting transfers between devices: 24.1 us -> 21.3 us
  local copies, waits for them, and re-layouts: 1.56 us -> 3.8 us
  blocking collectives: 37.3 us -> 35.6 us
  waiting for transfers between devices: 2.17 us -> 0.81 us
  other arithmetic: 0.08 us -> 1.04 us
  Pallas kernels: 13.9 us -> 13 us
    ppermute x4, starting transfers between devices: 24.1 us -> 21.3 us  [the longest x1 8.77 us: shards(): across = lax.ppermute(strips[1], 'sy', pairs('sy', 0))]
    squeeze x2, local copies, waits for them, and re-layouts: 0.01 us -> 2.51 us  [the longest x1 1.76 us: with_corners(): return jnp.concatenate([rows[slot]] + corners, axis=0)]
    ppermute x4, waiting for transfers between devices: 2.17 us -> 0.81 us  [the longest x1 0.8 us: shards(): near = lax.ppermute(strips[0], 'sy', pairs('sy', -1))]
    all_to_all x1, blocking collectives: 23.2 us -> 21.9 us  [shards(): mine = jnp.sum(lax.all_to_all(tile, 'sy', 0, 0), axis=0)]
    slice x1 -> x0, local copies, waits for them, and re-layouts: 0.93 us -> none  [shards(): ends = jnp.concatenate([own[:2], own[-2:]], axis=0)]
    concatenate x2 -> x1, other arithmetic: 0.06 us -> 0.97 us  [with_corners(): return jnp.concatenate([rows[slot]] + corners, axis=0)]
    pallas_call x3 -> x2, Pallas kernels: 11.1 us -> 10.3 us  [vmem_call(): pl.pallas_call(kernel, out_shape=out_shape, in_specs=[pl.BlockSpec(memory...]
  transfers between devices with their start and end apart: 4 -> 4, of which waited for: 1 -> 1; matrix products, arithmetic and copies ran while one was open for 2% -> 3% of each run, Pallas kernels for 8% -> 9%
where the time goes in v5:
time: 76.1 us; the launch traced here: 75.7 us
  blocking collectives  35.6 us (47%)
  starting transfers between devices  21.3 us (28%)
  Pallas kernels  13 us (17%)
  local copies, waits for them, and re-layouts  3.8 us (5%)
  other arithmetic  1.04 us (1%)
  waiting for transfers between devices  0.81 us (1%)
    all_to_all x1, blocking collectives, shards(): mine = jnp.sum(lax.all_to_all(tile, 'sy', 0, 0), axis=0)  21.9 us
    all_to_all x1, blocking collectives, shards(): lax.all_to_all(jnp.broadcast_to(mine[None], (nsx,) + mine.shape), 'sx', 0...  13.7 us
    pallas_call x2, Pallas kernels, vmem_call(): pl.pallas_call(kernel, out_shape=out_shape, in_specs=[pl.BlockSpec(memory...  10.3 us
    ppermute x1, starting transfers between devices, shards(): across = lax.ppermute(strips[1], 'sy', pairs('sy', 0))  8.77 us
    ppermute x1, starting transfers between devices, shards(): near_rows = lax.ppermute(with_corners(0), 'sx', pairs('sx', -1))  8.66 us
    pallas_call x1, Pallas kernels, prepare(): pl.pallas_call(prepare_kernel, out_shape=(jax.ShapeDtypeStruct((rows, nri...  2.7 us
    ppermute x1, starting transfers between devices, shards(): near = lax.ppermute(strips[0], 'sy', pairs('sy', -1))  1.92 us
    ppermute x1, starting transfers between devices, shards(): next_rows = lax.ppermute(with_corners(1), 'sx', pairs('sx', 0))  1.92 us
  transfers between devices with their start and end apart: 4, of which 1 were waited for; matrix products, arithmetic and copies ran while one was open for 3% of the time, Pallas kernels for 9%

profile of v5, /device:TPU:1, one launch (start us, length us, event | category | flops | bytes accessed | tf_op | source)
XLA Modules:
  0.0 75.7 jit_solution(5213820130125876614)
XLA Ops:
  0.0 0.0 copy-start.3
  0.0 2.7 %prepare.1 = (f32[32,32,256]{2,1,0:T(8,128)}, f32[3,32,256]{2,1,0:T(8,128)}, f32[2,216,256]{2,1,0:T(8,128)}, f32[2,5,8,128]{3,2,1,0:T(8,128)}) custom-call(f32[4]{0:T(128)} %refs_0_.1, bf16[32,32,256]{2,1,0:T(8,128)(2,1)} %refs_1_.1, s32[32,256]{1,0:T(8,128)} %refs_2_.1, s32[2,32,256]{2,1,0:T(8,128)} %refs_3_.1), custom_call_target="tpu_custom_call" | custom-call | tf_op jit(solution)/shard_map/prepare/pallas_call | solution.py:113
  2.7 0.8 slice_bitcast_fusion.2
  3.5 8.8 %collective-permute-start.1 = (f32[5,8,128]{2,1,0:T(8,128)S(1)}, f32[5,8,128]{2,1,0:T(8,128)S(1)}, u32[]{:S(2)}, u32[]{:S(2)}) collective-permute-start(f32[5,8,128]{2,1,0:T(8,128)S(1)} %get-tuple-element.25), channel_id=1, source_target_pairs={{0,1},{2,3},{4,5},{6,7},{8,9},{10,11},{12,13},{14,15},{1,0},{3,2},... | collective-permute-start | bytes 61448 | tf_op jit(solution)/shard_map/halo_y/ppermute | solution.py:454
  12.2 1.9 %collective-permute-start = (f32[5,8,128]{2,1,0:T(8,128)S(1)}, f32[5,8,128]{2,1,0:T(8,128)S(1)}, u32[]{:S(2)}, u32[]{:S(2)}) collective-permute-start(f32[5,8,128]{2,1,0:T(8,128)S(1)} %get-tuple-element.26), channel_id=1, source_target_pairs={{15,0},{1,2},{3,4},{5,6},{7,8},{9,10},{11,12},{13,14},{0,15},{2,1}... | collective-permute-start | bytes 61448 | tf_op jit(solution)/shard_map/halo_y/ppermute | solution.py:453
  14.2 1.8 %slice_bitcast_fusion = (f32[216,256]{1,0:T(8,128)S(1)}, f32[216,256]{1,0:T(8,128)}) fusion(f32[2,216,256]{2,1,0:T(8,128)} %get-tuple-element.17), kind=kLoop, calls=%fused_computation.9 | loop fusion | bytes 884736 | tf_op jit(solution)/shard_map/halo_x/squeeze | solution.py:462
  15.9 0.0 copy-done.3
  15.9 0.0 copy-start
  15.9 0.0 copy-start.1
  15.9 0.6 copy.13
  16.5 0.0 collective-permute-done.1
  16.5 0.8 %collective-permute-done = f32[5,8,128]{2,1,0:T(8,128)S(1)} collective-permute-done((f32[5,8,128]{2,1,0:T(8,128)S(1)}, f32[5,8,128]{2,1,0:T(8,128)S(1)}, u32[]{:S(2)}, u32[]{:S(2)}) %collective-permute-start) | collective-permute-done | bytes 20512 | tf_op jit(solution)/shard_map/halo_y/ppermute | solution.py:453
  17.4 1.0 %fusion.3 = (f32[232,256]{1,0:T(8,128)S(1)}, f32[232,256]{1,0:T(8,128)S(1)}) fusion(f32[8,128]{1,0:T(8,128)S(1)} %get-tuple-element.36, f32[8,128]{1,0:T(8,128)S(1)} %get-tuple-element.31, f32[8,128]{1,0:T(8,128)S(1)} %get-tuple-element.30, f32[8,128]{1,0:T(8,128)S(1)} %get-tuple-element.37, f32[216,256]{1,0:T(8,128)S(1)} %get-tuple-element.21, ...), kind=kLoop, calls=%fused_computation.8 | loop fusion | flops 475136 | bytes 942080 | tf_op jit(solution)/shard_map/halo_x/concatenate | solution.py:462
  18.3 8.7 %collective-permute-start.2 = (f32[232,256]{1,0:T(8,128)S(1)}, f32[232,256]{1,0:T(8,128)S(1)}, u32[]{:S(2)}, u32[]{:S(2)}) collective-permute-start(f32[232,256]{1,0:T(8,128)S(1)} %get-tuple-element.34), channel_id=1, source_target_pairs={{496,0},{16,32},{48,64},{80,96},{112,128},{144,160},{176,192},{208... | collective-permute-start | bytes 712712 | tf_op jit(solution)/shard_map/halo_x/ppermute | solution.py:464
  27.0 1.9 %collective-permute-start.3 = (f32[232,256]{1,0:T(8,128)S(1)}, f32[232,256]{1,0:T(8,128)S(1)}, u32[]{:S(2)}, u32[]{:S(2)}) collective-permute-start(f32[232,256]{1,0:T(8,128)S(1)} %get-tuple-element.33), channel_id=1, source_target_pairs={{0,16},{32,48},{64,80},{96,112},{128,144},{160,176},{192,208},{224... | collective-permute-start | bytes 712712 | tf_op jit(solution)/shard_map/halo_x/ppermute | solution.py:465
  28.9 0.0 copy-done
  28.9 0.0 copy-done.1
  29.0 0.0 copy-start.2
  29.0 6.7 %interior.1 = (f32[160,128]{1,0:T(8,128)S(1)}, f32[2,4,5,32,256]{4,3,2,1,0:T(8,128)S(1)}, f32[2,4,5,8,128]{4,3,2,1,0:T(8,128)S(1)}, f32[4,32,256]{2,1,0:T(8,128)S(1)}) custom-call(f32[32,32,256]{2,1,0:T(8,128)S(1)} %copy-done, f32[3,32,256]{2,1,0:T(8,128)S(1)} %copy-done.1, f32[5,8,128]{2,1,0:T(8,128)S(1)} %get-tuple-element.24.before_ref, ...), custom_call_target="tpu_custom_call" | custom-call | flops 8589934592 | bytes 4194304 | tf_op jit(solution)/shard_map/interior/pallas_call | solution.py:416
  35.6 0.0 collective-permute-done.2.near_ref
  35.6 0.0 collective-permute-done.3.next_ref
  35.6 0.0 copy-done.2
  35.7 3.6 %border.1 = f32[16,5,128]{2,1,0:T(8,128)S(1)} custom-call(s32[5]{0:T(128)S(1)} %copy-done.2, f32[4,32,256]{2,1,0:T(8,128)S(1)} %get-tuple-element.16.ends_ref, f32[3,32,256]{2,1,0:T(8,128)S(1)} %copy-done.1, f32[232,256]{1,0:T(8,128)S(1)} %collective-permute-done.2.near_ref, f32[232,256]{1,0:T(8,128)S(1)} %collective-permute-done.3.next_ref, ...), custom_call_target="tpu_custom_call" | custom-call | flops 4294967296 | bytes 4194304 | tf_op jit(solution)/shard_map/border/pallas_call | solution.py:416
  39.3 21.9 %all_to_all.10 = f32[16,5,128]{2,1,0:T(8,128)S(1)} all-to-all(f32[16,5,128]{2,1,0:T(8,128)S(1)} %border.1), channel_id=1, replica_groups=mesh['sx'=32,'sy'=16] {'sy'}, dimensions={0} | all-to-all | bytes 81920 | tf_op jit(solution)/shard_map/reduce_sy/all_to_all | solution.py:497
  61.3 13.7 %all_to_all.11 = f32[32,5,128]{2,1,0:T(8,128)S(1)} all-to-all(f32[32,5,128]{2,1,0:T(8,128)S(1)} %broadcast_in_dim.2), channel_id=1, replica_groups=mesh['sx'=32,'sy'=16] {'sx'}, dimensions={0} | all-to-all | bytes 163840 | tf_op jit(solution)/shard_map/reduce_sx/all_to_all | solution.py:499
  75.0 0.7 reshape.12
  (5 shorter events, 0.1 us)
Async XLA Ops:
  0.0 15.9 %copy-start.3 = (bf16[64,32,256]{2,1,0:T(8,128)(2,1)S(1)}, bf16[64,32,256]{2,1,0:T(8,128)(2,1)}, u32[]{:S(2)}) copy-start(bf16[64,32,256]{2,1,0:T(8,128)(2,1)} %param.7) | copy-start | bytes 3145732
  3.5 13.1 %collective-permute-start.1 = (f32[5,8,128]{2,1,0:T(8,128)S(1)}, f32[5,8,128]{2,1,0:T(8,128)S(1)}, u32[]{:S(2)}, u32[]{:S(2)}) collective-permute-start(f32[5,8,128]{2,1,0:T(8,128)S(1)} %get-tuple-element.25), channel_id=1, source_target_pairs={{0,1},{2,3},{4,5},{6,7},{8,9},{10,11},{12,13},{14,15},{1,0},{3,2},... | collective-permute-start | bytes 61448 | tf_op jit(solution)/shard_map/halo_y/ppermute | solution.py:454
  12.2 5.1 %collective-permute-start = (f32[5,8,128]{2,1,0:T(8,128)S(1)}, f32[5,8,128]{2,1,0:T(8,128)S(1)}, u32[]{:S(2)}, u32[]{:S(2)}) collective-permute-start(f32[5,8,128]{2,1,0:T(8,128)S(1)} %get-tuple-element.26), channel_id=1, source_target_pairs={{15,0},{1,2},{3,4},{5,6},{7,8},{9,10},{11,12},{13,14},{0,15},{2,1}... | collective-permute-start | bytes 61448 | tf_op jit(solution)/shard_map/halo_y/ppermute | solution.py:453
  15.9 13.0 %copy-start = (f32[32,32,256]{2,1,0:T(8,128)S(1)}, f32[32,32,256]{2,1,0:T(8,128)}, u32[]{:S(2)}) copy-start(f32[32,32,256]{2,1,0:T(8,128)} %get-tuple-element.13.own_ref) | copy-start | bytes 3145732
  15.9 13.0 %copy-start.1 = (f32[3,32,256]{2,1,0:T(8,128)S(1)}, f32[3,32,256]{2,1,0:T(8,128)}, u32[]{:S(2)}) copy-start(f32[3,32,256]{2,1,0:T(8,128)} %get-tuple-element.14.coup_ref) | copy-start | bytes 294916
  18.3 17.3 %collective-permute-start.2 = (f32[232,256]{1,0:T(8,128)S(1)}, f32[232,256]{1,0:T(8,128)S(1)}, u32[]{:S(2)}, u32[]{:S(2)}) collective-permute-start(f32[232,256]{1,0:T(8,128)S(1)} %get-tuple-element.34), channel_id=1, source_target_pairs={{496,0},{16,32},{48,64},{80,96},{112,128},{144,160},{176,192},{208... | collective-permute-start | bytes 712712 | tf_op jit(solution)/shard_map/halo_x/ppermute | solution.py:464
  27.0 8.6 %collective-permute-start.3 = (f32[232,256]{1,0:T(8,128)S(1)}, f32[232,256]{1,0:T(8,128)S(1)}, u32[]{:S(2)}, u32[]{:S(2)}) collective-permute-start(f32[232,256]{1,0:T(8,128)S(1)} %get-tuple-element.33), channel_id=1, source_target_pairs={{0,16},{32,48},{64,80},{96,112},{128,144},{160,176},{192,208},{224... | collective-permute-start | bytes 712712 | tf_op jit(solution)/shard_map/halo_x/ppermute | solution.py:465
  29.0 6.7 %copy-start.2 = (s32[5]{0:T(128)S(1)}, s32[5]{0:T(128)}, u32[]{:S(2)}) copy-start(s32[5]{0:T(128)} %order_ref.1) | copy-start | bytes 64

commit v6 on v5

--- a/solution.py
+++ b/solution.py
@@ -40,20 +40,26 @@
     return blocks
 
 
-def prepare_kernel(*refs):
-    sources, outputs, held, sems = refs[:4], refs[4:8], refs[8:12], refs[12]
-    copies = [pltpu.make_async_copy(a, b, sems.at[n]) for n, (a, b) in enumerate(zip(sources, held))]
-    for copy in copies:
-        copy.start()
-    for copy in copies:
-        copy.wait()
-    energy_ref, right_ref, class_ref, bond_ref = held
-    own_ref, coup_ref, rows_ref, strips_ref = outputs
-    top_at, first_at = lax.axis_index("sx") % 2, lax.axis_index("sy") % 2
+def prepare_kernel(energy_hbm, right_hbm, class_hbm, bond_hbm, own_hbm, coup_hbm, near_hbm, next_hbm, beside_hbm, across_hbm,
+                   energy_ref, right_ref, class_ref, bond_ref, own_ref, coup_ref, rows_ref, strips_ref, in_sem, out_sem):
     nright, rows, width = right_ref.shape
     lane = lane_iota()
     sub = lax.broadcasted_iota(jnp.int32, (SUB, LANES), 0)
     xtiles, rtiles, inner = rows // SUB, nright // SUB, width // LANES
+    halves = [pl.ds(h * 2 * SUB, 2 * SUB) for h in range(xtiles // 2)]
+    reads = [pltpu.make_async_copy(right_hbm.at[:, h, :], right_ref.at[:, h, :], in_sem.at[n]) for n, h in enumerate(halves)]
+    for n, (a, b) in enumerate(((energy_hbm, energy_ref), (class_hbm, class_ref), (bond_hbm, bond_ref))):
+        reads.append(pltpu.make_async_copy(a, b, in_sem.at[len(halves) + n]))
+    for copy in reads:
+        copy.start()
+    writes = []
+
+    def write(source, target):
+        copy = pltpu.make_async_copy(source, target, out_sem.at[len(writes)])
+        copy.start()
+        writes.append(copy)
+
+    top_at, first_at = lax.axis_index("sx") % 2, lax.axis_index("sy") % 2
     zero = jnp.zeros((SUB, LANES), jnp.float32)
     first, last = [zero] * (xtiles + 1), [zero] * (xtiles + 1)
 
@@ -65,6 +71,7 @@
             last[v] = jnp.where(here, turn(block, at + REACH), last[v])
 
     for half in range(xtiles // 2):
+        reads[half].wait()
         for i in range(inner):
             lanes = slice(i * LANES, (i + 1) * LANES)
             for t in range(rtiles):
@@ -84,6 +91,9 @@
                             at = (x - rows + DEPTH) * nright + t * SUB
                             rows_ref[1 - top_at, at : at + SUB, lanes] = turned[j]
                         strip(xt, t * SPAN + j * SLOT, i, turned[j])
+        write(own_ref.at[halves[half]], own_hbm.at[halves[half]])
+    for copy in reads[len(halves) :]:
+        copy.wait()
     for xt in range(xtiles):
         here = slice(xt * SUB, (xt + 1) * SUB)
         for i in range(inner):
@@ -104,28 +114,42 @@
     for v in range(xtiles + 1):
         strips_ref[first_at, v] = first[v]
         strips_ref[1 - first_at, v] = last[v]
+    write(strips_ref.at[0], beside_hbm)
+    write(strips_ref.at[1], across_hbm)
+    filled = pl.ds(0, rows_ref.shape[1])
+    write(rows_ref.at[0], near_hbm.at[filled])
+    write(rows_ref.at[1], next_hbm.at[filled])
+    write(coup_ref, coup_hbm)
+    for copy in writes:
+        copy.wait()
 
 
 def prepare(right, classes, energy, bonds):
     nright, rows, width = right.shape
-    rim = jax.ShapeDtypeStruct((2, DEPTH * nright + COUPLINGS * SUB, width), jnp.float32)
-    strip = jax.ShapeDtypeStruct((2, rows // SUB + 1, SUB, LANES), jnp.float32)
+    edge = DEPTH * nright + COUPLINGS * SUB
+    f32 = jnp.float32
+    own, coup = (rows, nright, width), (COUPLINGS, rows, width)
+    strip = (rows // SUB + 1, SUB, LANES)
+    halves = rows // (2 * SUB)
     return pl.pallas_call(
         prepare_kernel,
-        out_shape=(
-            jax.ShapeDtypeStruct((rows, nright, width), jnp.float32),
-            jax.ShapeDtypeStruct((COUPLINGS, rows, width), jnp.float32),
-            rim,
-            strip,
+        out_shape=tuple(
+            jax.ShapeDtypeStruct(shape, f32)
+            for shape in (own, coup, (edge + 2 * SUB, width), (edge + 2 * SUB, width), strip, strip)
         ),
         in_specs=[pl.BlockSpec(memory_space=pltpu.HBM)] * 4,
-        out_specs=(pl.BlockSpec(memory_space=pltpu.VMEM),) * 4,
+        out_specs=(pl.BlockSpec(memory_space=pltpu.HBM),) * 6,
         scratch_shapes=[
             pltpu.SMEM(energy.shape, energy.dtype),
             pltpu.VMEM(right.shape, right.dtype),
             pltpu.VMEM(classes.shape, classes.dtype),
             pltpu.VMEM(bonds.shape, bonds.dtype),
-            pltpu.SemaphoreType.DMA((4,)),
+            pltpu.VMEM(own, f32),
+            pltpu.VMEM(coup, f32),
+            pltpu.VMEM((2, edge, width), f32),
+            pltpu.VMEM((2,) + strip, f32),
+            pltpu.SemaphoreType.DMA((halves + 3,)),
+            pltpu.SemaphoreType.DMA((halves + 5,)),
         ],
         name="prepare",
     )(energy, right, classes, bonds)
@@ -397,8 +421,8 @@
         for row in (DEPTH - 1 + n, rows - DEPTH - n):
             contract(row, 0 <= row - 1 - DEPTH < rows_x, 0 <= row + 1 - DEPTH < rows_x)
 
-    groups, _, flat = out_ref.shape
-    owned = flat // nright
+    near, far, _, flat = out_ref.shape
+    groups, owned = near * far, flat // nright
     both_sides = acc[...].T
     half = both_sides.shape[0] // 2
     total = (both_sides[:half] - both_sides[half:]) * scale
@@ -407,7 +431,8 @@
         rows_of = [spaced[pl.ds(q, groups, stride=owned), :] for q in range(owned)]
         ranked[k] = jnp.concatenate([r[:, 0:nright] for r in rows_of], axis=1)
     for j in range(MOMENTS):
-        out_ref[:, j, :] = ranked[order_ref[j]]
+        for n in range(far):
+            out_ref[:, n, j, :] = ranked[order_ref[j], n * near : (n + 1) * near]
 
 
 def vmem_call(kernel, name, out_shape, scratch, flops, *args, scalars=()):
@@ -441,6 +466,10 @@
     return swaps + [(b, a) for a, b in swaps]
 
 
+def near_part(size):
+    return 8 if size % 8 == 0 else size
+
+
 def shards(right_vectors, left_vectors, classes, class_energy, bond_mask_grid, order):
     rows_x, rows_y = classes.shape
     nright, nleft = right_vectors.shape[0], left_vectors.shape[0]
@@ -448,21 +477,23 @@
     owned = nleft // nsy
     even_x, even_y = lax.axis_index("sx") % 2 == 0, lax.axis_index("sy") % 2 == 0
 
-    own, coup, rows, strips = prepare(right_vectors, classes, class_energy, bond_mask_grid)
+    own, coup, near_payload, next_payload, beside, across = prepare(
+        right_vectors, classes, class_energy, bond_mask_grid
+    )
     with jax.named_scope("halo_y"):
-        near = lax.ppermute(strips[0], "sy", pairs("sy", -1))
-        across = lax.ppermute(strips[1], "sy", pairs("sy", 0))
-    before, after = jnp.where(even_y, near, across), jnp.where(even_y, across, near)
+        beside = lax.ppermute(beside, "sy", pairs("sy", -1))
+        across = lax.ppermute(across, "sy", pairs("sy", 0))
+    before, after = jnp.where(even_y, beside, across), jnp.where(even_y, across, beside)
     with jax.named_scope("halo_x"):
-        def with_corners(slot):
-            upper = even_x == (slot == 0)
+        def with_corners(payload, upper):
             corners = [
                 jnp.concatenate([jnp.where(upper, part[0], part[-2]), part[-1]], axis=1) for part in (before, after)
             ]
-            return jnp.concatenate([rows[slot]] + corners, axis=0)
-
-        near_rows = lax.ppermute(with_corners(0), "sx", pairs("sx", -1))
-        next_rows = lax.ppermute(with_corners(1), "sx", pairs("sx", 0))
+            corners = jnp.concatenate(corners, axis=0)
+            return lax.dynamic_update_slice(payload, corners, (payload.shape[0] - corners.shape[0], 0))
+
+        near_rows = lax.ppermute(with_corners(near_payload, even_x), "sx", pairs("sx", -1))
+        next_rows = lax.ppermute(with_corners(next_payload, ~even_x), "sx", pairs("sx", 0))
     left = left_vectors.transpose(1, 0, 2)
     f32 = jnp.float32
     part, edge_field, edge_rim, ends = vmem_call(
@@ -478,11 +509,12 @@
         1 << 33,
         own, coup, before, after, left,
     )
+    near, depth_z = near_part(nsy), near_part(nsx)
     sites = rows_x * rows_y * nsx * nsy
     tile = vmem_call(
         functools.partial(border_kernel, -HALF_ROOT / sites**0.5),
         "border",
-        jax.ShapeDtypeStruct((nsy, MOMENTS, owned * nright), f32),
+        jax.ShapeDtypeStruct((near, nsy // near, MOMENTS, owned * nright), f32),
         scratch_of(rows_x, nright, rows_y)
         + [
             pltpu.VMEM((MOMENTS * nright, 2 * nleft), f32),
@@ -493,10 +525,25 @@
         ends, coup, near_rows, next_rows, before, after, left, part, edge_field, edge_rim,
         scalars=(order,),
     )
-    with jax.named_scope("reduce_sy"):
-        mine = jnp.sum(lax.all_to_all(tile, "sy", 0, 0), axis=0)
-    with jax.named_scope("reduce_sx"):
-        shares = lax.all_to_all(jnp.broadcast_to(mine[None], (nsx,) + mine.shape), "sx", 0, 0)
+    far_y, far_x = nsy // near, nsx // depth_z
+    block = tile.shape[2:]
+    with jax.named_scope("reduce_near"):
+        runs = [[n * near + i for i in range(near)] for n in range(far_y)]
+        mine = jnp.sum(lax.all_to_all(tile, "sy", 0, 0, axis_index_groups=runs), axis=0)
+    with jax.named_scope("reduce_far"):
+        if far_y * far_x > 1:
+            spread = jnp.broadcast_to(mine[:, None], (far_y, far_x) + block).reshape((far_y * far_x,) + block)
+            rings = [
+                [(m * depth_z + z) * nsy + n * near + i for n in range(far_y) for m in range(far_x)]
+                for z in range(depth_z)
+                for i in range(near)
+            ]
+            mine = lax.all_to_all(spread, ("sx", "sy"), 0, 0, axis_index_groups=rings)
+        mine = jnp.sum(mine, axis=0)
+    with jax.named_scope("reduce_z"):
+        runs = [[m * depth_z + z for z in range(depth_z)] for m in range(far_x)]
+        spread = jnp.broadcast_to(mine[None], (depth_z,) + block)
+        shares = lax.all_to_all(spread, "sx", 0, 0, axis_index_groups=runs)
     return jnp.sum(shares, axis=0).reshape(MOMENTS, owned, nright)
 
 

time: 76.1 us -> 72.6 us (0.954)
  the two profiles are of different devices: /device:TPU:1 before, /device:TPU:2 now
where the time goes in v6:
time: 72.6 us; the launch traced here: 72.3 us
  blocking collectives  34.7 us (48%)
  starting transfers between devices  22 us (30%)
  Pallas kernels  12.7 us (17%)
  local copies, waits for them, and re-layouts  2.55 us (4%)
    all_to_all x1, blocking collectives, shards(): mine = lax.all_to_all(spread, ('sx', 'sy'), 0, 0, axis_index_groups=rings)  12.2 us
    ppermute x1, starting transfers between devices, shards(): lax.ppermute(with_corners(near_payload, even_x), 'sx', pairs('sx', -1))  12.2 us
    all_to_all x1, blocking collectives, shards(): lax.all_to_all(tile, 'sy', 0, 0, axis_index_groups=runs)  11.3 us
    all_to_all x1, blocking collectives, shards(): shares = lax.all_to_all(spread, 'sx', 0, 0, axis_index_groups=runs)  11.1 us
    pallas_call x2, Pallas kernels, vmem_call(): pl.pallas_call(kernel, out_shape=out_shape, in_specs=[pl.BlockSpec(memory...  10.3 us
    ppermute x1, starting transfers between devices, shards(): lax.ppermute(with_corners(next_payload, ~even_x), 'sx', pairs('sx', 0))  4.28 us
    ppermute x1, starting transfers between devices, shards(): across = lax.ppermute(across, 'sy', pairs('sy', 0))  3.5 us
    pallas_call x1, Pallas kernels, prepare(): pl.pallas_call(prepare_kernel, out_shape=tuple((jax.ShapeDtypeStruct(shap...  2.42 us
  transfers between devices with their start and end apart: 4, of which 0 were waited for; matrix products, arithmetic and copies ran while one was open for 3% of the time, Pallas kernels for 9%

profile of v6, /device:TPU:2, one launch (start us, length us, event | category | flops | bytes accessed | tf_op | source)
XLA Modules:
  0.0 72.3 jit_solution(2952689411087756172)
XLA Ops:
  0.0 2.4 %prepare.1 = (f32[32,32,256]{2,1,0:T(8,128)}, f32[3,32,256]{2,1,0:T(8,128)}, f32[232,256]{1,0:T(8,128)}, f32[232,256]{1,0:T(8,128)}, f32[5,8,128]{2,1,0:T(8,128)}, /*index=5*/f32[5,8,128]{2,1,0:T(8,128)}) custom-call(f32[4]{0:T(128)} %energy_hbm.1, bf16[32,32,256]{2,1,0:T(8,128)(2,1)} %right_hbm.1, s32[32,256]{1,0:T(8,128)} %class_hbm.1, s32[2,32,256]{2,1,0:T(8,128)} %bond_hbm.1), custom_call_target="tpu_custom_call" | custom-call | tf_op jit(solution)/shard_map/prepare/pallas_call | solution.py:134
  2.4 0.0 copy-start.3
  2.4 0.0 copy-start.4
  2.5 0.0 copy-start
  2.5 0.0 copy-start.1
  2.5 2.1 %collective-permute-start = (f32[5,8,128]{2,1,0:T(8,128)}, f32[5,8,128]{2,1,0:T(8,128)S(1)}, u32[]{:S(2)}, u32[]{:S(2)}) collective-permute-start(f32[5,8,128]{2,1,0:T(8,128)} %get-tuple-element.17), channel_id=1, source_target_pairs={{15,0},{1,2},{3,4},{5,6},{7,8},{9,10},{11,12},{13,14},{0,15},{2,1}... | collective-permute-start | bytes 61448 | tf_op jit(solution)/shard_map/halo_y/ppermute | solution.py:484
  4.5 3.5 %collective-permute-start.1 = (f32[5,8,128]{2,1,0:T(8,128)}, f32[5,8,128]{2,1,0:T(8,128)S(1)}, u32[]{:S(2)}, u32[]{:S(2)}) collective-permute-start(f32[5,8,128]{2,1,0:T(8,128)} %get-tuple-element.18), channel_id=1, source_target_pairs={{0,1},{2,3},{4,5},{6,7},{8,9},{10,11},{12,13},{14,15},{1,0},{3,2},... | collective-permute-start | bytes 61448 | tf_op jit(solution)/shard_map/halo_y/ppermute | solution.py:485
  8.1 1.8 %copy.23 = bf16[64,32,256]{2,0,1:T(8,128)(2,1)S(1)} copy(bf16[64,32,256]{2,1,0:T(8,128)(2,1)} %param.7) | data formatting | bytes 2097152 | tf_op args[1]
  9.9 0.0 collective-permute-done
  9.9 0.0 collective-permute-done.1
  9.9 0.0 copy-done.3
  9.9 0.0 copy-done.4
  10.0 4.3 %collective-permute-start.3 = (f32[232,256]{1,0:T(8,128)S(1)}, f32[232,256]{1,0:T(8,128)S(1)}, u32[]{:S(2)}, u32[]{:S(2)}) collective-permute-start(f32[232,256]{1,0:T(8,128)S(1)} %get-tuple-element.33), channel_id=1, source_target_pairs={{0,16},{32,48},{64,80},{96,112},{128,144},{160,176},{192,208},{224... | collective-permute-start | bytes 712712 | tf_op jit(solution)/shard_map/halo_x/ppermute | solution.py:496
  14.3 12.2 %collective-permute-start.2 = (f32[232,256]{1,0:T(8,128)S(1)}, f32[232,256]{1,0:T(8,128)S(1)}, u32[]{:S(2)}, u32[]{:S(2)}) collective-permute-start(f32[232,256]{1,0:T(8,128)S(1)} %get-tuple-element.34), channel_id=1, source_target_pairs={{496,0},{16,32},{48,64},{80,96},{112,128},{144,160},{176,192},{208... | collective-permute-start | bytes 712712 | tf_op jit(solution)/shard_map/halo_x/ppermute | solution.py:495
  26.4 0.0 copy-done
  26.4 0.0 copy-done.1
  26.5 0.0 copy-start.2
  26.5 6.6 %interior.1 = (f32[160,128]{1,0:T(8,128)S(1)}, f32[2,4,5,32,256]{4,3,2,1,0:T(8,128)S(1)}, f32[2,4,5,8,128]{4,3,2,1,0:T(8,128)S(1)}, f32[4,32,256]{2,1,0:T(8,128)S(1)}) custom-call(f32[32,32,256]{2,1,0:T(8,128)S(1)} %copy-done, f32[3,32,256]{2,1,0:T(8,128)S(1)} %copy-done.1, f32[5,8,128]{2,1,0:T(8,128)S(1)} %get-tuple-element.26.before_ref, ...), custom_call_target="tpu_custom_call" | custom-call | flops 8589934592 | bytes 4194304 | tf_op jit(solution)/shard_map/interior/pallas_call | solution.py:441
  33.1 0.0 collective-permute-done.3.next_ref
  33.1 0.0 collective-permute-done.2.near_ref
  33.1 0.0 copy-done.2
  33.1 3.6 %border.1 = f32[8,2,5,128]{3,2,1,0:T(8,128)S(1)} custom-call(s32[5]{0:T(128)S(1)} %copy-done.2, f32[4,32,256]{2,1,0:T(8,128)S(1)} %get-tuple-element.19.ends_ref, f32[3,32,256]{2,1,0:T(8,128)S(1)} %copy-done.1, f32[232,256]{1,0:T(8,128)S(1)} %collective-permute-done.2.near_ref, f32[232,256]{1,0:T(8,128)S(1)} %collective-permute-done.3.next_ref, ...), custom_call_target="tpu_custom_call" | custom-call | flops 4294967296 | bytes 4194304 | tf_op jit(solution)/shard_map/border/pallas_call | solution.py:441
  36.8 11.3 %all_to_all.15 = f32[8,2,5,128]{3,1,2,0:T(2,128)S(1)} all-to-all(f32[8,2,5,128]{3,1,2,0:T(2,128)S(1)} %copy.16), channel_id=1, replica_groups={{0,1,2,3,4,5,6,7},{8,9,10,11,12,13,14,15},{16,17,18,19,20,21,22,23},{24..., dimensions={0} | all-to-all | bytes 81920 | tf_op jit(solution)/shard_map/reduce_near/all_to_all | solution.py:532
  48.2 12.2 %all_to_all.16 = f32[8,5,128]{2,1,0:T(8,128)S(1)} all-to-all(f32[8,5,128]{2,1,0:T(8,128)S(1)} %bitcast.18), channel_id=1, replica_groups={{0,128,256,384,8,136,264,392},{1,129,257,385,9,137,265,393},{2,130,258,..., dimensions={0} | all-to-all | bytes 40960 | tf_op jit(solution)/shard_map/reduce_far/all_to_all | solution.py:541
  60.4 11.1 %all_to_all.17 = f32[8,5,128]{2,1,0:T(8,128)S(1)} all-to-all(f32[8,5,128]{2,1,0:T(8,128)S(1)} %broadcast_in_dim.5), channel_id=1, replica_groups={{0,16,32,48,64,80,96,112},{128,144,160,176,192,208,224,240},{256,272,28..., dimensions={0} | all-to-all | bytes 40960 | tf_op jit(solution)/shard_map/reduce_z/all_to_all | solution.py:546
  71.6 0.7 reshape.17
  (10 shorter events, 0.1 us)
Async XLA Ops:
  2.4 7.5 %copy-start.3 = (f32[232,256]{1,0:T(8,128)S(1)}, f32[232,256]{1,0:T(8,128)}, u32[]{:S(2)}) copy-start(f32[232,256]{1,0:T(8,128)} %get-tuple-element.20) | copy-start | bytes 712708
  2.4 7.5 %copy-start.4 = (f32[232,256]{1,0:T(8,128)S(1)}, f32[232,256]{1,0:T(8,128)}, u32[]{:S(2)}) copy-start(f32[232,256]{1,0:T(8,128)} %get-tuple-element.21) | copy-start | bytes 712708
  2.5 24.0 %copy-start = (f32[32,32,256]{2,1,0:T(8,128)S(1)}, f32[32,32,256]{2,1,0:T(8,128)}, u32[]{:S(2)}) copy-start(f32[32,32,256]{2,1,0:T(8,128)} %get-tuple-element.15.own_ref) | copy-start | bytes 3145732
  2.5 24.0 %copy-start.1 = (f32[3,32,256]{2,1,0:T(8,128)S(1)}, f32[3,32,256]{2,1,0:T(8,128)}, u32[]{:S(2)}) copy-start(f32[3,32,256]{2,1,0:T(8,128)} %get-tuple-element.16.coup_ref) | copy-start | bytes 294916
  2.5 7.4 %collective-permute-start = (f32[5,8,128]{2,1,0:T(8,128)}, f32[5,8,128]{2,1,0:T(8,128)S(1)}, u32[]{:S(2)}, u32[]{:S(2)}) collective-permute-start(f32[5,8,128]{2,1,0:T(8,128)} %get-tuple-element.17), channel_id=1, source_target_pairs={{15,0},{1,2},{3,4},{5,6},{7,8},{9,10},{11,12},{13,14},{0,15},{2,1}... | collective-permute-start | bytes 61448 | tf_op jit(solution)/shard_map/halo_y/ppermute | solution.py:484
  4.5 5.4 %collective-permute-start.1 = (f32[5,8,128]{2,1,0:T(8,128)}, f32[5,8,128]{2,1,0:T(8,128)S(1)}, u32[]{:S(2)}, u32[]{:S(2)}) collective-permute-start(f32[5,8,128]{2,1,0:T(8,128)} %get-tuple-element.18), channel_id=1, source_target_pairs={{0,1},{2,3},{4,5},{6,7},{8,9},{10,11},{12,13},{14,15},{1,0},{3,2},... | collective-permute-start | bytes 61448 | tf_op jit(solution)/shard_map/halo_y/ppermute | solution.py:485
  10.0 23.1 %collective-permute-start.3 = (f32[232,256]{1,0:T(8,128)S(1)}, f32[232,256]{1,0:T(8,128)S(1)}, u32[]{:S(2)}, u32[]{:S(2)}) collective-permute-start(f32[232,256]{1,0:T(8,128)S(1)} %get-tuple-element.33), channel_id=1, source_target_pairs={{0,16},{32,48},{64,80},{96,112},{128,144},{160,176},{192,208},{224... | collective-permute-start | bytes 712712 | tf_op jit(solution)/shard_map/halo_x/ppermute | solution.py:496
  14.3 18.9 %collective-permute-start.2 = (f32[232,256]{1,0:T(8,128)S(1)}, f32[232,256]{1,0:T(8,128)S(1)}, u32[]{:S(2)}, u32[]{:S(2)}) collective-permute-start(f32[232,256]{1,0:T(8,128)S(1)} %get-tuple-element.34), channel_id=1, source_target_pairs={{496,0},{16,32},{48,64},{80,96},{112,128},{144,160},{176,192},{208... | collective-permute-start | bytes 712712 | tf_op jit(solution)/shard_map/halo_x/ppermute | solution.py:495
  26.5 6.7 %copy-start.2 = (s32[5]{0:T(128)S(1)}, s32[5]{0:T(128)}, u32[]{:S(2)}) copy-start(s32[5]{0:T(128)} %order_ref.1) | copy-start | bytes 64

commit v7 on v6

--- a/solution.py
+++ b/solution.py
@@ -492,7 +492,9 @@
             corners = jnp.concatenate(corners, axis=0)
             return lax.dynamic_update_slice(payload, corners, (payload.shape[0] - corners.shape[0], 0))
 
-        near_rows = lax.ppermute(with_corners(near_payload, even_x), "sx", pairs("sx", -1))
+        near_payload = with_corners(near_payload, even_x)
+        next_payload, _ = lax.optimization_barrier((next_payload, near_payload))
+        near_rows = lax.ppermute(near_payload, "sx", pairs("sx", -1))
         next_rows = lax.ppermute(with_corners(next_payload, ~even_x), "sx", pairs("sx", 0))
     left = left_vectors.transpose(1, 0, 2)
     f32 = jnp.float32
@@ -544,7 +546,8 @@
         runs = [[m * depth_z + z for z in range(depth_z)] for m in range(far_x)]
         spread = jnp.broadcast_to(mine[None], (depth_z,) + block)
         shares = lax.all_to_all(spread, "sx", 0, 0, axis_index_groups=runs)
-    return jnp.sum(shares, axis=0).reshape(MOMENTS, owned, nright)
+    total = jnp.sum(shares, axis=0)
+    return jnp.stack([total[:, q * nright : (q + 1) * nright] for q in range(owned)], axis=1)
 
 
 def solution(mesh):

time: 72.6 us -> 72.6 us (level)
    ppermute x1, starting transfers between devices: 4.28 us -> 1.92 us  [shards(): lax.ppermute(with_corners(next_payload, ~even_x), 'sx', pairs('sx', 0))]
    ppermute x1, starting transfers between devices: 12.2 us -> 14 us  [shards(): near_rows = lax.ppermute(near_payload, 'sx', pairs('sx', -1))]
  transfers between devices with their start and end apart: 4 -> 4, of which waited for: 0 -> 1; matrix products, arithmetic and copies ran while one was open for 3% -> 3% of each run, Pallas kernels for 9% -> 9%
where the time goes in v7:
time: 72.6 us; the launch traced here: 72.3 us
  blocking collectives  34.5 us (48%)
  starting transfers between devices  21.5 us (30%)
  Pallas kernels  12.7 us (17%)
  local copies, waits for them, and re-layouts  2.56 us (4%)
    ppermute x1, starting transfers between devices, shards(): near_rows = lax.ppermute(near_payload, 'sx', pairs('sx', -1))  14 us
    all_to_all x1, blocking collectives, shards(): mine = lax.all_to_all(spread, ('sx', 'sy'), 0, 0, axis_index_groups=rings)  12.2 us
    all_to_all x1, blocking collectives, shards(): shares = lax.all_to_all(spread, 'sx', 0, 0, axis_index_groups=runs)  11.4 us
    all_to_all x1, blocking collectives, shards(): lax.all_to_all(tile, 'sy', 0, 0, axis_index_groups=runs)  10.9 us
    pallas_call x2, Pallas kernels, vmem_call(): pl.pallas_call(kernel, out_shape=out_shape, in_specs=[pl.BlockSpec(memory...  10.3 us
    ppermute x1, starting transfers between devices, shards(): across = lax.ppermute(across, 'sy', pairs('sy', 0))  3.5 us
    pallas_call x1, Pallas kernels, prepare(): pl.pallas_call(prepare_kernel, out_shape=tuple((jax.ShapeDtypeStruct(shap...  2.42 us
    ppermute x1, starting transfers between devices, shards(): beside = lax.ppermute(beside, 'sy', pairs('sy', -1))  2.05 us
  transfers between devices with their start and end apart: 4, of which 1 were waited for; matrix products, arithmetic and copies ran while one was open for 3% of the time, Pallas kernels for 9%

profile of v7, /device:TPU:2, one launch (start us, length us, event | category | flops | bytes accessed | tf_op | source)
XLA Modules:
  0.0 72.3 jit_solution(2461113271449381561)
XLA Ops:
  0.0 2.4 %prepare.1 = (f32[32,32,256]{2,1,0:T(8,128)}, f32[3,32,256]{2,1,0:T(8,128)}, f32[232,256]{1,0:T(8,128)}, f32[232,256]{1,0:T(8,128)}, f32[5,8,128]{2,1,0:T(8,128)}, /*index=5*/f32[5,8,128]{2,1,0:T(8,128)}) custom-call(f32[4]{0:T(128)} %energy_hbm.1, bf16[32,32,256]{2,1,0:T(8,128)(2,1)} %right_hbm.1, s32[32,256]{1,0:T(8,128)} %class_hbm.1, s32[2,32,256]{2,1,0:T(8,128)} %bond_hbm.1), custom_call_target="tpu_custom_call" | custom-call | tf_op jit(solution)/shard_map/prepare/pallas_call | solution.py:134
  2.4 0.0 copy-start.4
  2.4 0.0 copy-start.3
  2.5 0.0 copy-start
  2.5 0.0 copy-start.1
  2.5 2.1 %collective-permute-start = (f32[5,8,128]{2,1,0:T(8,128)}, f32[5,8,128]{2,1,0:T(8,128)S(1)}, u32[]{:S(2)}, u32[]{:S(2)}) collective-permute-start(f32[5,8,128]{2,1,0:T(8,128)} %get-tuple-element.18), channel_id=1, source_target_pairs={{15,0},{1,2},{3,4},{5,6},{7,8},{9,10},{11,12},{13,14},{0,15},{2,1}... | collective-permute-start | bytes 61448 | tf_op jit(solution)/shard_map/halo_y/ppermute | solution.py:484
  4.5 3.5 %collective-permute-start.1 = (f32[5,8,128]{2,1,0:T(8,128)}, f32[5,8,128]{2,1,0:T(8,128)S(1)}, u32[]{:S(2)}, u32[]{:S(2)}) collective-permute-start(f32[5,8,128]{2,1,0:T(8,128)} %get-tuple-element.19), channel_id=1, source_target_pairs={{0,1},{2,3},{4,5},{6,7},{8,9},{10,11},{12,13},{14,15},{1,0},{3,2},... | collective-permute-start | bytes 61448 | tf_op jit(solution)/shard_map/halo_y/ppermute | solution.py:485
  8.1 1.8 %copy.36 = bf16[64,32,256]{2,0,1:T(8,128)(2,1)S(1)} copy(bf16[64,32,256]{2,1,0:T(8,128)(2,1)} %param.7) | data formatting | bytes 2097152 | tf_op args[1]
  9.9 0.0 collective-permute-done
  9.9 0.0 collective-permute-done.1
  9.9 0.0 copy-done.4
  10.0 14.0 %collective-permute-start.2 = (f32[232,256]{1,0:T(8,128)S(1)}, f32[232,256]{1,0:T(8,128)S(1)}, u32[]{:S(2)}, u32[]{:S(2)}) collective-permute-start(f32[232,256]{1,0:T(8,128)S(1)} %fusion.1), channel_id=1, source_target_pairs={{496,0},{16,32},{48,64},{80,96},{112,128},{144,160},{176,192},{208... | collective-permute-start | bytes 712712 | tf_op jit(solution)/shard_map/halo_x/ppermute | solution.py:497
  23.9 0.0 copy-done.3
  24.0 1.9 %collective-permute-start.3 = (f32[232,256]{1,0:T(8,128)S(1)}, f32[232,256]{1,0:T(8,128)S(1)}, u32[]{:S(2)}, u32[]{:S(2)}) collective-permute-start(f32[232,256]{1,0:T(8,128)S(1)} %fusion.3), channel_id=1, source_target_pairs={{0,16},{32,48},{64,80},{96,112},{128,144},{160,176},{192,208},{224... | collective-permute-start | bytes 712712 | tf_op jit(solution)/shard_map/halo_x/ppermute | solution.py:498
  25.9 0.0 copy-done
  25.9 0.0 copy-done.1
  25.9 0.0 copy-start.2
  25.9 6.7 %interior.1 = (f32[160,128]{1,0:T(8,128)S(1)}, f32[2,4,5,32,256]{4,3,2,1,0:T(8,128)S(1)}, f32[2,4,5,8,128]{4,3,2,1,0:T(8,128)S(1)}, f32[4,32,256]{2,1,0:T(8,128)S(1)}) custom-call(f32[32,32,256]{2,1,0:T(8,128)S(1)} %copy-done, f32[3,32,256]{2,1,0:T(8,128)S(1)} %copy-done.1, f32[5,8,128]{2,1,0:T(8,128)S(1)} %get-tuple-element.28.before_ref, ...), custom_call_target="tpu_custom_call" | custom-call | flops 8589934592 | bytes 4194304 | tf_op jit(solution)/shard_map/interior/pallas_call | solution.py:441
  32.6 0.7 collective-permute-done.3.next_ref
  33.3 0.0 collective-permute-done.2.near_ref
  33.3 0.0 copy-done.2
  33.3 3.6 %border.1 = f32[8,2,5,128]{3,2,1,0:T(8,128)S(1)} custom-call(s32[5]{0:T(128)S(1)} %copy-done.2, f32[4,32,256]{2,1,0:T(8,128)S(1)} %get-tuple-element.20.ends_ref, f32[3,32,256]{2,1,0:T(8,128)S(1)} %copy-done.1, f32[232,256]{1,0:T(8,128)S(1)} %collective-permute-done.2.near_ref, f32[232,256]{1,0:T(8,128)S(1)} %collective-permute-done.3.next_ref, ...), custom_call_target="tpu_custom_call" | custom-call | flops 4294967296 | bytes 4194304 | tf_op jit(solution)/shard_map/border/pallas_call | solution.py:441
  37.0 10.9 %all_to_all.15 = f32[8,2,5,128]{3,1,2,0:T(2,128)S(1)} all-to-all(f32[8,2,5,128]{3,1,2,0:T(2,128)S(1)} %copy.24), channel_id=1, replica_groups={{0,1,2,3,4,5,6,7},{8,9,10,11,12,13,14,15},{16,17,18,19,20,21,22,23},{24..., dimensions={0} | all-to-all | bytes 81920 | tf_op jit(solution)/shard_map/reduce_near/all_to_all | solution.py:534
  47.9 12.2 %all_to_all.16 = f32[8,5,128]{2,1,0:T(8,128)S(1)} all-to-all(f32[8,5,128]{2,1,0:T(8,128)S(1)} %bitcast.26), channel_id=1, replica_groups={{0,128,256,384,8,136,264,392},{1,129,257,385,9,137,265,393},{2,130,258,..., dimensions={0} | all-to-all | bytes 40960 | tf_op jit(solution)/shard_map/reduce_far/all_to_all | solution.py:543
  60.2 11.4 %all_to_all.17 = f32[8,5,128]{2,1,0:T(8,128)S(1)} all-to-all(f32[8,5,128]{2,1,0:T(8,128)S(1)} %broadcast_in_dim.5), channel_id=1, replica_groups={{0,16,32,48,64,80,96,112},{128,144,160,176,192,208,224,240},{256,272,28..., dimensions={0} | all-to-all | bytes 40960 | tf_op jit(solution)/shard_map/reduce_z/all_to_all | solution.py:548
  71.6 0.1 slice_bitcast_fusion.5
  71.7 0.6 copy.28
  (12 shorter events, 0.1 us)
Async XLA Ops:
  2.4 7.5 %copy-start.4 = (f32[232,256]{1,0:T(8,128)S(1)}, f32[232,256]{1,0:T(8,128)}, u32[]{:S(2)}) copy-start(f32[232,256]{1,0:T(8,128)} %get-tuple-element.21) | copy-start | bytes 712708
  2.4 21.5 %copy-start.3 = (f32[232,256]{1,0:T(8,128)S(1)}, f32[232,256]{1,0:T(8,128)}, u32[]{:S(2)}) copy-start(f32[232,256]{1,0:T(8,128)} %get-tuple-element.23) | copy-start | bytes 712708
  2.5 23.4 %copy-start = (f32[32,32,256]{2,1,0:T(8,128)S(1)}, f32[32,32,256]{2,1,0:T(8,128)}, u32[]{:S(2)}) copy-start(f32[32,32,256]{2,1,0:T(8,128)} %get-tuple-element.16.own_ref) | copy-start | bytes 3145732
  2.5 23.4 %copy-start.1 = (f32[3,32,256]{2,1,0:T(8,128)S(1)}, f32[3,32,256]{2,1,0:T(8,128)}, u32[]{:S(2)}) copy-start(f32[3,32,256]{2,1,0:T(8,128)} %get-tuple-element.17.coup_ref) | copy-start | bytes 294916
  2.5 7.4 %collective-permute-start = (f32[5,8,128]{2,1,0:T(8,128)}, f32[5,8,128]{2,1,0:T(8,128)S(1)}, u32[]{:S(2)}, u32[]{:S(2)}) collective-permute-start(f32[5,8,128]{2,1,0:T(8,128)} %get-tuple-element.18), channel_id=1, source_target_pairs={{15,0},{1,2},{3,4},{5,6},{7,8},{9,10},{11,12},{13,14},{0,15},{2,1}... | collective-permute-start | bytes 61448 | tf_op jit(solution)/shard_map/halo_y/ppermute | solution.py:484
  4.5 5.4 %collective-permute-start.1 = (f32[5,8,128]{2,1,0:T(8,128)}, f32[5,8,128]{2,1,0:T(8,128)S(1)}, u32[]{:S(2)}, u32[]{:S(2)}) collective-permute-start(f32[5,8,128]{2,1,0:T(8,128)} %get-tuple-element.19), channel_id=1, source_target_pairs={{0,1},{2,3},{4,5},{6,7},{8,9},{10,11},{12,13},{14,15},{1,0},{3,2},... | collective-permute-start | bytes 61448 | tf_op jit(solution)/shard_map/halo_y/ppermute | solution.py:485
  10.0 23.3 %collective-permute-start.2 = (f32[232,256]{1,0:T(8,128)S(1)}, f32[232,256]{1,0:T(8,128)S(1)}, u32[]{:S(2)}, u32[]{:S(2)}) collective-permute-start(f32[232,256]{1,0:T(8,128)S(1)} %fusion.1), channel_id=1, source_target_pairs={{496,0},{16,32},{48,64},{80,96},{112,128},{144,160},{176,192},{208... | collective-permute-start | bytes 712712 | tf_op jit(solution)/shard_map/halo_x/ppermute | solution.py:497
  24.0 9.3 %collective-permute-start.3 = (f32[232,256]{1,0:T(8,128)S(1)}, f32[232,256]{1,0:T(8,128)S(1)}, u32[]{:S(2)}, u32[]{:S(2)}) collective-permute-start(f32[232,256]{1,0:T(8,128)S(1)} %fusion.3), channel_id=1, source_target_pairs={{0,16},{32,48},{64,80},{96,112},{128,144},{160,176},{192,208},{224... | collective-permute-start | bytes 712712 | tf_op jit(solution)/shard_map/halo_x/ppermute | solution.py:498
  25.9 7.4 %copy-start.2 = (s32[5]{0:T(128)S(1)}, s32[5]{0:T(128)}, u32[]{:S(2)}) copy-start(s32[5]{0:T(128)} %order_ref.1) | copy-start | bytes 64

commit v8 on v7

--- a/solution.py
+++ b/solution.py
@@ -219,7 +219,7 @@
     )
 
 
-def stepper(field, rim, coup, open_bond, acc, left_ref):
+def stepper(field, rim, coup, open_bond, acc, left_ref, source=None):
     nright, width = field.shape[2:]
     rtiles, inner = nright // SUB, width // LANES
     rows_x = left_ref.shape[0]
@@ -231,6 +231,8 @@
     def load(k, row, t, i):
         if i == inner:
             return rim[k, row]
+        if k == 0 and source is not None:
+            return source[row - DEPTH, t * SUB : (t + 1) * SUB, lanes_of(i)]
         return field[k, row, t * SUB : (t + 1) * SUB, lanes_of(i)]
 
     def coupling(c, row, i):
@@ -311,7 +313,6 @@
     inner, xtiles = width // LANES, rows_x // SUB
     for x in range(rows_x):
         rim[0, x + DEPTH] = rim_row(before_ref[x // SUB], after_ref[x // SUB], x)
-        field[0, x + DEPTH] = own_ref[x]
 
     def blocks_of(g, c, xt):
         return [coup_ref[c, xt * SUB : (xt + 1) * SUB, i * LANES : (i + 1) * LANES] for i in range(inner)]
@@ -321,7 +322,7 @@
 
     coupling_rows(blocks_of, strips_of, range(1, xtiles + 1), xtiles, inner, coup, open_bond, rows)
     acc[...] = jnp.zeros_like(acc)
-    advance, contract = stepper(field, rim, coup, open_bond, acc, left_ref)
+    advance, contract = stepper(field, rim, coup, open_bond, acc, left_ref, own_ref)
 
     first, last = DEPTH + 1, DEPTH + rows_x - 2
     lag = 2 * MOMENTS - 1
@@ -511,7 +512,7 @@
         1 << 33,
         own, coup, before, after, left,
     )
-    near, depth_z = near_part(nsy), near_part(nsx)
+    near = near_part(nsy)
     sites = rows_x * rows_y * nsx * nsy
     tile = vmem_call(
         functools.partial(border_kernel, -HALF_ROOT / sites**0.5),
@@ -527,25 +528,15 @@
         ends, coup, near_rows, next_rows, before, after, left, part, edge_field, edge_rim,
         scalars=(order,),
     )
-    far_y, far_x = nsy // near, nsx // depth_z
+    far_y = nsy // near
     block = tile.shape[2:]
     with jax.named_scope("reduce_near"):
         runs = [[n * near + i for i in range(near)] for n in range(far_y)]
         mine = jnp.sum(lax.all_to_all(tile, "sy", 0, 0, axis_index_groups=runs), axis=0)
     with jax.named_scope("reduce_far"):
-        if far_y * far_x > 1:
-            spread = jnp.broadcast_to(mine[:, None], (far_y, far_x) + block).reshape((far_y * far_x,) + block)
-            rings = [
-                [(m * depth_z + z) * nsy + n * near + i for n in range(far_y) for m in range(far_x)]
-                for z in range(depth_z)
-                for i in range(near)
-            ]
-            mine = lax.all_to_all(spread, ("sx", "sy"), 0, 0, axis_index_groups=rings)
-        mine = jnp.sum(mine, axis=0)
-    with jax.named_scope("reduce_z"):
-        runs = [[m * depth_z + z for z in range(depth_z)] for m in range(far_x)]
-        spread = jnp.broadcast_to(mine[None], (depth_z,) + block)
-        shares = lax.all_to_all(spread, "sx", 0, 0, axis_index_groups=runs)
+        spread = jnp.broadcast_to(mine[:, None], (far_y, nsx) + block).reshape((far_y * nsx,) + block)
+        planes = [[m * nsy + n * near + i for n in range(far_y) for m in range(nsx)] for i in range(near)]
+        shares = lax.all_to_all(spread, ("sx", "sy"), 0, 0, axis_index_groups=planes)
     total = jnp.sum(shares, axis=0)
     return jnp.stack([total[:, q * nright : (q + 1) * nright] for q in range(owned)], axis=1)
 

time: 72.6 us -> 70.9 us (0.977)
  blocking collectives: 34.5 us -> 32.8 us
    all_to_all x2 -> x1, blocking collectives: 23.6 us -> 21.9 us  [shards(): lax.all_to_all(spread, ('sx', 'sy'), 0, 0, axis_index_groups=planes)]
where the time goes in v8:
time: 70.9 us; the launch traced here: 70.6 us
  blocking collectives  32.8 us (46%)
  starting transfers between devices  21.5 us (30%)
  Pallas kernels  12.7 us (18%)
  local copies, waits for them, and re-layouts  2.56 us (4%)
  waiting for transfers between devices  0.75 us (1%)
    all_to_all x1, blocking collectives, shards(): lax.all_to_all(spread, ('sx', 'sy'), 0, 0, axis_index_groups=planes)  21.9 us
    ppermute x1, starting transfers between devices, shards(): near_rows = lax.ppermute(near_payload, 'sx', pairs('sx', -1))  14 us
    all_to_all x1, blocking collectives, shards(): lax.all_to_all(tile, 'sy', 0, 0, axis_index_groups=runs)  10.9 us
    pallas_call x2, Pallas kernels, vmem_call(): pl.pallas_call(kernel, out_shape=out_shape, in_specs=[pl.BlockSpec(memory...  10.2 us
    ppermute x1, starting transfers between devices, shards(): across = lax.ppermute(across, 'sy', pairs('sy', 0))  3.5 us
    pallas_call x1, Pallas kernels, prepare(): pl.pallas_call(prepare_kernel, out_shape=tuple((jax.ShapeDtypeStruct(shap...  2.46 us
    ppermute x1, starting transfers between devices, shards(): beside = lax.ppermute(beside, 'sy', pairs('sy', -1))  2.05 us
    ppermute x1, starting transfers between devices, shards(): lax.ppermute(with_corners(next_payload, ~even_x), 'sx', pairs('sx', 0))  1.92 us
  transfers between devices with their start and end apart: 4, of which 1 were waited for; matrix products, arithmetic and copies ran while one was open for 3% of the time, Pallas kernels for 9%

profile of v8, /device:TPU:2, one launch (start us, length us, event | category | flops | bytes accessed | tf_op | source)
XLA Modules:
  0.0 70.6 jit_solution(8945520192397230502)
XLA Ops:
  0.0 2.5 %prepare.1 = (f32[32,32,256]{2,1,0:T(8,128)}, f32[3,32,256]{2,1,0:T(8,128)}, f32[232,256]{1,0:T(8,128)}, f32[232,256]{1,0:T(8,128)}, f32[5,8,128]{2,1,0:T(8,128)}, /*index=5*/f32[5,8,128]{2,1,0:T(8,128)}) custom-call(f32[4]{0:T(128)} %energy_hbm.1, bf16[32,32,256]{2,1,0:T(8,128)(2,1)} %right_hbm.1, s32[32,256]{1,0:T(8,128)} %class_hbm.1, s32[2,32,256]{2,1,0:T(8,128)} %bond_hbm.1), custom_call_target="tpu_custom_call" | custom-call | tf_op jit(solution)/shard_map/prepare/pallas_call | solution.py:134
  2.5 0.0 copy-start.4
  2.5 0.0 copy-start.3
  2.5 0.0 copy-start
  2.5 0.0 copy-start.1
  2.5 2.1 %collective-permute-start = (f32[5,8,128]{2,1,0:T(8,128)}, f32[5,8,128]{2,1,0:T(8,128)S(1)}, u32[]{:S(2)}, u32[]{:S(2)}) collective-permute-start(f32[5,8,128]{2,1,0:T(8,128)} %get-tuple-element.18), channel_id=1, source_target_pairs={{15,0},{1,2},{3,4},{5,6},{7,8},{9,10},{11,12},{13,14},{0,15},{2,1}... | collective-permute-start | bytes 61448 | tf_op jit(solution)/shard_map/halo_y/ppermute | solution.py:485
  4.6 3.5 %collective-permute-start.1 = (f32[5,8,128]{2,1,0:T(8,128)}, f32[5,8,128]{2,1,0:T(8,128)S(1)}, u32[]{:S(2)}, u32[]{:S(2)}) collective-permute-start(f32[5,8,128]{2,1,0:T(8,128)} %get-tuple-element.19), channel_id=1, source_target_pairs={{0,1},{2,3},{4,5},{6,7},{8,9},{10,11},{12,13},{14,15},{1,0},{3,2},... | collective-permute-start | bytes 61448 | tf_op jit(solution)/shard_map/halo_y/ppermute | solution.py:486
  8.1 1.8 %copy.34 = bf16[64,32,256]{2,0,1:T(8,128)(2,1)S(1)} copy(bf16[64,32,256]{2,1,0:T(8,128)(2,1)} %param.7) | data formatting | bytes 2097152 | tf_op args[1]
  9.9 0.0 collective-permute-done
  9.9 0.0 collective-permute-done.1
  10.0 0.0 copy-done.4
  10.0 14.0 %collective-permute-start.2 = (f32[232,256]{1,0:T(8,128)S(1)}, f32[232,256]{1,0:T(8,128)S(1)}, u32[]{:S(2)}, u32[]{:S(2)}) collective-permute-start(f32[232,256]{1,0:T(8,128)S(1)} %fusion.1), channel_id=1, source_target_pairs={{496,0},{16,32},{48,64},{80,96},{112,128},{144,160},{176,192},{208... | collective-permute-start | bytes 712712 | tf_op jit(solution)/shard_map/halo_x/ppermute | solution.py:498
  24.0 0.0 copy-done.3
  24.0 1.9 %collective-permute-start.3 = (f32[232,256]{1,0:T(8,128)S(1)}, f32[232,256]{1,0:T(8,128)S(1)}, u32[]{:S(2)}, u32[]{:S(2)}) collective-permute-start(f32[232,256]{1,0:T(8,128)S(1)} %fusion.3), channel_id=1, source_target_pairs={{0,16},{32,48},{64,80},{96,112},{128,144},{160,176},{192,208},{224... | collective-permute-start | bytes 712712 | tf_op jit(solution)/shard_map/halo_x/ppermute | solution.py:499
  25.9 0.0 copy-done
  25.9 0.0 copy-done.1
  26.0 0.0 copy-start.2
  26.0 6.6 %interior.1 = (f32[160,128]{1,0:T(8,128)S(1)}, f32[2,4,5,32,256]{4,3,2,1,0:T(8,128)S(1)}, f32[2,4,5,8,128]{4,3,2,1,0:T(8,128)S(1)}, f32[4,32,256]{2,1,0:T(8,128)S(1)}) custom-call(f32[32,32,256]{2,1,0:T(8,128)S(1)} %copy-done, f32[3,32,256]{2,1,0:T(8,128)S(1)} %copy-done.1, f32[5,8,128]{2,1,0:T(8,128)S(1)} %get-tuple-element.28.before_ref, ...), custom_call_target="tpu_custom_call" | custom-call | flops 8589934592 | bytes 4194304 | tf_op jit(solution)/shard_map/interior/pallas_call | solution.py:442
  32.6 0.7 %collective-permute-done.3.next_ref = f32[232,256]{1,0:T(8,128)S(1)} collective-permute-done((f32[232,256]{1,0:T(8,128)S(1)}, f32[232,256]{1,0:T(8,128)S(1)}, u32[]{:S(2)}, u32[]{:S(2)}) %collective-permute-start.3) | collective-permute-done | bytes 237600 | tf_op jit(solution)/shard_map/halo_x/ppermute | solution.py:499
  33.3 0.0 collective-permute-done.2.near_ref
  33.3 0.0 copy-done.2
  33.3 3.6 %border.1 = f32[8,2,5,128]{3,2,1,0:T(8,128)S(1)} custom-call(s32[5]{0:T(128)S(1)} %copy-done.2, f32[4,32,256]{2,1,0:T(8,128)S(1)} %get-tuple-element.20.ends_ref, f32[3,32,256]{2,1,0:T(8,128)S(1)} %copy-done.1, f32[232,256]{1,0:T(8,128)S(1)} %collective-permute-done.2.near_ref, f32[232,256]{1,0:T(8,128)S(1)} %collective-permute-done.3.next_ref, ...), custom_call_target="tpu_custom_call" | custom-call | flops 4294967296 | bytes 4194304 | tf_op jit(solution)/shard_map/border/pallas_call | solution.py:442
  37.0 10.9 %all_to_all.10 = f32[8,2,5,128]{3,1,2,0:T(2,128)S(1)} all-to-all(f32[8,2,5,128]{3,1,2,0:T(2,128)S(1)} %copy.24), channel_id=1, replica_groups={{0,1,2,3,4,5,6,7},{8,9,10,11,12,13,14,15},{16,17,18,19,20,21,22,23},{24..., dimensions={0} | all-to-all | bytes 81920 | tf_op jit(solution)/shard_map/reduce_near/all_to_all | solution.py:535
  47.9 21.9 %all_to_all.11 = f32[64,5,128]{2,1,0:T(8,128)S(1)} all-to-all(f32[64,5,128]{2,1,0:T(8,128)S(1)} %bitcast.26), channel_id=1, replica_groups={{0,16,32,48,64,80,96,112,128,144,160,176,192,208,224,240,256,272,288,30..., dimensions={0} | all-to-all | bytes 327680 | tf_op jit(solution)/shard_map/reduce_far/all_to_all | solution.py:539
  69.8 0.1 reduce_sum.19
  69.9 0.1 slice_bitcast_fusion.5
  70.0 0.6 copy.27
  (9 shorter events, 0.1 us)
Async XLA Ops:
  2.5 7.5 %copy-start.4 = (f32[232,256]{1,0:T(8,128)S(1)}, f32[232,256]{1,0:T(8,128)}, u32[]{:S(2)}) copy-start(f32[232,256]{1,0:T(8,128)} %get-tuple-element.21) | copy-start | bytes 712708
  2.5 21.5 %copy-start.3 = (f32[232,256]{1,0:T(8,128)S(1)}, f32[232,256]{1,0:T(8,128)}, u32[]{:S(2)}) copy-start(f32[232,256]{1,0:T(8,128)} %get-tuple-element.23) | copy-start | bytes 712708
  2.5 23.4 %copy-start = (f32[32,32,256]{2,1,0:T(8,128)S(1)}, f32[32,32,256]{2,1,0:T(8,128)}, u32[]{:S(2)}) copy-start(f32[32,32,256]{2,1,0:T(8,128)} %get-tuple-element.16.own_ref) | copy-start | bytes 3145732
  2.5 23.4 %copy-start.1 = (f32[3,32,256]{2,1,0:T(8,128)S(1)}, f32[3,32,256]{2,1,0:T(8,128)}, u32[]{:S(2)}) copy-start(f32[3,32,256]{2,1,0:T(8,128)} %get-tuple-element.17.coup_ref) | copy-start | bytes 294916
  2.5 7.4 %collective-permute-start = (f32[5,8,128]{2,1,0:T(8,128)}, f32[5,8,128]{2,1,0:T(8,128)S(1)}, u32[]{:S(2)}, u32[]{:S(2)}) collective-permute-start(f32[5,8,128]{2,1,0:T(8,128)} %get-tuple-element.18), channel_id=1, source_target_pairs={{15,0},{1,2},{3,4},{5,6},{7,8},{9,10},{11,12},{13,14},{0,15},{2,1}... | collective-permute-start | bytes 61448 | tf_op jit(solution)/shard_map/halo_y/ppermute | solution.py:485
  4.6 5.4 %collective-permute-start.1 = (f32[5,8,128]{2,1,0:T(8,128)}, f32[5,8,128]{2,1,0:T(8,128)S(1)}, u32[]{:S(2)}, u32[]{:S(2)}) collective-permute-start(f32[5,8,128]{2,1,0:T(8,128)} %get-tuple-element.19), channel_id=1, source_target_pairs={{0,1},{2,3},{4,5},{6,7},{8,9},{10,11},{12,13},{14,15},{1,0},{3,2},... | collective-permute-start | bytes 61448 | tf_op jit(solution)/shard_map/halo_y/ppermute | solution.py:486
  10.0 23.3 %collective-permute-start.2 = (f32[232,256]{1,0:T(8,128)S(1)}, f32[232,256]{1,0:T(8,128)S(1)}, u32[]{:S(2)}, u32[]{:S(2)}) collective-permute-start(f32[232,256]{1,0:T(8,128)S(1)} %fusion.1), channel_id=1, source_target_pairs={{496,0},{16,32},{48,64},{80,96},{112,128},{144,160},{176,192},{208... | collective-permute-start | bytes 712712 | tf_op jit(solution)/shard_map/halo_x/ppermute | solution.py:498
  24.0 9.3 %collective-permute-start.3 = (f32[232,256]{1,0:T(8,128)S(1)}, f32[232,256]{1,0:T(8,128)S(1)}, u32[]{:S(2)}, u32[]{:S(2)}) collective-permute-start(f32[232,256]{1,0:T(8,128)S(1)} %fusion.3), channel_id=1, source_target_pairs={{0,16},{32,48},{64,80},{96,112},{128,144},{160,176},{192,208},{224... | collective-permute-start | bytes 712712 | tf_op jit(solution)/shard_map/halo_x/ppermute | solution.py:499
  26.0 7.4 %copy-start.2 = (s32[5]{0:T(128)S(1)}, s32[5]{0:T(128)}, u32[]{:S(2)}) copy-start(s32[5]{0:T(128)} %order_ref.1) | copy-start | bytes 64

commit v9 on v8

--- a/solution.py
+++ b/solution.py
@@ -423,6 +423,7 @@
             contract(row, 0 <= row - 1 - DEPTH < rows_x, 0 <= row + 1 - DEPTH < rows_x)
 
     near, far, _, flat = out_ref.shape
+    flat //= MOMENTS
     groups, owned = near * far, flat // nright
     both_sides = acc[...].T
     half = both_sides.shape[0] // 2
@@ -433,7 +434,7 @@
         ranked[k] = jnp.concatenate([r[:, 0:nright] for r in rows_of], axis=1)
     for j in range(MOMENTS):
         for n in range(far):
-            out_ref[:, n, j, :] = ranked[order_ref[j], n * near : (n + 1) * near]
+            out_ref[:, n, 0, j * flat : (j + 1) * flat] = ranked[order_ref[j], n * near : (n + 1) * near]
 
 
 def vmem_call(kernel, name, out_shape, scratch, flops, *args, scalars=()):
@@ -517,7 +518,7 @@
     tile = vmem_call(
         functools.partial(border_kernel, -HALF_ROOT / sites**0.5),
         "border",
-        jax.ShapeDtypeStruct((near, nsy // near, MOMENTS, owned * nright), f32),
+        jax.ShapeDtypeStruct((near, nsy // near, 1, MOMENTS * owned * nright), f32),
         scratch_of(rows_x, nright, rows_y)
         + [
             pltpu.VMEM((MOMENTS * nright, 2 * nleft), f32),
@@ -538,6 +539,8 @@
         planes = [[m * nsy + n * near + i for n in range(far_y) for m in range(nsx)] for i in range(near)]
         shares = lax.all_to_all(spread, ("sx", "sy"), 0, 0, axis_index_groups=planes)
     total = jnp.sum(shares, axis=0)
+    wide = owned * nright
+    total = jnp.concatenate([total[:, j * wide : (j + 1) * wide] for j in range(MOMENTS)], axis=0)
     return jnp.stack([total[:, q * nright : (q + 1) * nright] for q in range(owned)], axis=1)
 
 

time: 70.9 us -> 69.3 us (0.977)
  the two profiles are of different devices: /device:TPU:2 before, /device:TPU:1 now
where the time goes in v9:
time: 69.3 us; the launch traced here: 69 us
  blocking collectives  27.3 us (39%)
  starting transfers between devices  25.8 us (37%)
  Pallas kernels  12.7 us (18%)
  local copies, waits for them, and re-layouts  2.72 us (4%)
    all_to_all x1, blocking collectives, shards(): lax.all_to_all(spread, ('sx', 'sy'), 0, 0, axis_index_groups=planes)  18.4 us
    ppermute x1, starting transfers between devices, shards(): near_rows = lax.ppermute(near_payload, 'sx', pairs('sx', -1))  11 us
    pallas_call x2, Pallas kernels, vmem_call(): pl.pallas_call(kernel, out_shape=out_shape, in_specs=[pl.BlockSpec(memory...  10.3 us
    all_to_all x1, blocking collectives, shards(): lax.all_to_all(tile, 'sy', 0, 0, axis_index_groups=runs)  8.89 us
    ppermute x1, starting transfers between devices, shards(): across = lax.ppermute(across, 'sy', pairs('sy', 0))  8.27 us
    ppermute x1, starting transfers between devices, shards(): beside = lax.ppermute(beside, 'sy', pairs('sy', -1))  4.64 us
    pallas_call x1, Pallas kernels, prepare(): pl.pallas_call(prepare_kernel, out_shape=tuple((jax.ShapeDtypeStruct(shap...  2.44 us
    ppermute x1, starting transfers between devices, shards(): lax.ppermute(with_corners(next_payload, ~even_x), 'sx', pairs('sx', 0))  1.92 us
  transfers between devices with their start and end apart: 4, of which 0 were waited for; matrix products, arithmetic and copies ran while one was open for 3% of the time, Pallas kernels for 10%

profile of v9, /device:TPU:1, one launch (start us, length us, event | category | flops | bytes accessed | tf_op | source)
XLA Modules:
  0.0 69.0 jit_solution(12634921042910703201)
XLA Ops:
  0.0 2.4 %prepare.1 = (f32[32,32,256]{2,1,0:T(8,128)}, f32[3,32,256]{2,1,0:T(8,128)}, f32[232,256]{1,0:T(8,128)}, f32[232,256]{1,0:T(8,128)}, f32[5,8,128]{2,1,0:T(8,128)}, /*index=5*/f32[5,8,128]{2,1,0:T(8,128)}) custom-call(f32[4]{0:T(128)} %energy_hbm.1, bf16[32,32,256]{2,1,0:T(8,128)(2,1)} %right_hbm.1, s32[32,256]{1,0:T(8,128)} %class_hbm.1, s32[2,32,256]{2,1,0:T(8,128)} %bond_hbm.1), custom_call_target="tpu_custom_call" | custom-call | tf_op jit(solution)/shard_map/prepare/pallas_call | solution.py:134
  2.4 0.0 copy-start.4
  2.5 0.0 copy-start.3
  2.5 0.0 copy-start
  2.5 0.0 copy-start.1
  2.5 4.6 %collective-permute-start = (f32[5,8,128]{2,1,0:T(8,128)}, f32[5,8,128]{2,1,0:T(8,128)S(1)}, u32[]{:S(2)}, u32[]{:S(2)}) collective-permute-start(f32[5,8,128]{2,1,0:T(8,128)} %get-tuple-element.18), channel_id=1, source_target_pairs={{15,0},{1,2},{3,4},{5,6},{7,8},{9,10},{11,12},{13,14},{0,15},{2,1}... | collective-permute-start | bytes 61448 | tf_op jit(solution)/shard_map/halo_y/ppermute | solution.py:486
  7.1 8.3 %collective-permute-start.1 = (f32[5,8,128]{2,1,0:T(8,128)}, f32[5,8,128]{2,1,0:T(8,128)S(1)}, u32[]{:S(2)}, u32[]{:S(2)}) collective-permute-start(f32[5,8,128]{2,1,0:T(8,128)} %get-tuple-element.19), channel_id=1, source_target_pairs={{0,1},{2,3},{4,5},{6,7},{8,9},{10,11},{12,13},{14,15},{1,0},{3,2},... | collective-permute-start | bytes 61448 | tf_op jit(solution)/shard_map/halo_y/ppermute | solution.py:487
  15.4 1.8 %copy.16 = bf16[64,32,256]{2,0,1:T(8,128)(2,1)S(1)} copy(bf16[64,32,256]{2,1,0:T(8,128)(2,1)} %param.7) | data formatting | bytes 2097152 | tf_op args[1]
  17.2 0.0 collective-permute-done
  17.3 0.0 collective-permute-done.1
  17.3 0.0 copy-done.4
  17.3 11.0 %collective-permute-start.2 = (f32[232,256]{1,0:T(8,128)S(1)}, f32[232,256]{1,0:T(8,128)S(1)}, u32[]{:S(2)}, u32[]{:S(2)}) collective-permute-start(f32[232,256]{1,0:T(8,128)S(1)} %fusion.1), channel_id=1, source_target_pairs={{496,0},{16,32},{48,64},{80,96},{112,128},{144,160},{176,192},{208... | collective-permute-start | bytes 712712 | tf_op jit(solution)/shard_map/halo_x/ppermute | solution.py:499
  28.3 0.0 copy-done.3
  28.4 1.9 %collective-permute-start.3 = (f32[232,256]{1,0:T(8,128)S(1)}, f32[232,256]{1,0:T(8,128)S(1)}, u32[]{:S(2)}, u32[]{:S(2)}) collective-permute-start(f32[232,256]{1,0:T(8,128)S(1)} %fusion.3), channel_id=1, source_target_pairs={{0,16},{32,48},{64,80},{96,112},{128,144},{160,176},{192,208},{224... | collective-permute-start | bytes 712712 | tf_op jit(solution)/shard_map/halo_x/ppermute | solution.py:500
  30.3 0.0 copy-done
  30.3 0.0 copy-done.1
  30.3 0.0 copy-start.2
  30.3 6.6 %interior.1 = (f32[160,128]{1,0:T(8,128)S(1)}, f32[2,4,5,32,256]{4,3,2,1,0:T(8,128)S(1)}, f32[2,4,5,8,128]{4,3,2,1,0:T(8,128)S(1)}, f32[4,32,256]{2,1,0:T(8,128)S(1)}) custom-call(f32[32,32,256]{2,1,0:T(8,128)S(1)} %copy-done, f32[3,32,256]{2,1,0:T(8,128)S(1)} %copy-done.1, f32[5,8,128]{2,1,0:T(8,128)S(1)} %get-tuple-element.28.before_ref, ...), custom_call_target="tpu_custom_call" | custom-call | flops 8589934592 | bytes 4194304 | tf_op jit(solution)/shard_map/interior/pallas_call | solution.py:443
  36.9 0.0 collective-permute-done.3.next_ref
  36.9 0.0 collective-permute-done.2.near_ref
  36.9 0.0 copy-done.2
  37.0 3.6 %border.1 = f32[8,2,1,640]{3,2,1,0:T(1,128)S(1)} custom-call(s32[5]{0:T(128)S(1)} %copy-done.2, f32[4,32,256]{2,1,0:T(8,128)S(1)} %get-tuple-element.20.ends_ref, f32[3,32,256]{2,1,0:T(8,128)S(1)} %copy-done.1, f32[232,256]{1,0:T(8,128)S(1)} %collective-permute-done.2.near_ref, f32[232,256]{1,0:T(8,128)S(1)} %collective-permute-done.3.next_ref, ...), custom_call_target="tpu_custom_call" | custom-call | flops 4294967296 | bytes 4194304 | tf_op jit(solution)/shard_map/border/pallas_call | solution.py:443
  40.6 8.9 %all_to_all.10 = f32[8,2,1,640]{3,2,1,0:T(1,128)S(1)} all-to-all(f32[8,2,1,640]{3,2,1,0:T(1,128)S(1)} %border.1), channel_id=1, replica_groups={{0,1,2,3,4,5,6,7},{8,9,10,11,12,13,14,15},{16,17,18,19,20,21,22,23},{24..., dimensions={0} | all-to-all | bytes 81920 | tf_op jit(solution)/shard_map/reduce_near/all_to_all | solution.py:536
  49.6 0.2 broadcast_in_dim.9
  49.7 18.4 %all_to_all.11 = f32[64,1,640]{2,1,0:T(1,128)S(1)} all-to-all(f32[64,1,640]{2,1,0:T(1,128)S(1)} %broadcast_in_dim.9), channel_id=1, replica_groups={{0,16,32,48,64,80,96,112,128,144,160,176,192,208,224,240,256,272,288,30..., dimensions={0} | all-to-all | bytes 327680 | tf_op jit(solution)/shard_map/reduce_far/all_to_all | solution.py:540
  68.1 0.1 reduce_sum.21
  68.3 0.1 slice_bitcast_fusion.5
  68.4 0.6 copy.14
  (10 shorter events, 0.1 us)
Async XLA Ops:
  2.4 14.9 %copy-start.4 = (f32[232,256]{1,0:T(8,128)S(1)}, f32[232,256]{1,0:T(8,128)}, u32[]{:S(2)}) copy-start(f32[232,256]{1,0:T(8,128)} %get-tuple-element.21) | copy-start | bytes 712708
  2.5 25.9 %copy-start.3 = (f32[232,256]{1,0:T(8,128)S(1)}, f32[232,256]{1,0:T(8,128)}, u32[]{:S(2)}) copy-start(f32[232,256]{1,0:T(8,128)} %get-tuple-element.23) | copy-start | bytes 712708
  2.5 27.8 %copy-start = (f32[32,32,256]{2,1,0:T(8,128)S(1)}, f32[32,32,256]{2,1,0:T(8,128)}, u32[]{:S(2)}) copy-start(f32[32,32,256]{2,1,0:T(8,128)} %get-tuple-element.16.own_ref) | copy-start | bytes 3145732
  2.5 27.8 %copy-start.1 = (f32[3,32,256]{2,1,0:T(8,128)S(1)}, f32[3,32,256]{2,1,0:T(8,128)}, u32[]{:S(2)}) copy-start(f32[3,32,256]{2,1,0:T(8,128)} %get-tuple-element.17.coup_ref) | copy-start | bytes 294916
  2.5 14.8 %collective-permute-start = (f32[5,8,128]{2,1,0:T(8,128)}, f32[5,8,128]{2,1,0:T(8,128)S(1)}, u32[]{:S(2)}, u32[]{:S(2)}) collective-permute-start(f32[5,8,128]{2,1,0:T(8,128)} %get-tuple-element.18), channel_id=1, source_target_pairs={{15,0},{1,2},{3,4},{5,6},{7,8},{9,10},{11,12},{13,14},{0,15},{2,1}... | collective-permute-start | bytes 61448 | tf_op jit(solution)/shard_map/halo_y/ppermute | solution.py:486
  7.1 10.1 %collective-permute-start.1 = (f32[5,8,128]{2,1,0:T(8,128)}, f32[5,8,128]{2,1,0:T(8,128)S(1)}, u32[]{:S(2)}, u32[]{:S(2)}) collective-permute-start(f32[5,8,128]{2,1,0:T(8,128)} %get-tuple-element.19), channel_id=1, source_target_pairs={{0,1},{2,3},{4,5},{6,7},{8,9},{10,11},{12,13},{14,15},{1,0},{3,2},... | collective-permute-start | bytes 61448 | tf_op jit(solution)/shard_map/halo_y/ppermute | solution.py:487
  17.3 19.6 %collective-permute-start.2 = (f32[232,256]{1,0:T(8,128)S(1)}, f32[232,256]{1,0:T(8,128)S(1)}, u32[]{:S(2)}, u32[]{:S(2)}) collective-permute-start(f32[232,256]{1,0:T(8,128)S(1)} %fusion.1), channel_id=1, source_target_pairs={{496,0},{16,32},{48,64},{80,96},{112,128},{144,160},{176,192},{208... | collective-permute-start | bytes 712712 | tf_op jit(solution)/shard_map/halo_x/ppermute | solution.py:499
  28.4 8.6 %collective-permute-start.3 = (f32[232,256]{1,0:T(8,128)S(1)}, f32[232,256]{1,0:T(8,128)S(1)}, u32[]{:S(2)}, u32[]{:S(2)}) collective-permute-start(f32[232,256]{1,0:T(8,128)S(1)} %fusion.3), channel_id=1, source_target_pairs={{0,16},{32,48},{64,80},{96,112},{128,144},{160,176},{192,208},{224... | collective-permute-start | bytes 712712 | tf_op jit(solution)/shard_map/halo_x/ppermute | solution.py:500
  30.3 6.6 %copy-start.2 = (s32[5]{0:T(128)S(1)}, s32[5]{0:T(128)}, u32[]{:S(2)}) copy-start(s32[5]{0:T(128)} %order_ref.1) | copy-start | bytes 64

commit v10 on v9

--- a/solution.py
+++ b/solution.py
@@ -334,21 +334,7 @@
             if first + 3 * k <= front <= last + k:
                 advance(k, front - 2 * k, front % 2 == 1)
 
-    lead = first + MOMENTS - 1 + lag
-    pairs = (last - lead + 1) // 2
-    for front in range(first, lead):
-        front_step(front)
-
-    def both(n, _):
-        for part in range(2):
-            front = lead + 2 * n + part
-            contract(front - lag)
-            for k in reversed(range(MOMENTS)):
-                advance(k, front - 2 * k, (lead + part) % 2 == 1)
-        return 0
-
-    lax.fori_loop(0, pairs, both, 0)
-    for front in range(lead + 2 * pairs, last - MOMENTS + 1 + lag + 1):
+    for front in range(first, last - MOMENTS + 1 + lag + 1):
         front_step(front)
     for k in range(MOMENTS - 1):
         for side, at in enumerate((first, last - MOMENTS + 1)):

time: 69.3 us -> 69.2 us (level)
  transfers between devices with their start and end apart: 4 -> 4, of which waited for: 0 -> 0; matrix products, arithmetic and copies ran while one was open for 3% -> 3% of each run, Pallas kernels for 10% -> 9%
where the time goes in v10:
time: 69.2 us; the launch traced here: 68.8 us
  blocking collectives  27.3 us (39%)
  starting transfers between devices  25.8 us (37%)
  Pallas kernels  12.5 us (18%)
  local copies, waits for them, and re-layouts  2.72 us (4%)
    all_to_all x1, blocking collectives, shards(): lax.all_to_all(spread, ('sx', 'sy'), 0, 0, axis_index_groups=planes)  18.4 us
    ppermute x1, starting transfers between devices, shards(): near_rows = lax.ppermute(near_payload, 'sx', pairs('sx', -1))  11 us
    pallas_call x2, Pallas kernels, vmem_call(): pl.pallas_call(kernel, out_shape=out_shape, in_specs=[pl.BlockSpec(memory...  10.1 us
    all_to_all x1, blocking collectives, shards(): lax.all_to_all(tile, 'sy', 0, 0, axis_index_groups=runs)  8.89 us
    ppermute x1, starting transfers between devices, shards(): across = lax.ppermute(across, 'sy', pairs('sy', 0))  8.27 us
    ppermute x1, starting transfers between devices, shards(): beside = lax.ppermute(beside, 'sy', pairs('sy', -1))  4.64 us
    pallas_call x1, Pallas kernels, prepare(): pl.pallas_call(prepare_kernel, out_shape=tuple((jax.ShapeDtypeStruct(shap...  2.44 us
    ppermute x1, starting transfers between devices, shards(): lax.ppermute(with_corners(next_payload, ~even_x), 'sx', pairs('sx', 0))  1.92 us
  transfers between devices with their start and end apart: 4, of which 0 were waited for; matrix products, arithmetic and copies ran while one was open for 3% of the time, Pallas kernels for 9%

profile of v10, /device:TPU:1, one launch (start us, length us, event | category | flops | bytes accessed | tf_op | source)
XLA Modules:
  0.0 68.8 jit_solution(9030787057918739260)
XLA Ops:
  0.0 2.4 %prepare.1 = (f32[32,32,256]{2,1,0:T(8,128)}, f32[3,32,256]{2,1,0:T(8,128)}, f32[232,256]{1,0:T(8,128)}, f32[232,256]{1,0:T(8,128)}, f32[5,8,128]{2,1,0:T(8,128)}, /*index=5*/f32[5,8,128]{2,1,0:T(8,128)}) custom-call(f32[4]{0:T(128)} %energy_hbm.1, bf16[32,32,256]{2,1,0:T(8,128)(2,1)} %right_hbm.1, s32[32,256]{1,0:T(8,128)} %class_hbm.1, s32[2,32,256]{2,1,0:T(8,128)} %bond_hbm.1), custom_call_target="tpu_custom_call" | custom-call | tf_op jit(solution)/shard_map/prepare/pallas_call | solution.py:134
  2.4 0.0 copy-start.4
  2.5 0.0 copy-start.3
  2.5 0.0 copy-start
  2.5 0.0 copy-start.1
  2.5 4.6 %collective-permute-start = (f32[5,8,128]{2,1,0:T(8,128)}, f32[5,8,128]{2,1,0:T(8,128)S(1)}, u32[]{:S(2)}, u32[]{:S(2)}) collective-permute-start(f32[5,8,128]{2,1,0:T(8,128)} %get-tuple-element.18), channel_id=1, source_target_pairs={{15,0},{1,2},{3,4},{5,6},{7,8},{9,10},{11,12},{13,14},{0,15},{2,1}... | collective-permute-start | bytes 61448 | tf_op jit(solution)/shard_map/halo_y/ppermute | solution.py:472
  7.1 8.3 %collective-permute-start.1 = (f32[5,8,128]{2,1,0:T(8,128)}, f32[5,8,128]{2,1,0:T(8,128)S(1)}, u32[]{:S(2)}, u32[]{:S(2)}) collective-permute-start(f32[5,8,128]{2,1,0:T(8,128)} %get-tuple-element.19), channel_id=1, source_target_pairs={{0,1},{2,3},{4,5},{6,7},{8,9},{10,11},{12,13},{14,15},{1,0},{3,2},... | collective-permute-start | bytes 61448 | tf_op jit(solution)/shard_map/halo_y/ppermute | solution.py:473
  15.4 1.8 %copy.16 = bf16[64,32,256]{2,0,1:T(8,128)(2,1)S(1)} copy(bf16[64,32,256]{2,1,0:T(8,128)(2,1)} %param.7) | data formatting | bytes 2097152 | tf_op args[1]
  17.2 0.0 collective-permute-done
  17.3 0.0 collective-permute-done.1
  17.3 0.0 copy-done.4
  17.3 11.0 %collective-permute-start.2 = (f32[232,256]{1,0:T(8,128)S(1)}, f32[232,256]{1,0:T(8,128)S(1)}, u32[]{:S(2)}, u32[]{:S(2)}) collective-permute-start(f32[232,256]{1,0:T(8,128)S(1)} %fusion.1), channel_id=1, source_target_pairs={{496,0},{16,32},{48,64},{80,96},{112,128},{144,160},{176,192},{208... | collective-permute-start | bytes 712712 | tf_op jit(solution)/shard_map/halo_x/ppermute | solution.py:485
  28.3 0.0 copy-done.3
  28.4 1.9 %collective-permute-start.3 = (f32[232,256]{1,0:T(8,128)S(1)}, f32[232,256]{1,0:T(8,128)S(1)}, u32[]{:S(2)}, u32[]{:S(2)}) collective-permute-start(f32[232,256]{1,0:T(8,128)S(1)} %fusion.3), channel_id=1, source_target_pairs={{0,16},{32,48},{64,80},{96,112},{128,144},{160,176},{192,208},{224... | collective-permute-start | bytes 712712 | tf_op jit(solution)/shard_map/halo_x/ppermute | solution.py:486
  30.3 0.0 copy-done
  30.3 0.0 copy-done.1
  30.3 0.0 copy-start.2
  30.3 6.4 %interior.1 = (f32[160,128]{1,0:T(8,128)S(1)}, f32[2,4,5,32,256]{4,3,2,1,0:T(8,128)S(1)}, f32[2,4,5,8,128]{4,3,2,1,0:T(8,128)S(1)}, f32[4,32,256]{2,1,0:T(8,128)S(1)}) custom-call(f32[32,32,256]{2,1,0:T(8,128)S(1)} %copy-done, f32[3,32,256]{2,1,0:T(8,128)S(1)} %copy-done.1, f32[5,8,128]{2,1,0:T(8,128)S(1)} %get-tuple-element.28.before_ref, ...), custom_call_target="tpu_custom_call" | custom-call | flops 8589934592 | bytes 4194304 | tf_op jit(solution)/shard_map/interior/pallas_call | solution.py:429
  36.8 0.0 collective-permute-done.3.next_ref
  36.8 0.0 collective-permute-done.2.near_ref
  36.8 0.0 copy-done.2
  36.8 3.6 %border.1 = f32[8,2,1,640]{3,2,1,0:T(1,128)S(1)} custom-call(s32[5]{0:T(128)S(1)} %copy-done.2, f32[4,32,256]{2,1,0:T(8,128)S(1)} %get-tuple-element.20.ends_ref, f32[3,32,256]{2,1,0:T(8,128)S(1)} %copy-done.1, f32[232,256]{1,0:T(8,128)S(1)} %collective-permute-done.2.near_ref, f32[232,256]{1,0:T(8,128)S(1)} %collective-permute-done.3.next_ref, ...), custom_call_target="tpu_custom_call" | custom-call | flops 4294967296 | bytes 4194304 | tf_op jit(solution)/shard_map/border/pallas_call | solution.py:429
  40.5 8.9 %all_to_all.10 = f32[8,2,1,640]{3,2,1,0:T(1,128)S(1)} all-to-all(f32[8,2,1,640]{3,2,1,0:T(1,128)S(1)} %border.1), channel_id=1, replica_groups={{0,1,2,3,4,5,6,7},{8,9,10,11,12,13,14,15},{16,17,18,19,20,21,22,23},{24..., dimensions={0} | all-to-all | bytes 81920 | tf_op jit(solution)/shard_map/reduce_near/all_to_all | solution.py:522
  49.4 0.2 broadcast_in_dim.9
  49.6 18.4 %all_to_all.11 = f32[64,1,640]{2,1,0:T(1,128)S(1)} all-to-all(f32[64,1,640]{2,1,0:T(1,128)S(1)} %broadcast_in_dim.9), channel_id=1, replica_groups={{0,16,32,48,64,80,96,112,128,144,160,176,192,208,224,240,256,272,288,30..., dimensions={0} | all-to-all | bytes 327680 | tf_op jit(solution)/shard_map/reduce_far/all_to_all | solution.py:526
  68.0 0.1 reduce_sum.21
  68.1 0.1 slice_bitcast_fusion.5
  68.2 0.6 copy.14
  (10 shorter events, 0.1 us)
Async XLA Ops:
  2.4 14.9 %copy-start.4 = (f32[232,256]{1,0:T(8,128)S(1)}, f32[232,256]{1,0:T(8,128)}, u32[]{:S(2)}) copy-start(f32[232,256]{1,0:T(8,128)} %get-tuple-element.21) | copy-start | bytes 712708
  2.5 25.9 %copy-start.3 = (f32[232,256]{1,0:T(8,128)S(1)}, f32[232,256]{1,0:T(8,128)}, u32[]{:S(2)}) copy-start(f32[232,256]{1,0:T(8,128)} %get-tuple-element.23) | copy-start | bytes 712708
  2.5 27.8 %copy-start = (f32[32,32,256]{2,1,0:T(8,128)S(1)}, f32[32,32,256]{2,1,0:T(8,128)}, u32[]{:S(2)}) copy-start(f32[32,32,256]{2,1,0:T(8,128)} %get-tuple-element.16.own_ref) | copy-start | bytes 3145732
  2.5 27.8 %copy-start.1 = (f32[3,32,256]{2,1,0:T(8,128)S(1)}, f32[3,32,256]{2,1,0:T(8,128)}, u32[]{:S(2)}) copy-start(f32[3,32,256]{2,1,0:T(8,128)} %get-tuple-element.17.coup_ref) | copy-start | bytes 294916
  2.5 14.8 %collective-permute-start = (f32[5,8,128]{2,1,0:T(8,128)}, f32[5,8,128]{2,1,0:T(8,128)S(1)}, u32[]{:S(2)}, u32[]{:S(2)}) collective-permute-start(f32[5,8,128]{2,1,0:T(8,128)} %get-tuple-element.18), channel_id=1, source_target_pairs={{15,0},{1,2},{3,4},{5,6},{7,8},{9,10},{11,12},{13,14},{0,15},{2,1}... | collective-permute-start | bytes 61448 | tf_op jit(solution)/shard_map/halo_y/ppermute | solution.py:472
  7.1 10.1 %collective-permute-start.1 = (f32[5,8,128]{2,1,0:T(8,128)}, f32[5,8,128]{2,1,0:T(8,128)S(1)}, u32[]{:S(2)}, u32[]{:S(2)}) collective-permute-start(f32[5,8,128]{2,1,0:T(8,128)} %get-tuple-element.19), channel_id=1, source_target_pairs={{0,1},{2,3},{4,5},{6,7},{8,9},{10,11},{12,13},{14,15},{1,0},{3,2},... | collective-permute-start | bytes 61448 | tf_op jit(solution)/shard_map/halo_y/ppermute | solution.py:473
  17.3 19.5 %collective-permute-start.2 = (f32[232,256]{1,0:T(8,128)S(1)}, f32[232,256]{1,0:T(8,128)S(1)}, u32[]{:S(2)}, u32[]{:S(2)}) collective-permute-start(f32[232,256]{1,0:T(8,128)S(1)} %fusion.1), channel_id=1, source_target_pairs={{496,0},{16,32},{48,64},{80,96},{112,128},{144,160},{176,192},{208... | collective-permute-start | bytes 712712 | tf_op jit(solution)/shard_map/halo_x/ppermute | solution.py:485
  28.4 8.4 %collective-permute-start.3 = (f32[232,256]{1,0:T(8,128)S(1)}, f32[232,256]{1,0:T(8,128)S(1)}, u32[]{:S(2)}, u32[]{:S(2)}) collective-permute-start(f32[232,256]{1,0:T(8,128)S(1)} %fusion.3), channel_id=1, source_target_pairs={{0,16},{32,48},{64,80},{96,112},{128,144},{160,176},{192,208},{224... | collective-permute-start | bytes 712712 | tf_op jit(solution)/shard_map/halo_x/ppermute | solution.py:486
  30.3 6.5 %copy-start.2 = (s32[5]{0:T(128)S(1)}, s32[5]{0:T(128)}, u32[]{:S(2)}) copy-start(s32[5]{0:T(128)} %order_ref.1) | copy-start | bytes 64

commit v11 on v10

--- a/solution.py
+++ b/solution.py
@@ -484,7 +484,8 @@
         next_payload, _ = lax.optimization_barrier((next_payload, near_payload))
         near_rows = lax.ppermute(near_payload, "sx", pairs("sx", -1))
         next_rows = lax.ppermute(with_corners(next_payload, ~even_x), "sx", pairs("sx", 0))
-    left = left_vectors.transpose(1, 0, 2)
+    left, _ = lax.optimization_barrier((left_vectors, near_payload))
+    left = left.transpose(1, 0, 2)
     f32 = jnp.float32
     part, edge_field, edge_rim, ends = vmem_call(
         interior_kernel,

time: 69.2 us -> 72.1 us (1.042)
  other arithmetic: 0.21 us -> 1.4 us
  waiting for transfers between devices: 0.01 us -> 1.01 us
  blocking collectives: 27.3 us -> 28.1 us
    unnamed x11 -> x6, local copies, waits for them, and re-layouts: 1.83 us -> 0.01 us
    optimization_barrier x0 -> x1, local copies, waits for them, and re-layouts: none -> 1.81 us  [shards(): left, _ = lax.optimization_barrier((left_vectors, near_payload))]
    dynamic_update_slice x2, other arithmetic: 0.01 us -> 1.21 us  [with_corners(): lax.dynamic_update_slice(payload, corners, (payload.shape[0] - corners.sh...]
    ppermute x1, waiting for transfers between devices: 0.01 us -> 1 us  [shards(): across = lax.ppermute(across, 'sy', pairs('sy', 0))]
    all_to_all x1, blocking collectives: 8.89 us -> 9.73 us  [shards(): lax.all_to_all(tile, 'sy', 0, 0, axis_index_groups=runs)]
  transfers between devices with their start and end apart: 4 -> 4, of which waited for: 0 -> 1; matrix products, arithmetic and copies ran while one was open for 3% -> 3% of each run, Pallas kernels for 9% -> 9%
where the time goes in v11:
time: 72.1 us; the launch traced here: 71.7 us
  blocking collectives  28.1 us (39%)
  starting transfers between devices  25.8 us (36%)
  Pallas kernels  12.5 us (17%)
  local copies, waits for them, and re-layouts  2.71 us (4%)
  other arithmetic  1.4 us (2%)
  waiting for transfers between devices  1.01 us (1%)
    all_to_all x1, blocking collectives, shards(): lax.all_to_all(spread, ('sx', 'sy'), 0, 0, axis_index_groups=planes)  18.4 us
    ppermute x1, starting transfers between devices, shards(): near_rows = lax.ppermute(near_payload, 'sx', pairs('sx', -1))  11 us
    pallas_call x2, Pallas kernels, vmem_call(): pl.pallas_call(kernel, out_shape=out_shape, in_specs=[pl.BlockSpec(memory...  10.1 us
    all_to_all x1, blocking collectives, shards(): lax.all_to_all(tile, 'sy', 0, 0, axis_index_groups=runs)  9.73 us
    ppermute x1, starting transfers between devices, shards(): across = lax.ppermute(across, 'sy', pairs('sy', 0))  8.27 us
    ppermute x1, starting transfers between devices, shards(): beside = lax.ppermute(beside, 'sy', pairs('sy', -1))  4.64 us
    pallas_call x1, Pallas kernels, prepare(): pl.pallas_call(prepare_kernel, out_shape=tuple((jax.ShapeDtypeStruct(shap...  2.41 us
    ppermute x1, starting transfers between devices, shards(): lax.ppermute(with_corners(next_payload, ~even_x), 'sx', pairs('sx', 0))  1.91 us
  transfers between devices with their start and end apart: 4, of which 1 were waited for; matrix products, arithmetic and copies ran while one was open for 3% of the time, Pallas kernels for 9%

profile of v11, /device:TPU:1, one launch (start us, length us, event | category | flops | bytes accessed | tf_op | source)
XLA Modules:
  0.0 71.7 jit_solution(18258955279507094727)
XLA Ops:
  0.0 2.4 %prepare.1 = (f32[32,32,256]{2,1,0:T(8,128)}, f32[3,32,256]{2,1,0:T(8,128)}, f32[232,256]{1,0:T(8,128)}, f32[232,256]{1,0:T(8,128)}, f32[5,8,128]{2,1,0:T(8,128)}, /*index=5*/f32[5,8,128]{2,1,0:T(8,128)}) custom-call(f32[4]{0:T(128)} %energy_hbm.1, bf16[32,32,256]{2,1,0:T(8,128)(2,1)} %right_hbm.1, s32[32,256]{1,0:T(8,128)} %class_hbm.1, s32[2,32,256]{2,1,0:T(8,128)} %bond_hbm.1), custom_call_target="tpu_custom_call" | custom-call | tf_op jit(solution)/shard_map/prepare/pallas_call | solution.py:134
  2.4 0.0 copy-start
  2.4 0.0 copy-start.1
  2.4 4.6 %collective-permute-start = (f32[5,8,128]{2,1,0:T(8,128)}, f32[5,8,128]{2,1,0:T(8,128)S(1)}, u32[]{:S(2)}, u32[]{:S(2)}) collective-permute-start(f32[5,8,128]{2,1,0:T(8,128)} %get-tuple-element.19), channel_id=1, source_target_pairs={{15,0},{1,2},{3,4},{5,6},{7,8},{9,10},{11,12},{13,14},{0,15},{2,1}... | collective-permute-start | bytes 61448 | tf_op jit(solution)/shard_map/halo_y/ppermute | solution.py:472
  7.1 8.3 %collective-permute-start.1 = (f32[5,8,128]{2,1,0:T(8,128)}, f32[5,8,128]{2,1,0:T(8,128)S(1)}, u32[]{:S(2)}, u32[]{:S(2)}) collective-permute-start(f32[5,8,128]{2,1,0:T(8,128)} %get-tuple-element.20), channel_id=1, source_target_pairs={{0,1},{2,3},{4,5},{6,7},{8,9},{10,11},{12,13},{14,15},{1,0},{3,2},... | collective-permute-start | bytes 61448 | tf_op jit(solution)/shard_map/halo_y/ppermute | solution.py:473
  15.4 0.0 collective-permute-done
  15.4 1.0 %collective-permute-done.1 = f32[5,8,128]{2,1,0:T(8,128)S(1)} collective-permute-done((f32[5,8,128]{2,1,0:T(8,128)}, f32[5,8,128]{2,1,0:T(8,128)S(1)}, u32[]{:S(2)}, u32[]{:S(2)}) %collective-permute-start.1) | collective-permute-done | bytes 20512 | tf_op jit(solution)/shard_map/halo_y/ppermute | solution.py:473
  16.4 0.6 fusion.1
  17.0 11.0 %collective-permute-start.2 = (f32[232,256]{1,0:T(8,128)}, f32[232,256]{1,0:T(8,128)S(1)}, u32[]{:S(2)}, u32[]{:S(2)}) collective-permute-start(f32[232,256]{1,0:T(8,128)} %fusion.1), channel_id=1, source_target_pairs={{496,0},{16,32},{48,64},{80,96},{112,128},{144,160},{176,192},{208... | collective-permute-start | bytes 712712 | tf_op jit(solution)/shard_map/halo_x/ppermute | solution.py:485
  28.0 0.6 fusion.3
  28.6 1.9 %collective-permute-start.3 = (f32[232,256]{1,0:T(8,128)}, f32[232,256]{1,0:T(8,128)S(1)}, u32[]{:S(2)}, u32[]{:S(2)}) collective-permute-start(f32[232,256]{1,0:T(8,128)} %fusion.3), channel_id=1, source_target_pairs={{0,16},{32,48},{64,80},{96,112},{128,144},{160,176},{192,208},{224... | collective-permute-start | bytes 712712 | tf_op jit(solution)/shard_map/halo_x/ppermute | solution.py:486
  30.5 1.8 %copy.16 = bf16[64,32,256]{2,0,1:T(8,128)(2,1)S(1)} copy(bf16[64,32,256]{2,1,0:T(8,128)(2,1)} %param.7) | data formatting | bytes 2097152 | tf_op jit(solution)/shard_map/optimization_barrier | solution.py:487
  32.4 0.0 copy-done
  32.4 0.0 copy-done.1
  32.4 0.0 copy-start.2
  32.4 6.4 %interior.1 = (f32[160,128]{1,0:T(8,128)S(1)}, f32[2,4,5,32,256]{4,3,2,1,0:T(8,128)S(1)}, f32[2,4,5,8,128]{4,3,2,1,0:T(8,128)S(1)}, f32[4,32,256]{2,1,0:T(8,128)S(1)}) custom-call(f32[32,32,256]{2,1,0:T(8,128)S(1)} %copy-done, f32[3,32,256]{2,1,0:T(8,128)S(1)} %copy-done.1, f32[5,8,128]{2,1,0:T(8,128)S(1)} %get-tuple-element.30.before_ref, ...), custom_call_target="tpu_custom_call" | custom-call | flops 8589934592 | bytes 4194304 | tf_op jit(solution)/shard_map/interior/pallas_call | solution.py:429
  38.8 0.0 collective-permute-done.3.next_ref
  38.8 0.0 collective-permute-done.2.near_ref
  38.9 0.0 copy-done.2
  38.9 3.6 %border.1 = f32[8,2,1,640]{3,2,1,0:T(1,128)S(1)} custom-call(s32[5]{0:T(128)S(1)} %copy-done.2, f32[4,32,256]{2,1,0:T(8,128)S(1)} %get-tuple-element.23.ends_ref, f32[3,32,256]{2,1,0:T(8,128)S(1)} %copy-done.1, f32[232,256]{1,0:T(8,128)S(1)} %collective-permute-done.2.near_ref, f32[232,256]{1,0:T(8,128)S(1)} %collective-permute-done.3.next_ref, ...), custom_call_target="tpu_custom_call" | custom-call | flops 4294967296 | bytes 4194304 | tf_op jit(solution)/shard_map/border/pallas_call | solution.py:429
  42.5 9.7 %all_to_all.10 = f32[8,2,1,640]{3,2,1,0:T(1,128)S(1)} all-to-all(f32[8,2,1,640]{3,2,1,0:T(1,128)S(1)} %border.1), channel_id=1, replica_groups={{0,1,2,3,4,5,6,7},{8,9,10,11,12,13,14,15},{16,17,18,19,20,21,22,23},{24..., dimensions={0} | all-to-all | bytes 81920 | tf_op jit(solution)/shard_map/reduce_near/all_to_all | solution.py:523
  52.3 0.2 broadcast_in_dim.9
  52.5 18.4 %all_to_all.11 = f32[64,1,640]{2,1,0:T(1,128)S(1)} all-to-all(f32[64,1,640]{2,1,0:T(1,128)S(1)} %broadcast_in_dim.9), channel_id=1, replica_groups={{0,16,32,48,64,80,96,112,128,144,160,176,192,208,224,240,256,272,288,30..., dimensions={0} | all-to-all | bytes 327680 | tf_op jit(solution)/shard_map/reduce_far/all_to_all | solution.py:527
  70.9 0.1 reduce_sum.21
  71.0 0.1 slice_bitcast_fusion.5
  71.1 0.6 copy.14
  (8 shorter events, 0.1 us)
Async XLA Ops:
  2.4 29.9 %copy-start = (f32[32,32,256]{2,1,0:T(8,128)S(1)}, f32[32,32,256]{2,1,0:T(8,128)}, u32[]{:S(2)}) copy-start(f32[32,32,256]{2,1,0:T(8,128)} %get-tuple-element.17.own_ref) | copy-start | bytes 3145732
  2.4 29.9 %copy-start.1 = (f32[3,32,256]{2,1,0:T(8,128)S(1)}, f32[3,32,256]{2,1,0:T(8,128)}, u32[]{:S(2)}) copy-start(f32[3,32,256]{2,1,0:T(8,128)} %get-tuple-element.18.coup_ref) | copy-start | bytes 294916
  2.4 13.0 %collective-permute-start = (f32[5,8,128]{2,1,0:T(8,128)}, f32[5,8,128]{2,1,0:T(8,128)S(1)}, u32[]{:S(2)}, u32[]{:S(2)}) collective-permute-start(f32[5,8,128]{2,1,0:T(8,128)} %get-tuple-element.19), channel_id=1, source_target_pairs={{15,0},{1,2},{3,4},{5,6},{7,8},{9,10},{11,12},{13,14},{0,15},{2,1}... | collective-permute-start | bytes 61448 | tf_op jit(solution)/shard_map/halo_y/ppermute | solution.py:472
  7.1 9.3 %collective-permute-start.1 = (f32[5,8,128]{2,1,0:T(8,128)}, f32[5,8,128]{2,1,0:T(8,128)S(1)}, u32[]{:S(2)}, u32[]{:S(2)}) collective-permute-start(f32[5,8,128]{2,1,0:T(8,128)} %get-tuple-element.20), channel_id=1, source_target_pairs={{0,1},{2,3},{4,5},{6,7},{8,9},{10,11},{12,13},{14,15},{1,0},{3,2},... | collective-permute-start | bytes 61448 | tf_op jit(solution)/shard_map/halo_y/ppermute | solution.py:473
  17.0 21.8 %collective-permute-start.2 = (f32[232,256]{1,0:T(8,128)}, f32[232,256]{1,0:T(8,128)S(1)}, u32[]{:S(2)}, u32[]{:S(2)}) collective-permute-start(f32[232,256]{1,0:T(8,128)} %fusion.1), channel_id=1, source_target_pairs={{496,0},{16,32},{48,64},{80,96},{112,128},{144,160},{176,192},{208... | collective-permute-start | bytes 712712 | tf_op jit(solution)/shard_map/halo_x/ppermute | solution.py:485
  28.6 10.2 %collective-permute-start.3 = (f32[232,256]{1,0:T(8,128)}, f32[232,256]{1,0:T(8,128)S(1)}, u32[]{:S(2)}, u32[]{:S(2)}) collective-permute-start(f32[232,256]{1,0:T(8,128)} %fusion.3), channel_id=1, source_target_pairs={{0,16},{32,48},{64,80},{96,112},{128,144},{160,176},{192,208},{224... | collective-permute-start | bytes 712712 | tf_op jit(solution)/shard_map/halo_x/ppermute | solution.py:486
  32.4 6.5 %copy-start.2 = (s32[5]{0:T(128)S(1)}, s32[5]{0:T(128)}, u32[]{:S(2)}) copy-start(s32[5]{0:T(128)} %order_ref.1) | copy-start | bytes 64
